TPU v7x, 512 devices: a whole 4x4x16 slice. The times are simulated.
512 devices in a mesh: view: 32 (over y_lo, z), band: 4 (over x), batch: 4 (over y_hi, core).
Axes of the slice: x: 4, y: 4 (y_hi: 2, y_lo: 2; y = y_hi * 2 + y_lo), z: 16, core: 2. Of those that a mesh axis runs over, the one named last changes fastest.
Arguments:
- images: bfloat16 [128, 32, 16, 768], P(('batch', 'view'), 'band'), parts along dimension 0, may hold values from -6 to 6
- frame_gain: float32 [768], replicated, may hold values from 0.5 to 2.5
- frame_qkv: bfloat16 [768, 1536], replicated, may hold values from -0.3 to 0.3
- frame_out: bfloat16 [512, 768], replicated, may hold values from -0.25 to 0.25
- row1_gain: float32 [768], replicated, may hold values from 0.5 to 2.5
- row1_qkv: bfloat16 [768, 1536], P('band'), may hold values from -0.3 to 0.3
- row1_out: bfloat16 [512, 768], P(None, 'band'), may hold values from -0.25 to 0.25
- row2_gain: float32 [768], replicated, may hold values from 0.5 to 2.5
- row2_qkv: bfloat16 [768, 1536], P('band'), may hold values from -0.3 to 0.3
- row2_out: bfloat16 [512, 768], P(None, 'band'), may hold values from -0.25 to 0.25
Outputs:
- refined: bfloat16 [128, 32, 16, 768], P(('batch', 'view'), 'band'), parts along dimension 0
There are 4 independent parts, one for each index of `batch`. A program takes and returns all parts, laid end to end along the dimension named above; an argument that names none is the same for every part. Nothing has to cross between parts.
All inputs are finite; a program needn't handle non-finite values.
Results may differ from a plain program's by a relative error of at most 0.02.
Values may be sent and summed in bfloat16 or wider, within the bound.
No kernel may reach another device: no remote copies, remote signals or barrier semaphores. Data moves between devices by JAX's collectives and lax.ppermute only.
A program may use at most 64 MiB of HBM per device.

v0:
```python
import jax
import jax.numpy as jnp
from jax import lax
from jax.sharding import PartitionSpec as P

HEAD_DIM = 64


EPSILON = 1e-06
BLOCK_ROWS = 512


def rms_normed(stream, gain):
    values = stream.astype(jnp.float32)
    factor = lax.rsqrt(jnp.mean(values * values, axis=-1, keepdims=True) + EPSILON)
    return (values * factor * gain).astype(jnp.bfloat16)


def online_update(carry, queries, keys, values):
    running, total, accum = carry
    scores = jnp.einsum(
        "qhd,khd->hqk", queries, keys, preferred_element_type=jnp.float32
    ) * HEAD_DIM ** (-0.5)
    highest = jnp.maximum(running, jnp.max(scores, axis=-1))
    weights = jnp.exp(scores - highest[:, :, None])
    total = jnp.sum(weights, axis=-1)
    mixed = jnp.einsum(
        "hqk,khd->qhd", weights.astype(jnp.bfloat16), values, preferred_element_type=jnp.float32
    )
    accum = mixed
    return (highest, total, accum)


def unit_attention(trio):
    queries, keys, values = trio
    length, pair_width = queries.shape
    block = min(BLOCK_ROWS, length)
    keys = keys.reshape(length, 2, HEAD_DIM)
    values = values.reshape(length, 2, HEAD_DIM)
    blocks = queries.reshape(length // block, block, 2, HEAD_DIM)

    def one_block(query_block):
        scores = jnp.einsum(
            "qhd,khd->hqk", query_block, keys, preferred_element_type=jnp.float32
        ) * HEAD_DIM ** (-0.5)
        weights = jnp.exp(scores - jnp.max(scores, axis=-1, keepdims=True))
        mixed = jnp.einsum(
            "hqk,khd->qhd", weights.astype(jnp.bfloat16), values, preferred_element_type=jnp.float32
        )
        total = jnp.transpose(jnp.sum(weights, axis=-1))
        return (mixed / total[:, :, None]).astype(jnp.bfloat16).reshape(block, pair_width)

    return lax.map(one_block, blocks).reshape(length, pair_width)


def attend_units(pieces):
    queries, keys, values = pieces
    attended = lax.map(unit_attention, (queries[0], keys[0], values[0]))
    return lax.all_to_all(attended[None], "view", split_axis=2, concat_axis=0, tiled=True)


def project_parts(normed, shard):
    groups = shard.shape[1] // (2 * HEAD_DIM)
    piece = lax.all_gather(shard, "band", axis=0, tiled=True)
    count = piece.shape[0]
    return jnp.einsum(
        "rcd,dpw->rpcw",
        normed,
        piece.reshape(count, groups, 2 * HEAD_DIM),
        preferred_element_type=jnp.float32,
    )


def mix_parts(merged, shard):
    groups = merged.shape[1]
    piece = lax.all_gather(shard, "band", axis=1, tiled=True)
    count = piece.shape[1]
    return jnp.einsum(
        "rpcw,pwn->rcn",
        merged,
        piece.reshape(groups, 2 * HEAD_DIM, count),
        preferred_element_type=jnp.float32,
    )


def row_sublayer(stream, row_count, col_count, gain, project, mix):
    width = stream.shape[1]
    normed = rms_normed(stream, gain).reshape(row_count, col_count, width)
    projected = project(normed)
    groups = projected.shape[1] // 3
    views = lax.axis_size("view")

    def unit_layout(section):
        return section.astype(jnp.bfloat16).reshape(
            views, row_count * groups // views, col_count, 2 * HEAD_DIM
        )

    triple = (
        unit_layout(projected[:, :groups]),
        unit_layout(projected[:, groups : 2 * groups]),
        unit_layout(projected[:, 2 * groups :]),
    )
    returned = attend_units(
        (
            lax.all_to_all(triple[0], "view", split_axis=0, concat_axis=2, tiled=True),
            lax.all_to_all(triple[1], "view", split_axis=0, concat_axis=2, tiled=True),
            lax.all_to_all(triple[2], "view", split_axis=0, concat_axis=2, tiled=True),
        )
    )
    merged = returned.reshape(row_count, groups, col_count, 2 * HEAD_DIM)
    update = mix(merged).reshape(row_count * col_count, width)
    return (stream.astype(jnp.float32) + update).astype(jnp.bfloat16)


def local(
    images,
    frame_gain,
    frame_qkv,
    frame_out,
    row1_gain,
    row1_qkv,
    row1_out,
    row2_gain,
    row2_qkv,
    row2_out,
):
    _, row_count, col_count, width = images.shape
    inner = frame_out.shape[0]
    heads = inner // HEAD_DIM
    tokens = row_count * col_count
    stream = images.reshape(tokens, width)
    normed = rms_normed(stream, frame_gain)
    start_state = (
        jnp.full((heads, tokens), -1e30, jnp.float32),
        jnp.zeros((heads, tokens), jnp.float32),
        jnp.zeros((tokens, heads, HEAD_DIM), jnp.float32),
    )
    triple = jnp.dot(normed, frame_qkv, preferred_element_type=jnp.float32).astype(jnp.bfloat16)
    queries = triple[:, :inner].reshape(tokens, heads, HEAD_DIM)
    keys = lax.all_gather(triple[:, inner : 2 * inner], "band", axis=0, tiled=True)
    values = lax.all_gather(triple[:, 2 * inner :], "band", axis=0, tiled=True)
    count = keys.shape[0]
    result = online_update(
        start_state,
        queries,
        keys.reshape(count, heads, HEAD_DIM),
        values.reshape(count, heads, HEAD_DIM),
    )
    _, total, accum = result
    attended = (
        (accum / jnp.transpose(total)[:, :, None]).astype(jnp.bfloat16).reshape(tokens, inner)
    )
    update = jnp.dot(attended, frame_out, preferred_element_type=jnp.float32)
    stream = (stream.astype(jnp.float32) + update).astype(jnp.bfloat16)
    stream = row_sublayer(
        stream,
        row_count,
        col_count,
        row1_gain,
        lambda normed_rows: project_parts(normed_rows, row1_qkv),
        lambda merged: mix_parts(merged, row1_out),
    )
    stream = row_sublayer(
        stream,
        row_count,
        col_count,
        row2_gain,
        lambda normed_rows: project_parts(normed_rows, row2_qkv),
        lambda merged: mix_parts(merged, row2_out),
    )
    return stream.reshape(images.shape)


def solution(mesh):
    in_specs = (
        P(("batch", "view"), "band", None, None),
        P(),
        P(),
        P(),
        P(),
        P("band", None),
        P(None, "band"),
        P(),
        P("band", None),
        P(None, "band"),
    )
    out_specs = P(("batch", "view"), "band", None, None)
    return jax.shard_map(local, mesh=mesh, in_specs=in_specs, out_specs=out_specs, check_vma=False)
```

profile of v0, /device:TPU:8, one launch (start us, length us, event | category | flops | bytes accessed | tf_op | source)
XLA Modules:
  0.0 268.4 jit_solution(17750390809118338394)
XLA Ops:
  6.5 0.7 all-gather.3.cloned.1.call-update
  7.3 0.7 all-gather.5.cloned.1.call-update
  8.0 1.0 multiply_reduce_fusion.5
  9.1 1.0 fusion.31
  10.2 0.5 convolution_convert_fusion
  10.7 0.7 fusion.45
  11.4 13.1 %all_gather.19 = bf16[512,512]{1,0:T(8,128)(2,1)S(1)} all-gather(bf16[128,512]{1,0:T(8,128)(2,1)S(1)} %get-tuple-element.74), channel_id=1, replica_groups=mesh['view'=32,'band'=4,'batch'=4] {'band'}, dimensions={0}, use_global_device_ids=true | all-gather | bytes 655360 | tf_op jit(solution)/shard_map/all_gather | solution.py:140
  24.7 1.0 copy.48
  25.8 1.9 multiply_reduce_fusion.2
  27.6 15.3 %all_gather.18 = bf16[512,512]{1,0:T(8,128)(2,1)S(1)} all-gather(bf16[128,512]{1,0:T(8,128)(2,1)S(1)} %get-tuple-element.82), channel_id=1, replica_groups=mesh['view'=32,'band'=4,'batch'=4] {'band'}, dimensions={0}, use_global_device_ids=true | all-gather | bytes 655360 | tf_op jit(solution)/shard_map/all_gather | solution.py:141
  43.2 2.3 fusion
  45.5 0.6 fusion.18
  46.7 0.4 multiply_reduce_fusion.4
  47.2 9.3 %all-gather.3.cloned.1.call-done = bf16[768,1536]{1,0:T(8,128)(2,1)} async-done(((bf16[192,1536]{1,0:T(8,128)(2,1)}), bf16[768,1536]{1,0:T(8,128)(2,1)}) %all-gather.3.cloned.1.call-update) | async-done | bytes 2359312 | tf_op jit(solution)/shard_map/all_gather | solution.py:64
  56.6 4.3 %copy.50 = bf16[768,1536]{0,1:T(8,128)(2,1)} copy(bf16[768,1536]{1,0:T(8,128)(2,1)} %all-gather.3.cloned.1.call-done) | data formatting | bytes 4718592 | tf_op jit(solution)/shard_map/all_gather | solution.py:64
  60.8 2.6 fusion.6
  63.4 0.7 fusion.44
  64.1 30.6 %all_to_all.32 = bf16[32,1,16,128]{3,2,1,0:T(8,128)(2,1)S(1)} all-to-all(bf16[32,1,16,128]{3,2,1,0:T(8,128)(2,1)S(1)} %bitcast.147), channel_id=1, replica_groups=mesh['view'=32,'band'=4,'batch'=4] {'view'}, dimensions={0} | all-to-all | bytes 262144 | tf_op jit(solution)/shard_map/all_to_all | solution.py:106
  94.7 19.1 %all_to_all.33 = bf16[32,1,16,128]{3,2,1,0:T(8,128)(2,1)S(1)} all-to-all(bf16[32,1,16,128]{3,2,1,0:T(8,128)(2,1)S(1)} %bitcast.145), channel_id=1, replica_groups=mesh['view'=32,'band'=4,'batch'=4] {'view'}, dimensions={0} | all-to-all | bytes 262144 | tf_op jit(solution)/shard_map/all_to_all | solution.py:105
  113.8 5.1 %all-to-all-start = ((bf16[32,1,16,128]{3,2,1,0:T(8,128)(2,1)}), bf16[32,1,16,128]{3,2,1,0:T(8,128)(2,1)S(1)}, u32[]{:S(2)}, u32[]{:S(2)}) async-start(bf16[32,1,16,128]{3,2,1,0:T(8,128)(2,1)} %bitcast.14), calls=%async_computation | async-start | bytes 262144 | tf_op jit(solution)/shard_map/all_to_all | solution.py:107
  119.2 13.9 %all-to-all-done = bf16[32,1,16,128]{3,2,1,0:T(8,128)(2,1)S(1)} async-done(((bf16[32,1,16,128]{3,2,1,0:T(8,128)(2,1)}), bf16[32,1,16,128]{3,2,1,0:T(8,128)(2,1)S(1)}, u32[]{:S(2)}, u32[]{:S(2)}) %all-to-all-start) | async-done | bytes 131104 | tf_op jit(solution)/shard_map/all_to_all | solution.py:107
  133.1 0.8 reshape.193
  134.0 0.4 multiply_reduce_fusion.1
  134.9 0.5 fusion.20
  135.6 0.6 broadcast.95
  136.2 1.4 reduce.1
  137.6 0.7 reshape.216
  138.3 5.9 %all-to-all-start.3 = ((bf16[32,2,1024]{2,1,0:T(2,128)(2,1)}), bf16[32,2,1024]{2,1,0:T(2,128)(2,1)}, u32[]{:S(2)}, u32[]{:S(2)}) async-start(bf16[32,2,1024]{2,1,0:T(2,128)(2,1)} %reshape.216), calls=%async_computation.3 | async-start | bytes 262144 | tf_op jit(solution)/shard_map/all_to_all | solution.py:59
  144.2 13.5 %all_gather.21 = bf16[512,768]{0,1:T(8,128)(2,1)S(1)} all-gather(bf16[512,192]{0,1:T(8,128)(2,1)} %param.16), channel_id=1, replica_groups=mesh['view'=32,'band'=4,'batch'=4] {'band'}, dimensions={1}, use_global_device_ids=true | all-gather | bytes 983040 | tf_op jit(solution)/shard_map/all_gather | solution.py:76
  157.8 1.2 copy.61
  158.9 4.3 %copy.62 = bf16[768,1536]{0,1:T(8,128)(2,1)} copy(bf16[768,1536]{1,0:T(8,128)(2,1)} %all-gather.5.cloned.1.call-done) | data formatting | bytes 4718592 | tf_op jit(solution)/shard_map/all_gather | solution.py:64
  163.2 1.4 reshape.217
  164.6 1.6 multiply_reduce_fusion.3
  166.5 0.9 fusion.7
  167.4 0.7 fusion.43
  168.1 27.2 %all_to_all.34 = bf16[32,1,16,128]{3,2,1,0:T(8,128)(2,1)S(1)} all-to-all(bf16[32,1,16,128]{3,2,1,0:T(8,128)(2,1)S(1)} %bitcast.148), channel_id=1, replica_groups=mesh['view'=32,'band'=4,'batch'=4] {'view'}, dimensions={0} | all-to-all | bytes 262144 | tf_op jit(solution)/shard_map/all_to_all | solution.py:106
  195.3 18.5 %all_to_all.35 = bf16[32,1,16,128]{3,2,1,0:T(8,128)(2,1)S(1)} all-to-all(bf16[32,1,16,128]{3,2,1,0:T(8,128)(2,1)S(1)} %bitcast.146), channel_id=1, replica_groups=mesh['view'=32,'band'=4,'batch'=4] {'view'}, dimensions={0} | all-to-all | bytes 262144 | tf_op jit(solution)/shard_map/all_to_all | solution.py:105
  213.8 5.2 %all-to-all-start.4 = ((bf16[32,1,16,128]{3,2,1,0:T(8,128)(2,1)}), bf16[32,1,16,128]{3,2,1,0:T(8,128)(2,1)S(1)}, u32[]{:S(2)}, u32[]{:S(2)}) async-start(bf16[32,1,16,128]{3,2,1,0:T(8,128)(2,1)} %bitcast.33), calls=%async_computation.4 | async-start | bytes 262144 | tf_op jit(solution)/shard_map/all_to_all | solution.py:107
  219.3 0.5 multiply_reduce_fusion
  219.7 1.3 copy-done.2
  221.4 11.8 %all-to-all-done.4 = bf16[32,1,16,128]{3,2,1,0:T(8,128)(2,1)S(1)} async-done(((bf16[32,1,16,128]{3,2,1,0:T(8,128)(2,1)}), bf16[32,1,16,128]{3,2,1,0:T(8,128)(2,1)S(1)}, u32[]{:S(2)}, u32[]{:S(2)}) %all-to-all-start.4) | async-done | bytes 131104 | tf_op jit(solution)/shard_map/all_to_all | solution.py:107
  233.4 2.1 fusion.19
  235.7 1.5 reduce.2
  237.2 0.7 reshape.218
  237.8 5.1 %all-to-all-start.7 = ((bf16[32,2,1024]{2,1,0:T(2,128)(2,1)}), bf16[32,2,1024]{2,1,0:T(2,128)(2,1)S(1)}, u32[]{:S(2)}, u32[]{:S(2)}) async-start(bf16[32,2,1024]{2,1,0:T(2,128)(2,1)} %reshape.218), calls=%async_computation.7 | async-start | bytes 262144 | tf_op jit(solution)/shard_map/all_to_all | solution.py:59
  243.0 14.1 %all_gather.23 = bf16[512,768]{0,1:T(8,128)(2,1)} all-gather(bf16[512,192]{0,1:T(8,128)(2,1)S(1)} %copy-done.7), channel_id=1, replica_groups=mesh['view'=32,'band'=4,'batch'=4] {'band'}, dimensions={1}, use_global_device_ids=true | all-gather | bytes 983040 | tf_op jit(solution)/shard_map/all_gather | solution.py:76
  257.0 2.3 copy.73
  259.5 2.1 fusion.10
  (47 shorter events, 3.5 us)
Async XLA Ops:
  6.5 3.7 %copy-start = (bf16[768,1536]{1,0:T(8,128)(2,1)S(1)}, bf16[768,1536]{1,0:T(8,128)(2,1)}, u32[]{:S(2)}) copy-start(bf16[768,1536]{1,0:T(8,128)(2,1)} %param.12) | copy-start | bytes 7077892
  6.5 50.0 %all-gather.3.cloned.1.call-start = ((), (), s32[]{:S(2)}) async-start(), calls=%async_computation.8 | async-start | bytes 2949120 | tf_op jit(solution)/shard_map/all_gather | solution.py:64
  7.3 151.7 %all-gather.5.cloned.1.call-start = ((), (), s32[]{:S(2)}) async-start(), calls=%async_computation.9 | async-start | bytes 2949120 | tf_op jit(solution)/shard_map/all_gather | solution.py:64
  43.2 2.3 copy-start.3
  45.5 0.9 copy-start.4
  45.5 1.2 copy-start.5
  45.5 1.6 copy-start.8
  113.8 19.3 %all-to-all-start = ((bf16[32,1,16,128]{3,2,1,0:T(8,128)(2,1)}), bf16[32,1,16,128]{3,2,1,0:T(8,128)(2,1)S(1)}, u32[]{:S(2)}, u32[]{:S(2)}) async-start(bf16[32,1,16,128]{3,2,1,0:T(8,128)(2,1)} %bitcast.14), calls=%async_computation | async-start | bytes 262144 | tf_op jit(solution)/shard_map/all_to_all | solution.py:107
  134.0 0.9 copy-start.6
  138.3 24.9 %all-to-all-start.3 = ((bf16[32,2,1024]{2,1,0:T(2,128)(2,1)}), bf16[32,2,1024]{2,1,0:T(2,128)(2,1)}, u32[]{:S(2)}, u32[]{:S(2)}) async-start(bf16[32,2,1024]{2,1,0:T(2,128)(2,1)} %reshape.216), calls=%async_computation.3 | async-start | bytes 262144 | tf_op jit(solution)/shard_map/all_to_all | solution.py:59
  163.2 3.1 %copy-start.9 = (f32[768]{0:T(1024)S(1)}, f32[768]{0:T(1024)}, u32[]{:S(2)}) copy-start(f32[768]{0:T(1024)} %param.17) | copy-start | bytes 9220
  164.6 1.9 copy-start.1
  213.8 19.5 %all-to-all-start.4 = ((bf16[32,1,16,128]{3,2,1,0:T(8,128)(2,1)}), bf16[32,1,16,128]{3,2,1,0:T(8,128)(2,1)S(1)}, u32[]{:S(2)}, u32[]{:S(2)}) async-start(bf16[32,1,16,128]{3,2,1,0:T(8,128)(2,1)} %bitcast.33), calls=%async_computation.4 | async-start | bytes 262144 | tf_op jit(solution)/shard_map/all_to_all | solution.py:107
  219.7 1.4 copy-start.2
  233.4 9.6 %copy-start.7 = (bf16[512,192]{0,1:T(8,128)(2,1)S(1)}, bf16[512,192]{0,1:T(8,128)(2,1)}, u32[]{:S(2)}) copy-start(bf16[512,192]{0,1:T(8,128)(2,1)} %param.19) | copy-start | bytes 589828
  237.8 21.5 %all-to-all-start.7 = ((bf16[32,2,1024]{2,1,0:T(2,128)(2,1)}), bf16[32,2,1024]{2,1,0:T(2,128)(2,1)S(1)}, u32[]{:S(2)}, u32[]{:S(2)}) async-start(bf16[32,2,1024]{2,1,0:T(2,128)(2,1)} %reshape.218), calls=%async_computation.7 | async-start | bytes 262144 | tf_op jit(solution)/shard_map/all_to_all | solution.py:59
Sparse Core Ops, SparseCore 0:
  9.4 47.0 all-gather.2
  58.6 41.9 all-gather.4
where the time goes:
time: 269 us; the launch traced here: 268 us
  blocking collectives  152 us (57%)
  waiting for transfers between devices  36.4 us (14%)
  local copies, waits for them, and re-layouts  23.1 us (9%)
  starting transfers between devices  21.3 us (8%)
  matrix products  14 us (5%)
  between operations  13.8 us (5%)
  other arithmetic  8.23 us (3%)
    all_to_all x2, blocking collectives, row_sublayer(): lax.all_to_all(triple[1], 'view', split_axis=0, concat_axis=2, tiled=True)  57.8 us
    all_to_all x2, blocking collectives, row_sublayer(): lax.all_to_all(triple[0], 'view', split_axis=0, concat_axis=2, tiled=True)  37.7 us
    all_gather x2, blocking collectives, mix_parts(): piece = lax.all_gather(shard, 'band', axis=1, tiled=True)  27.6 us
    all_to_all x2, waiting for transfers between devices, row_sublayer(): lax.all_to_all(triple[2], 'view', split_axis=0, concat_axis=2, tiled=True)  25.7 us
    all_gather x1, blocking collectives, local(): values = lax.all_gather(triple[:, 2 * inner:], 'band', axis=0, tiled=True)  15.3 us
    all_gather x1, blocking collectives, local(): lax.all_gather(triple[:, inner:2 * inner], 'band', axis=0, tiled=True)  13.1 us
    all_to_all x2, starting transfers between devices, attend_units(): lax.all_to_all(attended[None], 'view', split_axis=2, concat_axis=0, tiled...  11 us
    all_to_all x2, starting transfers between devices, row_sublayer(): lax.all_to_all(triple[2], 'view', split_axis=0, concat_axis=2, tiled=True)  10.3 us
  transfers between devices with their start and end apart: 6, of which 3 were waited for; matrix products, arithmetic and copies ran while one was open for 12% of the time, Pallas kernels for 0%

commit v1 on v0

v1 whole, which is shorter than its diff:
```python
import functools

import jax
import jax.numpy as jnp
from jax import lax
from jax.experimental import pallas as pl
from jax.experimental.pallas import tpu as pltpu
from jax.sharding import PartitionSpec as P

HEAD_DIM = 64
EPSILON = 1e-06
PAIR = 2 * HEAD_DIM


def normed_block(block, gain):
    values = block.astype(jnp.float32)
    factor = lax.rsqrt(jnp.mean(values * values, axis=-1, keepdims=True) + EPSILON)
    return (values * factor * gain).astype(jnp.bfloat16)


def attention_body(transposed_out, all_ref, own_ref, gain_ref, qkv_ref, out_ref, result_ref, kv_ref):
    chunks, tokens, width = all_ref.shape
    inner = kv_ref.shape[1] // 2
    gain = gain_ref[...]
    for chunk in range(chunks):
        normed = normed_block(all_ref[chunk], gain)
        kv_ref[chunk * tokens : (chunk + 1) * tokens, :] = jnp.dot(
            normed, qkv_ref[:, inner : 3 * inner], preferred_element_type=jnp.float32
        ).astype(jnp.bfloat16)
    own = own_ref[...]
    normed = normed_block(own, gain)
    queries = (
        jnp.dot(normed, qkv_ref[:, :inner], preferred_element_type=jnp.float32)
        .astype(jnp.bfloat16)
    ) * jnp.bfloat16(HEAD_DIM ** (-0.5))
    lane = lax.broadcasted_iota(jnp.int32, (tokens, PAIR), 1)
    first = lane < HEAD_DIM
    attended = []
    for pair in range(inner // PAIR):
        columns = slice(pair * PAIR, (pair + 1) * PAIR)
        query = queries[:, columns]
        keys = kv_ref[:, columns]
        values = kv_ref[:, inner + pair * PAIR : inner + (pair + 1) * PAIR]
        halves = []
        for mask in (first, jnp.logical_not(first)):
            masked = jnp.where(mask, query, jnp.zeros_like(query))
            scores = lax.dot_general(
                masked, keys, (((1,), (1,)), ((), ())), preferred_element_type=jnp.float32
            )
            highest = jnp.max(scores, axis=-1, keepdims=True)
            weights = jnp.exp(scores - highest)
            total = jnp.sum(weights, axis=-1, keepdims=True)
            mixed = jnp.dot(
                weights.astype(jnp.bfloat16), values, preferred_element_type=jnp.float32
            )
            halves.append(mixed / total)
        attended.append(jnp.where(first, halves[0], halves[1]).astype(jnp.bfloat16))
    attended = jnp.concatenate(attended, axis=1)
    contract = (((1,), (1,)), ((), ())) if transposed_out else (((1,), (0,)), ((), ()))
    update = lax.dot_general(
        attended, out_ref[...], contract, preferred_element_type=jnp.float32
    )
    stream = (own.astype(jnp.float32) + update).astype(jnp.bfloat16)
    if len(result_ref.shape) == 2:
        result_ref[...] = stream
    else:
        for copy in range(result_ref.shape[0]):
            result_ref[copy] = stream


def row_body(copies, all_ref, own_ref, gain_ref, weight_ref, result_ref, kv_ref):
    inner = kv_ref.shape[1] // 2
    attention_body(
        True,
        all_ref,
        own_ref,
        gain_ref,
        weight_ref.at[:, : 3 * inner],
        weight_ref.at[:, 3 * inner :],
        result_ref,
        kv_ref,
    )


def sublayer(everything, own, gain, weights, inner, name, copies=None):
    chunks, tokens, width = everything.shape
    shape = (tokens, width) if copies is None else (copies, tokens, width)
    body = (
        functools.partial(attention_body, False)
        if len(weights) == 2
        else functools.partial(row_body, copies)
    )
    count = chunks * tokens
    return pl.pallas_call(
        body,
        out_shape=jax.ShapeDtypeStruct(shape, jnp.bfloat16),
        in_specs=[pl.BlockSpec(memory_space=pltpu.VMEM)] * (3 + len(weights)),
        out_specs=pl.BlockSpec(memory_space=pltpu.VMEM),
        scratch_shapes=[pltpu.VMEM((count, 2 * inner), jnp.bfloat16)],
        compiler_params=pltpu.CompilerParams(vmem_limit_bytes=24 << 20),
        cost_estimate=pl.CostEstimate(
            flops=2 * count * width * 2 * inner + 4 * tokens * width * inner + 4 * tokens * count * inner,
            bytes_accessed=2 * (count * width + 4 * width * inner),
            transcendentals=tokens * count * inner // HEAD_DIM,
        ),
        name=name,
    )(everything, own, gain.reshape(1, width), *weights)


def gathered(stream, copies, axis, groups=None):
    return lax.all_to_all(
        jnp.broadcast_to(stream[None], (copies,) + stream.shape),
        axis,
        split_axis=0,
        concat_axis=0,
        tiled=True,
        axis_index_groups=groups,
    )


def local(
    images,
    frame_gain,
    frame_qkv,
    frame_out,
    row1_gain,
    row1_qkv,
    row1_out,
    row2_gain,
    row2_qkv,
    row2_out,
):
    _, row_count, col_count, width = images.shape
    inner = frame_out.shape[0]
    tokens = row_count * col_count
    views = lax.axis_size("view")
    bands = lax.axis_size("band")
    share = views // row_count
    near = 2
    deep = views // near
    side = share // near
    spread = [
        [y * deep + h * side + l for h in range(row_count)] for y in range(near) for l in range(side)
    ]
    ring = [
        [h * side + l for l in range(side)] + [deep + h * side + l for l in reversed(range(side))]
        for h in range(row_count)
    ]
    row1 = lax.all_gather(jnp.concatenate([row1_qkv, row1_out.T], axis=1), "band", axis=0, tiled=True)
    row2 = lax.all_gather(jnp.concatenate([row2_qkv, row2_out.T], axis=1), "band", axis=0, tiled=True)

    stream = images.reshape(tokens, width)
    everything = gathered(stream, bands, "band")
    stream = sublayer(everything, stream, frame_gain, (frame_qkv, frame_out), inner, "frame")

    stream = lax.all_to_all(
        stream.reshape(row_count, col_count, width),
        "view",
        split_axis=0,
        concat_axis=0,
        tiled=True,
        axis_index_groups=spread,
    ).reshape(tokens, width)
    everything = gathered(stream, share, "view", ring)
    copies = sublayer(everything, stream, row1_gain, (row1,), inner, "row1", share)
    everything = lax.all_to_all(
        copies, "view", split_axis=0, concat_axis=0, tiled=True, axis_index_groups=ring
    )
    stream = sublayer(everything, copies[0], row2_gain, (row2,), inner, "row2")
    stream = lax.all_to_all(
        stream.reshape(row_count, col_count, width),
        "view",
        split_axis=0,
        concat_axis=0,
        tiled=True,
        axis_index_groups=spread,
    )
    return stream.reshape(images.shape)


def solution(mesh):
    in_specs = (
        P(("batch", "view"), "band", None, None),
        P(),
        P(),
        P(),
        P(),
        P("band", None),
        P(None, "band"),
        P(),
        P("band", None),
        P(None, "band"),
    )
    out_specs = P(("batch", "view"), "band", None, None)
    return jax.shard_map(local, mesh=mesh, in_specs=in_specs, out_specs=out_specs, check_vma=False)
```

time: 269 us -> 154 us (0.57)
  blocking collectives: 152 us -> 62.2 us
  local copies, waits for them, and re-layouts: 23.1 us -> 8.54 us
  matrix products: 14 us -> 0 us
  Pallas kernels: 0 us -> 11.8 us
  starting transfers between devices: 21.3 us -> 13.4 us
  other arithmetic: 8.23 us -> 3.19 us
  waiting for transfers between devices: 36.4 us -> 41.1 us
    all_gather x4 -> x0, blocking collectives: 56 us -> none  [the longest x2 27.6 us: mix_parts(): piece = lax.all_gather(shard, 'band', axis=1, tiled=True)]
    all_to_all x4 -> x2, blocking collectives: 95.5 us -> 62.2 us  [local(): lax.all_to_all(stream.reshape(row_count, col_count, width), 'view', split...]
    dot_general x12 -> x0, matrix products: 14 us -> none  [the longest x2 3.73 us: mix_parts(): jnp.einsum('rpcw,pwn->rcn', merged, piece.reshape(groups, 2 * HEAD_DIM, c...]
    all_gather x2, waiting for transfers between devices: 9.32 us -> 22.5 us  [the longest x1 22.5 us: local(): lax.all_gather(jnp.concatenate([row2_qkv, row2_out.T], axis=1), 'band', a...]
    all_gather x6 -> x0, local copies, waits for them, and re-layouts: 12.5 us -> none  [the longest x2 8.55 us: project_parts(): piece = lax.all_gather(shard, 'band', axis=0, tiled=True)]
    pallas_call x0 -> x3, Pallas kernels: none -> 11.8 us  [sublayer(): pl.pallas_call(body, out_shape=jax.ShapeDtypeStruct(shape, jnp.bfloat16),...]
    all_to_all x4 -> x3, starting transfers between devices: 21.3 us -> 13.4 us  [the longest x2 8.35 us: gathered(): lax.all_to_all(jnp.broadcast_to(stream[None], (copies,) + stream.shape),...]
    all_to_all x4 -> x3, waiting for transfers between devices: 25.7 us -> 18.6 us  [the longest x2 18.6 us: gathered(): lax.all_to_all(jnp.broadcast_to(stream[None], (copies,) + stream.shape),...]
  transfers between devices with their start and end apart: 6 -> 5, of which waited for: 3 -> 3; matrix products, arithmetic and copies ran while one was open for 12% -> 3% of each run, Pallas kernels for 0% -> 5%
where the time goes in v1:
time: 154 us
  blocking collectives  62.2 us (40%)
  waiting for transfers between devices  41.1 us (27%)
  between operations  13.5 us (9%)
  starting transfers between devices  13.4 us (9%)
  Pallas kernels  11.8 us (8%)
  local copies, waits for them, and re-layouts  8.54 us (6%)
  other arithmetic  3.19 us (2%)
    all_to_all x2, blocking collectives, local(): lax.all_to_all(stream.reshape(row_count, col_count, width), 'view', split...  62.2 us
    all_gather x1, waiting for transfers between devices, local(): lax.all_gather(jnp.concatenate([row2_qkv, row2_out.T], axis=1), 'band', a...  22.5 us
    all_to_all x2, waiting for transfers between devices, gathered(): lax.all_to_all(jnp.broadcast_to(stream[None], (copies,) + stream.shape),...  18.6 us
    pallas_call x3, Pallas kernels, sublayer(): pl.pallas_call(body, out_shape=jax.ShapeDtypeStruct(shape, jnp.bfloat16),...  11.8 us
    all_to_all x2, starting transfers between devices, gathered(): lax.all_to_all(jnp.broadcast_to(stream[None], (copies,) + stream.shape),...  8.35 us
    unnamed x21, local copies, waits for them, and re-layouts  5.62 us
    all_to_all x1, starting transfers between devices, local(): lax.all_to_all(copies, 'view', split_axis=0, concat_axis=0, tiled=True, a...  5.06 us
  transfers between devices with their start and end apart: 5, of which 3 were waited for; matrix products, arithmetic and copies ran while one was open for 3% of the time, Pallas kernels for 5%

profile of v1, /device:TPU:8, one launch (start us, length us, event | category | flops | bytes accessed | tf_op | source)
XLA Modules:
  0.0 153.8 jit_solution(9515395399028614568)
XLA Ops:
  6.5 0.0 copy-start.3
  6.5 0.0 all-gather.3.cloned.1.call-start
  6.5 2.2 %pad_maximum_fusion = bf16[192,2048]{1,0:T(8,128)(2,1)} fusion(bf16[192,512]{1,0:T(8,128)(2,1)} %bitcast.16, bf16[192,1536]{1,0:T(8,128)(2,1)} %param.15), kind=kLoop, calls=%fused_computation | loop fusion | flops 1572864 | bytes 1572864 | tf_op jit(solution)/shard_map/concatenate | solution.py:149
  8.7 0.0 copy-start.7
  8.7 0.0 copy-start.2
  8.7 0.0 all-gather.3.cloned.1.call-update
  8.8 0.0 copy-done.3
  8.8 0.9 broadcast_in_dim.15
  9.7 4.4 %all-to-all-start = ((bf16[4,128,768]{2,1,0:T(8,128)(2,1)}), bf16[4,128,768]{2,1,0:T(8,128)(2,1)S(1)}, u32[]{:S(2)}, u32[]{:S(2)}) async-start(bf16[4,128,768]{2,1,0:T(8,128)(2,1)} %broadcast_in_dim.15), calls=%async_computation | async-start | bytes 1572864 | tf_op jit(solution)/shard_map/all_to_all | solution.py:111
  14.1 0.0 copy-done.7
  14.2 12.3 %all-to-all-done.all_ref = bf16[4,128,768]{2,1,0:T(8,128)(2,1)S(1)} async-done(((bf16[4,128,768]{2,1,0:T(8,128)(2,1)}), bf16[4,128,768]{2,1,0:T(8,128)(2,1)S(1)}, u32[]{:S(2)}, u32[]{:S(2)}) %all-to-all-start) | async-done | bytes 786464 | tf_op jit(solution)/shard_map/all_to_all | solution.py:111
  26.4 0.0 copy-done.2
  26.4 0.0 copy-start.4
  26.4 1.1 copy-done.4
  27.6 3.6 %frame.1 = bf16[128,768]{1,0:T(8,128)(2,1)S(1)} custom-call(bf16[4,128,768]{2,1,0:T(8,128)(2,1)S(1)} %all-to-all-done.all_ref, bf16[128,768]{1,0:T(8,128)(2,1)S(1)} %bitcast.14, f32[1,768]{1,0:T(1,128)S(1)} %reshape.22.gain_ref, bf16[768,1536]{1,0:T(8,128)(2,1)S(1)} %copy-done.2, bf16[512,768]{1,0:T(8,128)(2,1)S(1)} %copy-done.4), custom_call_target="tpu_custom_call" | custom-call | flops 1140850688 | bytes 3932160 | tf_op jit(solution)/shard_map/frame/pallas_call | solution.py:94
  31.1 0.0 copy-start.5
  31.1 0.0 copy-start.6
  31.2 32.0 %all_to_all.25 = bf16[8,16,768]{2,1,0:T(8,128)(2,1)S(1)} all-to-all(bf16[8,16,768]{2,1,0:T(8,128)(2,1)S(1)} %bitcast.12), channel_id=1, replica_groups={{0,32,64,96,128,160,192,224},{16,48,80,112,144,176,208,240},{256,288,32..., dimensions={0} | all-to-all | bytes 393216 | tf_op jit(solution)/shard_map/all_to_all | solution.py:156
  63.2 1.0 broadcast_in_dim.17
  64.2 3.9 %all-to-all-start.2 = ((bf16[4,128,768]{2,1,0:T(8,128)(2,1)}), bf16[4,128,768]{2,1,0:T(8,128)(2,1)S(1)}, u32[]{:S(2)}, u32[]{:S(2)}) async-start(bf16[4,128,768]{2,1,0:T(8,128)(2,1)} %broadcast_in_dim.17), calls=%async_computation.2 | async-start | bytes 1572864 | tf_op jit(solution)/shard_map/all_to_all | solution.py:111
  68.1 0.0 copy-start.8
  68.1 0.0 all-gather.5.cloned.1.call-start
  68.1 0.0 copy-done.5
  68.1 0.0 copy-done.6
  68.1 1.0 pad_maximum_fusion.1
  69.1 0.0 all-gather.5.cloned.1.call-update
  69.1 0.0 copy-done.8
  69.2 6.4 %all-to-all-done.2.all_ref = bf16[4,128,768]{2,1,0:T(8,128)(2,1)S(1)} async-done(((bf16[4,128,768]{2,1,0:T(8,128)(2,1)}), bf16[4,128,768]{2,1,0:T(8,128)(2,1)S(1)}, u32[]{:S(2)}, u32[]{:S(2)}) %all-to-all-start.2) | async-done | bytes 786464 | tf_op jit(solution)/shard_map/all_to_all | solution.py:111
  75.5 0.0 all-gather.3.cloned.1.call-done.weight_ref
  75.5 0.0 copy-start
  75.5 1.9 %copy-done = bf16[768,2048]{1,0:T(8,128)(2,1)S(1)} copy-done((bf16[768,2048]{1,0:T(8,128)(2,1)S(1)}, bf16[768,2048]{1,0:T(8,128)(2,1)}, u32[]{:S(2)}) %copy-start) | copy-done | bytes 3145752
  77.4 4.6 %row1.1 = bf16[4,128,768]{2,1,0:T(8,128)(2,1)} custom-call(bf16[4,128,768]{2,1,0:T(8,128)(2,1)S(1)} %all-to-all-done.2.all_ref, bf16[128,768]{1,0:T(8,128)(2,1)S(1)} %bitcast.10, f32[1,768]{1,0:T(1,128)S(1)} %reshape.24.gain_ref, bf16[768,2048]{1,0:T(8,128)(2,1)S(1)} %copy-done), custom_call_target="tpu_custom_call" | custom-call | flops 1140850688 | bytes 3932160 | tf_op jit(solution)/shard_map/row1/pallas_call | solution.py:94
  82.0 0.0 copy-start.9
  82.0 5.1 %all-to-all-start.3 = ((bf16[4,128,768]{2,1,0:T(8,128)(2,1)}), bf16[4,128,768]{2,1,0:T(8,128)(2,1)S(1)}, u32[]{:S(2)}, u32[]{:S(2)}) async-start(bf16[4,128,768]{2,1,0:T(8,128)(2,1)} %row1.1), calls=%async_computation.3 | async-start | bytes 1572864 | tf_op jit(solution)/shard_map/all_to_all | solution.py:166
  87.1 0.0 copy-done.9
  87.1 1.0 slice_bitcast_fusion.own_ref
  88.1 22.5 %all-gather.5.cloned.1.call-done.weight_ref = bf16[768,2048]{1,0:T(8,128)(2,1)} async-done(((bf16[192,2048]{1,0:T(8,128)(2,1)}), bf16[768,2048]{1,0:T(8,128)(2,1)}) %all-gather.5.cloned.1.call-update) | async-done | bytes 3145744 | tf_op jit(solution)/shard_map/all_gather | solution.py:150
  110.5 0.0 all-to-all-done.3.all_ref
  110.5 0.0 copy-start.1
  110.5 1.9 %copy-done.1 = bf16[768,2048]{1,0:T(8,128)(2,1)S(1)} copy-done((bf16[768,2048]{1,0:T(8,128)(2,1)S(1)}, bf16[768,2048]{1,0:T(8,128)(2,1)}, u32[]{:S(2)}) %copy-start.1) | copy-done | bytes 3145752
  112.4 3.7 %row2.1 = bf16[128,768]{1,0:T(8,128)(2,1)S(1)} custom-call(bf16[4,128,768]{2,1,0:T(8,128)(2,1)S(1)} %all-to-all-done.3.all_ref, bf16[128,768]{1,0:T(8,128)(2,1)S(1)} %slice_bitcast_fusion.own_ref, f32[1,768]{1,0:T(1,128)S(1)} %reshape.25.gain_ref, bf16[768,2048]{1,0:T(8,128)(2,1)S(1)} %copy-done.1), custom_call_target="tpu_custom_call" | custom-call | flops 1140850688 | bytes 3932160 | tf_op jit(solution)/shard_map/row2/pallas_call | solution.py:94
  116.1 30.2 %all_to_all.26 = bf16[8,16,768]{2,1,0:T(8,128)(2,1)S(1)} all-to-all(bf16[8,16,768]{2,1,0:T(8,128)(2,1)S(1)} %bitcast.11), channel_id=1, replica_groups={{0,32,64,96,128,160,192,224},{16,48,80,112,144,176,208,240},{256,288,32..., dimensions={0} | all-to-all | bytes 393216 | tf_op jit(solution)/shard_map/all_to_all | solution.py:170
  146.2 0.7 copy.12
  (3 shorter events, 0.0 us)
Async XLA Ops:
  6.5 2.2 %copy-start.3 = (bf16[1,8,16,768]{3,2,1,0:T(8,128)(2,1)S(1)}, bf16[1,8,16,768]{3,2,1,0:T(8,128)(2,1)}, u32[]{:S(2)}) copy-start(bf16[1,8,16,768]{3,2,1,0:T(8,128)(2,1)} %param.10) | copy-start | bytes 589828
  6.5 69.0 %all-gather.3.cloned.1.call-start = ((), (), s32[]{:S(2)}) async-start(), calls=%async_computation.5 | async-start | bytes 3932160 | tf_op jit(solution)/shard_map/all_gather | solution.py:149
  8.7 5.4 %copy-start.7 = (f32[768]{0:T(1024)S(1)}, f32[768]{0:T(1024)}, u32[]{:S(2)}) copy-start(f32[768]{0:T(1024)} %param.11) | copy-start | bytes 9220
  8.7 17.7 %copy-start.2 = (bf16[768,1536]{1,0:T(8,128)(2,1)S(1)}, bf16[768,1536]{1,0:T(8,128)(2,1)}, u32[]{:S(2)}) copy-start(bf16[768,1536]{1,0:T(8,128)(2,1)} %qkv_ref.1) | copy-start | bytes 7077892
  9.7 16.7 %all-to-all-start = ((bf16[4,128,768]{2,1,0:T(8,128)(2,1)}), bf16[4,128,768]{2,1,0:T(8,128)(2,1)S(1)}, u32[]{:S(2)}, u32[]{:S(2)}) async-start(bf16[4,128,768]{2,1,0:T(8,128)(2,1)} %broadcast_in_dim.15), calls=%async_computation | async-start | bytes 1572864 | tf_op jit(solution)/shard_map/all_to_all | solution.py:111
  26.4 1.1 copy-start.4
  31.1 37.0 %copy-start.5 = (bf16[192,1536]{1,0:T(8,128)(2,1)S(1)}, bf16[192,1536]{1,0:T(8,128)(2,1)}, u32[]{:S(2)}) copy-start(bf16[192,1536]{1,0:T(8,128)(2,1)} %param.18) | copy-start | bytes 1769476
  31.1 37.0 %copy-start.6 = (bf16[512,192]{0,1:T(8,128)(2,1)S(1)}, bf16[512,192]{0,1:T(8,128)(2,1)}, u32[]{:S(2)}) copy-start(bf16[512,192]{0,1:T(8,128)(2,1)} %param.19) | copy-start | bytes 589828
  64.2 11.3 %all-to-all-start.2 = ((bf16[4,128,768]{2,1,0:T(8,128)(2,1)}), bf16[4,128,768]{2,1,0:T(8,128)(2,1)S(1)}, u32[]{:S(2)}, u32[]{:S(2)}) async-start(bf16[4,128,768]{2,1,0:T(8,128)(2,1)} %broadcast_in_dim.17), calls=%async_computation.2 | async-start | bytes 1572864 | tf_op jit(solution)/shard_map/all_to_all | solution.py:111
  68.1 1.0 copy-start.8
  68.1 42.4 %all-gather.5.cloned.1.call-start = ((), (), s32[]{:S(2)}) async-start(), calls=%async_computation.6 | async-start | bytes 3932160 | tf_op jit(solution)/shard_map/all_gather | solution.py:150
  75.5 1.9 %copy-start = (bf16[768,2048]{1,0:T(8,128)(2,1)S(1)}, bf16[768,2048]{1,0:T(8,128)(2,1)}, u32[]{:S(2)}) copy-start(bf16[768,2048]{1,0:T(8,128)(2,1)} %all-gather.3.cloned.1.call-done.weight_ref) | copy-start | bytes 9437188
  82.0 5.1 %copy-start.9 = (f32[768]{0:T(1024)S(1)}, f32[768]{0:T(1024)}, u32[]{:S(2)}) copy-start(f32[768]{0:T(1024)} %param.17) | copy-start | bytes 9220
  82.0 28.5 %all-to-all-start.3 = ((bf16[4,128,768]{2,1,0:T(8,128)(2,1)}), bf16[4,128,768]{2,1,0:T(8,128)(2,1)S(1)}, u32[]{:S(2)}, u32[]{:S(2)}) async-start(bf16[4,128,768]{2,1,0:T(8,128)(2,1)} %row1.1), calls=%async_computation.3 | async-start | bytes 1572864 | tf_op jit(solution)/shard_map/all_to_all | solution.py:166
  110.5 1.9 %copy-start.1 = (bf16[768,2048]{1,0:T(8,128)(2,1)S(1)}, bf16[768,2048]{1,0:T(8,128)(2,1)}, u32[]{:S(2)}) copy-start(bf16[768,2048]{1,0:T(8,128)(2,1)} %all-gather.5.cloned.1.call-done.weight_ref) | copy-start | bytes 9437188
Sparse Core Ops, SparseCore 0:
  9.4 51.5 all-gather.2
  71.0 39.4 all-gather.4

commit v2 on v1

--- a/solution.py
+++ b/solution.py
@@ -7,6 +7,7 @@
 from jax.experimental.pallas import tpu as pltpu
 from jax.sharding import PartitionSpec as P
 
+
 HEAD_DIM = 64
 EPSILON = 1e-06
 PAIR = 2 * HEAD_DIM
@@ -19,7 +20,7 @@
 
 
 def attention_body(transposed_out, all_ref, own_ref, gain_ref, qkv_ref, out_ref, result_ref, kv_ref):
-    chunks, tokens, width = all_ref.shape
+    chunks, tokens, _ = all_ref.shape
     inner = kv_ref.shape[1] // 2
     gain = gain_ref[...]
     for chunk in range(chunks):
@@ -68,8 +69,34 @@
             result_ref[copy] = stream
 
 
-def row_body(copies, all_ref, own_ref, gain_ref, weight_ref, result_ref, kv_ref):
+def row_body(
+    all_ref,
+    own_ref,
+    gain_ref,
+    qkv_ref,
+    out_ref,
+    one_ref,
+    two_ref,
+    three_ref,
+    other_ref,
+    result_ref,
+    kv_ref,
+    weight_ref,
+):
     inner = kv_ref.shape[1] // 2
+    pieces, rows, _ = other_ref.shape
+    bands = pieces + 1
+    band = lax.axis_index("band")
+    core = lax.rem(lax.axis_index("batch"), 2)
+    start = pl.multiple_of(2 * band * rows, rows)
+    weight_ref[pl.ds(start, 2 * rows), : 3 * inner] = qkv_ref[...]
+    weight_ref[pl.ds(start, 2 * rows), 3 * inner :] = out_ref[...]
+    for index, mine_ref in enumerate((one_ref, two_ref, three_ref)):
+        source = lax.rem(band + bands - 1 - index, bands)
+        here = pl.multiple_of((2 * source + core) * rows, rows)
+        there = pl.multiple_of((2 * source + 1 - core) * rows, rows)
+        weight_ref[pl.ds(here, rows), :] = mine_ref[...]
+        weight_ref[pl.ds(there, rows), :] = other_ref[index]
     attention_body(
         True,
         all_ref,
@@ -82,29 +109,26 @@
     )
 
 
-def sublayer(everything, own, gain, weights, inner, name, copies=None):
+def sublayer(everything, own, gain, weights, inner, copies=None):
+    rows = len(weights) > 2
     chunks, tokens, width = everything.shape
     shape = (tokens, width) if copies is None else (copies, tokens, width)
-    body = (
-        functools.partial(attention_body, False)
-        if len(weights) == 2
-        else functools.partial(row_body, copies)
-    )
+    body = row_body if rows else functools.partial(attention_body, False)
     count = chunks * tokens
     return pl.pallas_call(
         body,
         out_shape=jax.ShapeDtypeStruct(shape, jnp.bfloat16),
         in_specs=[pl.BlockSpec(memory_space=pltpu.VMEM)] * (3 + len(weights)),
         out_specs=pl.BlockSpec(memory_space=pltpu.VMEM),
-        scratch_shapes=[pltpu.VMEM((count, 2 * inner), jnp.bfloat16)],
-        compiler_params=pltpu.CompilerParams(vmem_limit_bytes=24 << 20),
+        scratch_shapes=[pltpu.VMEM((count, 2 * inner), jnp.bfloat16)]
+        + [pltpu.VMEM((width, 4 * inner), jnp.bfloat16)] * rows,
+        compiler_params=pltpu.CompilerParams(vmem_limit_bytes=12 << 20),
         cost_estimate=pl.CostEstimate(
             flops=2 * count * width * 2 * inner + 4 * tokens * width * inner + 4 * tokens * count * inner,
             bytes_accessed=2 * (count * width + 4 * width * inner),
             transcendentals=tokens * count * inner // HEAD_DIM,
         ),
-        name=name,
-    )(everything, own, gain.reshape(1, width), *weights)
+    )(everything, own, gain, *weights)
 
 
 def gathered(stream, copies, axis, groups=None):
@@ -118,7 +142,7 @@
     )
 
 
-def local(
+def layers(
     images,
     frame_gain,
     frame_qkv,
@@ -146,13 +170,34 @@
         [h * side + l for l in range(side)] + [deep + h * side + l for l in reversed(range(side))]
         for h in range(row_count)
     ]
-    row1 = lax.all_gather(jnp.concatenate([row1_qkv, row1_out.T], axis=1), "band", axis=0, tiled=True)
-    row2 = lax.all_gather(jnp.concatenate([row2_qkv, row2_out.T], axis=1), "band", axis=0, tiled=True)
+    siblings = [(i, i ^ 1) for i in range(lax.axis_size("batch"))]
+    core = lax.rem(lax.axis_index("batch"), 2)
+
+    def half(qkv, out):
+        rows = qkv.shape[0] // 2
+        shard = jnp.concatenate([qkv, out.T], axis=1)
+        return lax.dynamic_slice(shard, (core * rows, 0), (rows, shard.shape[1]))
 
     stream = images.reshape(tokens, width)
-    everything = gathered(stream, bands, "band")
-    stream = sublayer(everything, stream, frame_gain, (frame_qkv, frame_out), inner, "frame")
-
+    everything = lax.all_gather(stream, "band", axis=0, tiled=False)
+    stream = sublayer(everything, stream, frame_gain.reshape(1, width), (frame_qkv, frame_out), inner)
+    stream, row1_qkv, row1_out, row2_qkv, row2_out = lax.optimization_barrier(
+        (stream, row1_qkv, row1_out, row2_qkv, row2_out)
+    )
+
+    def pulled(qkv, out):
+        piece = half(qkv, out)
+        pieces = []
+        for step in range(1, bands):
+            pieces.append(
+                lax.ppermute(piece, "band", [(i, (i + step) % bands) for i in range(bands)])
+            )
+        return pieces
+
+    gain1 = row1_gain.reshape(1, width)
+    gain2 = row2_gain.reshape(1, width)
+    mine1 = pulled(row1_qkv, row1_out)
+    mine2 = pulled(row2_qkv, row2_out)
     stream = lax.all_to_all(
         stream.reshape(row_count, col_count, width),
         "view",
@@ -161,12 +206,14 @@
         tiled=True,
         axis_index_groups=spread,
     ).reshape(tokens, width)
+    other1 = lax.ppermute(jnp.stack(mine1), "batch", siblings)
+    other2 = lax.ppermute(jnp.stack(mine2), "batch", siblings)
     everything = gathered(stream, share, "view", ring)
-    copies = sublayer(everything, stream, row1_gain, (row1,), inner, "row1", share)
+    copies = sublayer(everything, stream, gain1, (row1_qkv, row1_out.T, *mine1, other1), inner, share)
     everything = lax.all_to_all(
         copies, "view", split_axis=0, concat_axis=0, tiled=True, axis_index_groups=ring
     )
-    stream = sublayer(everything, copies[0], row2_gain, (row2,), inner, "row2")
+    stream = sublayer(everything, copies[0], gain2, (row2_qkv, row2_out.T, *mine2, other2), inner)
     stream = lax.all_to_all(
         stream.reshape(row_count, col_count, width),
         "view",
@@ -192,4 +239,4 @@
         P(None, "band"),
     )
     out_specs = P(("batch", "view"), "band", None, None)
-    return jax.shard_map(local, mesh=mesh, in_specs=in_specs, out_specs=out_specs, check_vma=False)
+    return jax.shard_map(layers, mesh=mesh, in_specs=in_specs, out_specs=out_specs, check_vma=False)

time: 154 us -> 156 us (1.013)
  the two profiles are of different devices: /device:TPU:8 before, /device:TPU:56 now
where the time goes in v2:
time: 156 us; the launch traced here: 155 us
  blocking collectives  66.4 us (43%)
  starting transfers between devices  33.9 us (22%)
  waiting for transfers between devices  30.5 us (20%)
  Pallas kernels  12.2 us (8%)
  local copies, waits for them, and re-layouts  11.6 us (7%)
    all_to_all x2, blocking collectives, layers(): lax.all_to_all(stream.reshape(row_count, col_count, width), 'view', split...  52.6 us
    ppermute x6, waiting for transfers between devices, pulled(): lax.ppermute(piece, 'band', [(i, (i + step) % bands) for i in range(bands)])  25.8 us
    ppermute x6, starting transfers between devices, pulled(): lax.ppermute(piece, 'band', [(i, (i + step) % bands) for i in range(bands)])  19.3 us
    all_gather x1, blocking collectives, layers(): everything = lax.all_gather(stream, 'band', axis=0, tiled=False)  13.9 us
    pallas_call x3, Pallas kernels, sublayer(): pl.pallas_call(body, out_shape=jax.ShapeDtypeStruct(shape, jnp.bfloat16),...  12.2 us
    unnamed x27, local copies, waits for them, and re-layouts  9.02 us
    all_to_all x1, starting transfers between devices, gathered(): lax.all_to_all(jnp.broadcast_to(stream[None], (copies,) + stream.shape),...  6.45 us
    all_to_all x1, starting transfers between devices, layers(): lax.all_to_all(copies, 'view', split_axis=0, concat_axis=0, tiled=True, a...  4.32 us
  transfers between devices with their start and end apart: 10, of which 7 were waited for; matrix products, arithmetic and copies ran while one was open for 1% of the time, Pallas kernels for 0%

profile of v2, /device:TPU:56, one launch (start us, length us, event | category | flops | bytes accessed | tf_op | source)
XLA Modules:
  0.0 155.1 jit_solution(4270784044661576365)
XLA Ops:
  0.0 13.9 %all_gather.3.all_ref = bf16[4,128,768]{2,1,0:T(8,128)(2,1)S(1)} all-gather(bf16[1,128,768]{2,1,0:T(8,128)(2,1)} %bitcast.26), channel_id=1, replica_groups=mesh['view'=32,'band'=4,'batch'=4] {'band'}, dimensions={0}, use_global_device_ids=true | all-gather | bytes 983040 | tf_op jit(solution)/shard_map/all_gather | solution.py:182
  13.9 0.7 reshape.24.gain_ref
  14.6 0.0 copy-start.2
  14.6 1.7 %copy-done.2 = bf16[768,1536]{1,0:T(8,128)(2,1)S(1)} copy-done((bf16[768,1536]{1,0:T(8,128)(2,1)S(1)}, bf16[768,1536]{1,0:T(8,128)(2,1)}, u32[]{:S(2)}) %copy-start.2) | copy-done | bytes 2359320
  16.2 0.0 copy-start.7
  16.2 0.9 copy-done.7
  17.1 0.0 copy-start.10
  17.1 1.1 copy-done.10
  18.3 3.7 %shard_map.100 = bf16[128,768]{1,0:T(8,128)(2,1)S(1)} custom-call(bf16[4,128,768]{2,1,0:T(8,128)(2,1)S(1)} %all_gather.3.all_ref, bf16[128,768]{1,0:T(8,128)(2,1)S(1)} %bitcast.27, f32[1,768]{1,0:T(1,128)S(1)} %reshape.24.gain_ref, bf16[768,1536]{1,0:T(8,128)(2,1)S(1)} %copy-done.2, bf16[512,768]{1,0:T(8,128)(2,1)S(1)} %copy-done.10), custom_call_target="tpu_custom_call" | custom-call | flops 1140850688 | bytes 3932160 | tf_op jit(solution)/shard_map/pallas_call | solution.py:118
  22.0 29.6 %all_to_all.20 = bf16[8,16,768]{2,1,0:T(8,128)(2,1)S(1)} all-to-all(bf16[8,16,768]{2,1,0:T(8,128)(2,1)S(1)} %bitcast.25), channel_id=1, replica_groups={{0,32,64,96,128,160,192,224},{16,48,80,112,144,176,208,240},{256,288,32..., dimensions={0} | all-to-all | bytes 393216 | tf_op jit(solution)/shard_map/all_to_all | solution.py:201
  51.7 1.0 broadcast_in_dim.8
  52.6 6.5 %all-to-all-start.1 = ((bf16[4,128,768]{2,1,0:T(8,128)(2,1)}), bf16[4,128,768]{2,1,0:T(8,128)(2,1)S(1)}, u32[]{:S(2)}, u32[]{:S(2)}) async-start(bf16[4,128,768]{2,1,0:T(8,128)(2,1)} %broadcast_in_dim.8), calls=%async_computation.1 | async-start | bytes 1572864 | tf_op jit(solution)/shard_map/all_to_all | solution.py:135
  59.1 0.0 copy-done
  59.1 0.0 copy-done.8
  59.1 2.2 %collective-permute-start = (bf16[96,2048]{1,0:T(8,128)(2,1)S(1)}, bf16[96,2048]{1,0:T(8,128)(2,1)S(1)}, u32[]{:S(2)}, u32[]{:S(2)}) collective-permute-start(bf16[96,2048]{1,0:T(8,128)(2,1)S(1)} %fusion.1), channel_id=1, source_target_pairs={{0,4},{4,8},{8,12},{12,0},{1,5},{5,9},{9,13},{13,1},{2,6},{6,10},{... | collective-permute-start | bytes 1179656 | tf_op jit(solution)/shard_map/ppermute | solution.py:193
  61.3 4.6 %collective-permute-start.1 = (bf16[96,2048]{1,0:T(8,128)(2,1)S(1)}, bf16[96,2048]{1,0:T(8,128)(2,1)S(1)}, u32[]{:S(2)}, u32[]{:S(2)}) collective-permute-start(bf16[96,2048]{1,0:T(8,128)(2,1)S(1)} %fusion.1), channel_id=1, source_target_pairs={{0,8},{4,12},{8,0},{12,4},{1,9},{5,13},{9,1},{13,5},{2,10},{6,14},... | collective-permute-start | bytes 1179656 | tf_op jit(solution)/shard_map/ppermute | solution.py:193
  65.9 2.5 %collective-permute-start.2 = (bf16[96,2048]{1,0:T(8,128)(2,1)S(1)}, bf16[96,2048]{1,0:T(8,128)(2,1)S(1)}, u32[]{:S(2)}, u32[]{:S(2)}) collective-permute-start(bf16[96,2048]{1,0:T(8,128)(2,1)S(1)} %fusion.1), channel_id=1, source_target_pairs={{0,12},{4,0},{8,4},{12,8},{1,13},{5,1},{9,5},{13,9},{2,14},{6,2},{... | collective-permute-start | bytes 1179656 | tf_op jit(solution)/shard_map/ppermute | solution.py:193
  68.4 8.6 %collective-permute-done.one_ref = bf16[96,2048]{1,0:T(8,128)(2,1)S(1)} collective-permute-done((bf16[96,2048]{1,0:T(8,128)(2,1)S(1)}, bf16[96,2048]{1,0:T(8,128)(2,1)S(1)}, u32[]{:S(2)}, u32[]{:S(2)}) %collective-permute-start) | collective-permute-done | bytes 393248 | tf_op jit(solution)/shard_map/ppermute | solution.py:193
  77.0 0.0 collective-permute-done.1.two_ref
  77.0 2.6 %collective-permute-done.2.three_ref = bf16[96,2048]{1,0:T(8,128)(2,1)S(1)} collective-permute-done((bf16[96,2048]{1,0:T(8,128)(2,1)S(1)}, bf16[96,2048]{1,0:T(8,128)(2,1)S(1)}, u32[]{:S(2)}, u32[]{:S(2)}) %collective-permute-start.2) | collective-permute-done | bytes 393248 | tf_op jit(solution)/shard_map/ppermute | solution.py:193
  79.6 0.1 pad_maximum_fusion
  79.7 1.9 %collective-permute-start.3 = (bf16[3,96,2048]{2,1,0:T(8,128)(2,1)S(1)}, bf16[3,96,2048]{2,1,0:T(8,128)(2,1)S(1)}, u32[]{:S(2)}, u32[]{:S(2)}) collective-permute-start(bf16[3,96,2048]{2,1,0:T(8,128)(2,1)S(1)} %pad_maximum_fusion), channel_id=1, source_target_pairs={{0,1},{1,0},{2,3},{3,2},{4,5},{5,4},{6,7},{7,6},{8,9},{9,8},{10,11... | collective-permute-start | bytes 3538952 | tf_op jit(solution)/shard_map/ppermute | solution.py:209
  81.7 0.0 copy-done.11
  81.7 2.8 %collective-permute-done.3.other_ref = bf16[3,96,2048]{2,1,0:T(8,128)(2,1)S(1)} collective-permute-done((bf16[3,96,2048]{2,1,0:T(8,128)(2,1)S(1)}, bf16[3,96,2048]{2,1,0:T(8,128)(2,1)S(1)}, u32[]{:S(2)}, u32[]{:S(2)}) %collective-permute-start.3) | collective-permute-done | bytes 1179680 | tf_op jit(solution)/shard_map/ppermute | solution.py:209
  84.5 1.0 copy-done.3
  85.5 0.0 all-to-all-done.1.all_ref
  85.5 1.3 copy-done.4
  86.8 4.7 %shard_map.101 = bf16[4,128,768]{2,1,0:T(8,128)(2,1)} custom-call(bf16[4,128,768]{2,1,0:T(8,128)(2,1)S(1)} %all-to-all-done.1.all_ref, bf16[128,768]{1,0:T(8,128)(2,1)S(1)} %bitcast.17, f32[1,768]{1,0:T(1,128)S(1)} %reshape.26.gain_ref, bf16[192,1536]{1,0:T(8,128)(2,1)S(1)} %copy-done, bf16[192,512]{1,0:T(8,128)(2,1)S(1)} %bitcast.29, ...), custom_call_target="tpu_custom_call" | custom-call | flops 1140850688 | bytes 3932160 | tf_op jit(solution)/shard_map/pallas_call | solution.py:118
  91.5 4.3 %all-to-all-start.2 = ((bf16[4,128,768]{2,1,0:T(8,128)(2,1)}), bf16[4,128,768]{2,1,0:T(8,128)(2,1)S(1)}, u32[]{:S(2)}, u32[]{:S(2)}) async-start(bf16[4,128,768]{2,1,0:T(8,128)(2,1)} %shard_map.101), calls=%async_computation.2 | async-start | bytes 1572864 | tf_op jit(solution)/shard_map/all_to_all | solution.py:213
  95.8 0.0 copy-done.1
  95.8 0.0 copy-done.9
  95.8 2.9 %collective-permute-start.4 = (bf16[96,2048]{1,0:T(8,128)(2,1)S(1)}, bf16[96,2048]{1,0:T(8,128)(2,1)S(1)}, u32[]{:S(2)}, u32[]{:S(2)}) collective-permute-start(bf16[96,2048]{1,0:T(8,128)(2,1)S(1)} %fusion), channel_id=1, source_target_pairs={{0,4},{4,8},{8,12},{12,0},{1,5},{5,9},{9,13},{13,1},{2,6},{6,10},{... | collective-permute-start | bytes 1179656 | tf_op jit(solution)/shard_map/ppermute | solution.py:193
  98.8 4.9 %collective-permute-start.5 = (bf16[96,2048]{1,0:T(8,128)(2,1)S(1)}, bf16[96,2048]{1,0:T(8,128)(2,1)S(1)}, u32[]{:S(2)}, u32[]{:S(2)}) collective-permute-start(bf16[96,2048]{1,0:T(8,128)(2,1)S(1)} %fusion), channel_id=1, source_target_pairs={{0,8},{4,12},{8,0},{12,4},{1,9},{5,13},{9,1},{13,5},{2,10},{6,14},... | collective-permute-start | bytes 1179656 | tf_op jit(solution)/shard_map/ppermute | solution.py:193
  103.7 2.1 %collective-permute-start.6 = (bf16[96,2048]{1,0:T(8,128)(2,1)S(1)}, bf16[96,2048]{1,0:T(8,128)(2,1)S(1)}, u32[]{:S(2)}, u32[]{:S(2)}) collective-permute-start(bf16[96,2048]{1,0:T(8,128)(2,1)S(1)} %fusion), channel_id=1, source_target_pairs={{0,12},{4,0},{8,4},{12,8},{1,13},{5,1},{9,5},{13,9},{2,14},{6,2},{... | collective-permute-start | bytes 1179656 | tf_op jit(solution)/shard_map/ppermute | solution.py:193
  105.9 4.2 %collective-permute-done.4.one_ref = bf16[96,2048]{1,0:T(8,128)(2,1)S(1)} collective-permute-done((bf16[96,2048]{1,0:T(8,128)(2,1)S(1)}, bf16[96,2048]{1,0:T(8,128)(2,1)S(1)}, u32[]{:S(2)}, u32[]{:S(2)}) %collective-permute-start.4) | collective-permute-done | bytes 393248 | tf_op jit(solution)/shard_map/ppermute | solution.py:193
  110.1 8.7 %collective-permute-done.5.two_ref = bf16[96,2048]{1,0:T(8,128)(2,1)S(1)} collective-permute-done((bf16[96,2048]{1,0:T(8,128)(2,1)S(1)}, bf16[96,2048]{1,0:T(8,128)(2,1)S(1)}, u32[]{:S(2)}, u32[]{:S(2)}) %collective-permute-start.5) | collective-permute-done | bytes 393248 | tf_op jit(solution)/shard_map/ppermute | solution.py:193
  118.8 1.7 %collective-permute-done.6.three_ref = bf16[96,2048]{1,0:T(8,128)(2,1)S(1)} collective-permute-done((bf16[96,2048]{1,0:T(8,128)(2,1)S(1)}, bf16[96,2048]{1,0:T(8,128)(2,1)S(1)}, u32[]{:S(2)}, u32[]{:S(2)}) %collective-permute-start.6) | collective-permute-done | bytes 393248 | tf_op jit(solution)/shard_map/ppermute | solution.py:193
  120.5 0.1 pad_maximum_fusion.1
  120.6 1.9 %collective-permute-start.7 = (bf16[3,96,2048]{2,1,0:T(8,128)(2,1)S(1)}, bf16[3,96,2048]{2,1,0:T(8,128)(2,1)S(1)}, u32[]{:S(2)}, u32[]{:S(2)}) collective-permute-start(bf16[3,96,2048]{2,1,0:T(8,128)(2,1)S(1)} %pad_maximum_fusion.1), channel_id=1, source_target_pairs={{0,1},{1,0},{2,3},{3,2},{4,5},{5,4},{6,7},{7,6},{8,9},{9,8},{10,11... | collective-permute-start | bytes 3538952 | tf_op jit(solution)/shard_map/ppermute | solution.py:210
  122.6 0.0 copy-done.12
  122.6 0.9 slice_bitcast_fusion.own_ref
  123.5 1.8 %collective-permute-done.7.other_ref = bf16[3,96,2048]{2,1,0:T(8,128)(2,1)S(1)} collective-permute-done((bf16[3,96,2048]{2,1,0:T(8,128)(2,1)S(1)}, bf16[3,96,2048]{2,1,0:T(8,128)(2,1)S(1)}, u32[]{:S(2)}, u32[]{:S(2)}) %collective-permute-start.7) | collective-permute-done | bytes 1179680 | tf_op jit(solution)/shard_map/ppermute | solution.py:210
  125.4 1.0 copy-done.5
  126.4 0.0 all-to-all-done.2.all_ref
  126.4 1.3 copy-done.6
  127.7 3.8 %shard_map.102 = bf16[128,768]{1,0:T(8,128)(2,1)S(1)} custom-call(bf16[4,128,768]{2,1,0:T(8,128)(2,1)S(1)} %all-to-all-done.2.all_ref, bf16[128,768]{1,0:T(8,128)(2,1)S(1)} %slice_bitcast_fusion.own_ref, f32[1,768]{1,0:T(1,128)S(1)} %reshape.27.gain_ref, bf16[192,1536]{1,0:T(8,128)(2,1)S(1)} %copy-done.1, bf16[192,512]{1,0:T(8,128)(2,1)S(1)} %bitcast.31, ...), custom_call_target="tpu_custom_call" | custom-call | flops 1140850688 | bytes 3932160 | tf_op jit(solution)/shard_map/pallas_call | solution.py:118
  131.5 22.9 %all_to_all.21 = bf16[8,16,768]{2,1,0:T(8,128)(2,1)S(1)} all-to-all(bf16[8,16,768]{2,1,0:T(8,128)(2,1)S(1)} %bitcast.24), channel_id=1, replica_groups={{0,32,64,96,128,160,192,224},{16,48,80,112,144,176,208,240},{256,288,32..., dimensions={0} | all-to-all | bytes 393216 | tf_op jit(solution)/shard_map/all_to_all | solution.py:217
  154.4 0.7 copy.12
  (14 shorter events, 0.1 us)
Async XLA Ops:
  14.6 1.7 %copy-start.2 = (bf16[768,1536]{1,0:T(8,128)(2,1)S(1)}, bf16[768,1536]{1,0:T(8,128)(2,1)}, u32[]{:S(2)}) copy-start(bf16[768,1536]{1,0:T(8,128)(2,1)} %qkv_ref.1) | copy-start | bytes 7077892
  16.2 0.9 copy-start.7
  17.1 1.1 copy-start.10
  51.7 7.4 %copy-start = (bf16[192,1536]{1,0:T(8,128)(2,1)S(1)}, bf16[192,1536]{1,0:T(8,128)(2,1)}, u32[]{:S(2)}) copy-start(bf16[192,1536]{1,0:T(8,128)(2,1)} %qkv_ref.2) | copy-start | bytes 1769476
  51.7 7.4 %copy-start.8 = (bf16[512,192]{0,1:T(8,128)(2,1)S(1)}, bf16[512,192]{0,1:T(8,128)(2,1)}, u32[]{:S(2)}) copy-start(bf16[512,192]{0,1:T(8,128)(2,1)} %param.16) | copy-start | bytes 589828
  52.6 32.9 %all-to-all-start.1 = ((bf16[4,128,768]{2,1,0:T(8,128)(2,1)}), bf16[4,128,768]{2,1,0:T(8,128)(2,1)S(1)}, u32[]{:S(2)}, u32[]{:S(2)}) async-start(bf16[4,128,768]{2,1,0:T(8,128)(2,1)} %broadcast_in_dim.8), calls=%async_computation.1 | async-start | bytes 1572864 | tf_op jit(solution)/shard_map/all_to_all | solution.py:135
  59.1 17.9 %collective-permute-start = (bf16[96,2048]{1,0:T(8,128)(2,1)S(1)}, bf16[96,2048]{1,0:T(8,128)(2,1)S(1)}, u32[]{:S(2)}, u32[]{:S(2)}) collective-permute-start(bf16[96,2048]{1,0:T(8,128)(2,1)S(1)} %fusion.1), channel_id=1, source_target_pairs={{0,4},{4,8},{8,12},{12,0},{1,5},{5,9},{9,13},{13,1},{2,6},{6,10},{... | collective-permute-start | bytes 1179656 | tf_op jit(solution)/shard_map/ppermute | solution.py:193
  61.3 15.7 %collective-permute-start.1 = (bf16[96,2048]{1,0:T(8,128)(2,1)S(1)}, bf16[96,2048]{1,0:T(8,128)(2,1)S(1)}, u32[]{:S(2)}, u32[]{:S(2)}) collective-permute-start(bf16[96,2048]{1,0:T(8,128)(2,1)S(1)} %fusion.1), channel_id=1, source_target_pairs={{0,8},{4,12},{8,0},{12,4},{1,9},{5,13},{9,1},{13,5},{2,10},{6,14},... | collective-permute-start | bytes 1179656 | tf_op jit(solution)/shard_map/ppermute | solution.py:193
  65.9 13.7 %collective-permute-start.2 = (bf16[96,2048]{1,0:T(8,128)(2,1)S(1)}, bf16[96,2048]{1,0:T(8,128)(2,1)S(1)}, u32[]{:S(2)}, u32[]{:S(2)}) collective-permute-start(bf16[96,2048]{1,0:T(8,128)(2,1)S(1)} %fusion.1), channel_id=1, source_target_pairs={{0,12},{4,0},{8,4},{12,8},{1,13},{5,1},{9,5},{13,9},{2,14},{6,2},{... | collective-permute-start | bytes 1179656 | tf_op jit(solution)/shard_map/ppermute | solution.py:193
  79.6 2.1 %copy-start.11 = (f32[768]{0:T(1024)S(1)}, f32[768]{0:T(1024)}, u32[]{:S(2)}) copy-start(f32[768]{0:T(1024)} %param.14) | copy-start | bytes 9220
  79.7 4.7 %collective-permute-start.3 = (bf16[3,96,2048]{2,1,0:T(8,128)(2,1)S(1)}, bf16[3,96,2048]{2,1,0:T(8,128)(2,1)S(1)}, u32[]{:S(2)}, u32[]{:S(2)}) collective-permute-start(bf16[3,96,2048]{2,1,0:T(8,128)(2,1)S(1)} %pad_maximum_fusion), channel_id=1, source_target_pairs={{0,1},{1,0},{2,3},{3,2},{4,5},{5,4},{6,7},{7,6},{8,9},{9,8},{10,11... | collective-permute-start | bytes 3538952 | tf_op jit(solution)/shard_map/ppermute | solution.py:209
  84.5 1.0 copy-start.3
  85.5 1.3 copy-start.4
  91.5 4.3 %copy-start.1 = (bf16[192,1536]{1,0:T(8,128)(2,1)S(1)}, bf16[192,1536]{1,0:T(8,128)(2,1)}, u32[]{:S(2)}) copy-start(bf16[192,1536]{1,0:T(8,128)(2,1)} %qkv_ref.3) | copy-start | bytes 1769476
  91.5 4.3 %copy-start.9 = (bf16[512,192]{0,1:T(8,128)(2,1)S(1)}, bf16[512,192]{0,1:T(8,128)(2,1)}, u32[]{:S(2)}) copy-start(bf16[512,192]{0,1:T(8,128)(2,1)} %param.19) | copy-start | bytes 589828
  91.5 34.9 %all-to-all-start.2 = ((bf16[4,128,768]{2,1,0:T(8,128)(2,1)}), bf16[4,128,768]{2,1,0:T(8,128)(2,1)S(1)}, u32[]{:S(2)}, u32[]{:S(2)}) async-start(bf16[4,128,768]{2,1,0:T(8,128)(2,1)} %shard_map.101), calls=%async_computation.2 | async-start | bytes 1572864 | tf_op jit(solution)/shard_map/all_to_all | solution.py:213
  95.8 14.2 %collective-permute-start.4 = (bf16[96,2048]{1,0:T(8,128)(2,1)S(1)}, bf16[96,2048]{1,0:T(8,128)(2,1)S(1)}, u32[]{:S(2)}, u32[]{:S(2)}) collective-permute-start(bf16[96,2048]{1,0:T(8,128)(2,1)S(1)} %fusion), channel_id=1, source_target_pairs={{0,4},{4,8},{8,12},{12,0},{1,5},{5,9},{9,13},{13,1},{2,6},{6,10},{... | collective-permute-start | bytes 1179656 | tf_op jit(solution)/shard_map/ppermute | solution.py:193
  98.8 20.0 %collective-permute-start.5 = (bf16[96,2048]{1,0:T(8,128)(2,1)S(1)}, bf16[96,2048]{1,0:T(8,128)(2,1)S(1)}, u32[]{:S(2)}, u32[]{:S(2)}) collective-permute-start(bf16[96,2048]{1,0:T(8,128)(2,1)S(1)} %fusion), channel_id=1, source_target_pairs={{0,8},{4,12},{8,0},{12,4},{1,9},{5,13},{9,1},{13,5},{2,10},{6,14},... | collective-permute-start | bytes 1179656 | tf_op jit(solution)/shard_map/ppermute | solution.py:193
  103.7 16.8 %collective-permute-start.6 = (bf16[96,2048]{1,0:T(8,128)(2,1)S(1)}, bf16[96,2048]{1,0:T(8,128)(2,1)S(1)}, u32[]{:S(2)}, u32[]{:S(2)}) collective-permute-start(bf16[96,2048]{1,0:T(8,128)(2,1)S(1)} %fusion), channel_id=1, source_target_pairs={{0,12},{4,0},{8,4},{12,8},{1,13},{5,1},{9,5},{13,9},{2,14},{6,2},{... | collective-permute-start | bytes 1179656 | tf_op jit(solution)/shard_map/ppermute | solution.py:193
  120.5 2.1 %copy-start.12 = (f32[768]{0:T(1024)S(1)}, f32[768]{0:T(1024)}, u32[]{:S(2)}) copy-start(f32[768]{0:T(1024)} %param.17) | copy-start | bytes 9220
  120.6 4.7 %collective-permute-start.7 = (bf16[3,96,2048]{2,1,0:T(8,128)(2,1)S(1)}, bf16[3,96,2048]{2,1,0:T(8,128)(2,1)S(1)}, u32[]{:S(2)}, u32[]{:S(2)}) collective-permute-start(bf16[3,96,2048]{2,1,0:T(8,128)(2,1)S(1)} %pad_maximum_fusion.1), channel_id=1, source_target_pairs={{0,1},{1,0},{2,3},{3,2},{4,5},{5,4},{6,7},{7,6},{8,9},{9,8},{10,11... | collective-permute-start | bytes 3538952 | tf_op jit(solution)/shard_map/ppermute | solution.py:210
  125.4 1.0 copy-start.5
  126.4 1.3 copy-start.6

commit v3 on v1

v3 whole, which is shorter than its diff:
```python
import jax
import jax.numpy as jnp
from jax import lax
from jax.experimental import pallas as pl
from jax.experimental.pallas import tpu as pltpu
from jax.sharding import PartitionSpec as P


HEAD_DIM = 64
EPSILON = 1e-06
PAIR = 2 * HEAD_DIM


def attend(own, all_ref, gain_ref, waits, weight_ref, out_ref, contract, normed_ref, kv_ref, between=None):
    chunks, tokens, width = all_ref.shape
    inner = kv_ref.shape[1] // 2
    gain = gain_ref[...].reshape(1, width)
    for chunk in range(chunks):
        values = all_ref[chunk].astype(jnp.float32)
        factor = lax.rsqrt(jnp.mean(values * values, axis=-1, keepdims=True) + EPSILON)
        normed_ref[chunk * tokens : (chunk + 1) * tokens, :] = (values * factor * gain).astype(
            jnp.bfloat16
        )
    for part in range(2):
        waits[1 + part]()
        for chunk in range(chunks):
            rows = slice(chunk * tokens, (chunk + 1) * tokens)
            kv_ref[rows, part * inner : (part + 1) * inner] = jnp.dot(
                normed_ref[rows, :],
                weight_ref[:, (1 + part) * inner : (2 + part) * inner],
                preferred_element_type=jnp.float32,
            ).astype(jnp.bfloat16)
    waits[0]()
    normed = normed_ref[pl.ds(pl.multiple_of(own * tokens, tokens), tokens), :]
    queries = jnp.dot(
        normed, weight_ref[:, :inner], preferred_element_type=jnp.float32
    ).astype(jnp.bfloat16) * jnp.bfloat16(HEAD_DIM ** (-0.5))
    if between is not None:
        between()
    first = lax.broadcasted_iota(jnp.int32, (tokens, PAIR), 1) < HEAD_DIM
    attended = []
    for pair in range(inner // PAIR):
        columns = slice(pair * PAIR, (pair + 1) * PAIR)
        query = queries[:, columns]
        keys = kv_ref[:, columns]
        values = kv_ref[:, inner + pair * PAIR : inner + (pair + 1) * PAIR]
        halves = []
        for mask in (first, jnp.logical_not(first)):
            scores = lax.dot_general(
                jnp.where(mask, query, jnp.zeros_like(query)),
                keys,
                (((1,), (1,)), ((), ())),
                preferred_element_type=jnp.float32,
            )
            weights = jnp.exp(scores - jnp.max(scores, axis=-1, keepdims=True))
            total = jnp.sum(weights, axis=-1, keepdims=True)
            mixed = jnp.dot(
                weights.astype(jnp.bfloat16), values, preferred_element_type=jnp.float32
            )
            halves.append(mixed / total)
        attended.append(jnp.where(first, halves[0], halves[1]).astype(jnp.bfloat16))
    waits[3]()
    update = lax.dot_general(
        jnp.concatenate(attended, axis=1), out_ref[...], contract, preferred_element_type=jnp.float32
    )
    return (all_ref[own].astype(jnp.float32) + update).astype(jnp.bfloat16)


def started(copies):
    for copy in copies:
        copy.start()

    def wait():
        for copy in copies:
            copy.wait()

    return wait


def frame_body(
    all_ref,
    gain_ref,
    qkv_ref,
    out_ref,
    *refs,
):
    shards, results, scratch = refs[:4], refs[4:9], refs[9:]
    weight_ref, mix_ref, normed_ref, kv_ref, whole_ref, sems = scratch
    inner = kv_ref.shape[1] // 2
    band = lax.axis_index("band")
    core = lax.rem(lax.axis_index("batch"), 2)
    waits = {}
    for order, part in enumerate((1, 2, 0)):
        columns = slice(part * inner, (part + 1) * inner)
        waits[part] = started(
            [pltpu.make_async_copy(qkv_ref.at[:, columns], weight_ref.at[:, columns], sems.at[order])]
        )
    waits[3] = started([pltpu.make_async_copy(out_ref, mix_ref, sems.at[3])])
    loads = [
        started(
            [
                pltpu.make_async_copy(
                    shards[2 * layer], whole_ref.at[layer, :, : 3 * inner], sems.at[4 + 2 * layer]
                ),
                pltpu.make_async_copy(
                    shards[2 * layer + 1], whole_ref.at[layer, :, 3 * inner :], sems.at[5 + 2 * layer]
                ),
            ]
        )
        for layer in range(2)
    ]
    stores = []

    def between():
        for layer, wait in enumerate(loads):
            near, far = results[1 + 2 * layer : 3 + 2 * layer]
            rows = far.shape[0]
            half = pl.ds(pl.multiple_of(core * rows, rows), rows)
            wait()
            stores.append(
                started(
                    [
                        pltpu.make_async_copy(whole_ref.at[layer], near, sems.at[8 + 2 * layer]),
                        pltpu.make_async_copy(whole_ref.at[layer, half, :], far, sems.at[9 + 2 * layer]),
                    ]
                )
            )

    results[0][...] = attend(
        band,
        all_ref,
        gain_ref,
        waits,
        weight_ref,
        mix_ref,
        (((1,), (0,)), ((), ())),
        normed_ref,
        kv_ref,
        between,
    )
    for wait in stores:
        wait()


def kept(*arrays):
    return [pltpu.with_memory_space_constraint(array, pltpu.HBM) for array in arrays]


def frame_layer(everything, gain, qkv, out, shards):
    chunks, tokens, width = everything.shape
    inner = out.shape[0]
    count = chunks * tokens
    rows = shards[0].shape[0]
    near = jax.ShapeDtypeStruct((rows, 4 * inner), jnp.bfloat16)
    far = jax.ShapeDtypeStruct((rows // 2, 4 * inner), jnp.bfloat16)
    vmem = pl.BlockSpec(memory_space=pltpu.VMEM)
    return pl.pallas_call(
        frame_body,
        out_shape=(jax.ShapeDtypeStruct((tokens, width), jnp.bfloat16), near, far, near, far),
        in_specs=[vmem, vmem] + [pl.BlockSpec(memory_space=pltpu.HBM)] * 6,
        out_specs=(vmem,) + (pl.BlockSpec(memory_space=pltpu.HBM),) * 4,
        scratch_shapes=[
            pltpu.VMEM((width, 3 * inner), jnp.bfloat16),
            pltpu.VMEM((inner, width), jnp.bfloat16),
            pltpu.VMEM((count, width), jnp.bfloat16),
            pltpu.VMEM((count, 2 * inner), jnp.bfloat16),
            pltpu.VMEM((2, rows, 4 * inner), jnp.bfloat16),
            pltpu.SemaphoreType.DMA((12,)),
        ],
        compiler_params=pltpu.CompilerParams(vmem_limit_bytes=20 << 20),
        cost_estimate=estimate(chunks, tokens, width, inner),
        name="frame",
    )(everything, gain, *kept(qkv, out, *shards))


def estimate(chunks, tokens, width, inner):
    count = chunks * tokens
    return pl.CostEstimate(
        flops=4 * count * width * inner + 4 * tokens * width * inner + 4 * tokens * count * inner,
        bytes_accessed=2 * (count * width + 4 * width * inner),
        transcendentals=tokens * count * inner // HEAD_DIM,
    )


def row_body(
    all_ref, gain_ref, qkv_ref, out_ref, near_ref, far_ref, other_ref, result_ref, weight_ref, normed_ref, kv_ref, sems
):
    chunks = all_ref.shape[0]
    inner = kv_ref.shape[1] // 2
    rows = far_ref.shape[0]
    bands = lax.axis_size("band")
    band = lax.axis_index("band")
    core = lax.rem(lax.axis_index("batch"), 2)
    view = lax.axis_index("view")
    deep = lax.axis_size("view") // 2
    left = lax.rem(view, 2)
    own = jnp.where(view < deep, left, chunks - 1 - left)

    def place(index, half, count):
        return pl.ds(pl.multiple_of((2 * lax.rem(index, bands) + half) * rows, rows), count)

    down, up = band + bands - 1, band + 1
    target = (
        place(band, 0, 2 * rows),
        place(down + 2 * core, 0, 2 * rows),
        place(band + 2, core, rows),
        place(up + 2 * core, 0, 2 * rows),
        place(band + 2, 1 - core, rows),
    )
    waits = {}
    for order, part in enumerate((1, 2, 0, 3)):
        columns = slice(part * inner, (part + 1) * inner)
        sources = (
            out_ref if part == 3 else qkv_ref.at[:, columns],
            near_ref.at[:, columns],
            far_ref.at[:, columns],
            other_ref.at[: 2 * rows, columns],
            other_ref.at[2 * rows :, columns],
        )
        waits[part] = started(
            [
                pltpu.make_async_copy(source, weight_ref.at[goal, columns], sems.at[order, index])
                for index, (source, goal) in enumerate(zip(sources, target))
            ]
        )
    stream = attend(
        own,
        all_ref,
        gain_ref,
        waits,
        weight_ref,
        weight_ref.at[:, 3 * inner :],
        (((1,), (1,)), ((), ())),
        normed_ref,
        kv_ref,
    )
    if len(result_ref.shape) == 2:
        result_ref[...] = stream
    else:
        for copy in range(result_ref.shape[0]):
            result_ref[copy] = stream


def row_layer(everything, gain, weights, copies=None):
    chunks, tokens, width = everything.shape
    inner = weights[0].shape[1] // 3
    shape = (tokens, width) if copies is None else (copies, tokens, width)
    count = chunks * tokens
    vmem = pl.BlockSpec(memory_space=pltpu.VMEM)
    return pl.pallas_call(
        row_body,
        out_shape=jax.ShapeDtypeStruct(shape, jnp.bfloat16),
        in_specs=[vmem, vmem] + [pl.BlockSpec(memory_space=pltpu.HBM)] * 5,
        out_specs=vmem,
        scratch_shapes=[
            pltpu.VMEM((width, 4 * inner), jnp.bfloat16),
            pltpu.VMEM((count, width), jnp.bfloat16),
            pltpu.VMEM((count, 2 * inner), jnp.bfloat16),
            pltpu.SemaphoreType.DMA((4, 5)),
        ],
        compiler_params=pltpu.CompilerParams(vmem_limit_bytes=20 << 20),
        cost_estimate=estimate(chunks, tokens, width, inner),
    )(everything, gain, *kept(*weights))


def exchanged(stream, rows, groups):
    tokens, width = stream.shape
    return lax.all_to_all(
        stream.reshape(rows, tokens // rows, width),
        "view",
        split_axis=0,
        concat_axis=0,
        tiled=True,
        axis_index_groups=groups,
    ).reshape(tokens, width)


def shared(copies, groups):
    return lax.all_to_all(
        copies, "view", split_axis=0, concat_axis=0, tiled=True, axis_index_groups=groups
    )


def layers(
    images,
    frame_gain,
    frame_qkv,
    frame_out,
    row1_gain,
    row1_qkv,
    row1_out,
    row2_gain,
    row2_qkv,
    row2_out,
):
    _, row_count, col_count, width = images.shape
    tokens = row_count * col_count
    views = lax.axis_size("view")
    bands = lax.axis_size("band")
    batches = lax.axis_size("batch")
    share = views // row_count
    near = 2
    deep = views // near
    side = share // near
    spread = [
        [y * deep + h * side + l for h in range(row_count)] for y in range(near) for l in range(side)
    ]
    ring = [
        [h * side + l for l in range(side)] + [deep + h * side + l for l in reversed(range(side))]
        for h in range(row_count)
    ]
    siblings = [(i, i ^ 1) for i in range(batches)]
    turn = [
        (b * batches + c, ((b + 1 - 2 * (c % 2)) % bands) * batches + c)
        for b in range(bands)
        for c in range(batches)
    ]
    across = [(b, (b + 2) % bands) for b in range(bands)]

    everything = lax.all_gather(images.reshape(tokens, width), "band", axis=0, tiled=False)
    shards = (row1_qkv, row1_out.T, row2_qkv, row2_out.T)
    stream, near1, far1, near2, far2 = frame_layer(
        everything, frame_gain, frame_qkv, frame_out, shards
    )
    stream = exchanged(stream, row_count, spread)
    near1 = lax.ppermute(near1, ("band", "batch"), turn)
    far1 = lax.ppermute(far1, "band", across)
    near2 = lax.ppermute(near2, ("band", "batch"), turn)
    far2 = lax.ppermute(far2, "band", across)
    gain1 = row1_gain.reshape(1, width)
    gain2 = row2_gain.reshape(1, width)
    other1 = lax.ppermute(jnp.concatenate([near1, far1]), "batch", siblings)
    other2 = lax.ppermute(jnp.concatenate([near2, far2]), "batch", siblings)
    everything = shared(jnp.broadcast_to(stream[None], (share, tokens, width)), ring)
    copies = row_layer(everything, gain1, (*shards[:2], near1, far1, other1), share)
    everything = shared(copies, ring)
    stream = row_layer(everything, gain2, (*shards[2:], near2, far2, other2))
    stream = exchanged(stream, row_count, spread)
    return stream.reshape(images.shape)


def solution(mesh):
    in_specs = (
        P(("batch", "view"), "band", None, None),
        P(),
        P(),
        P(),
        P(),
        P("band", None),
        P(None, "band"),
        P(),
        P("band", None),
        P(None, "band"),
    )
    out_specs = P(("batch", "view"), "band", None, None)
    return jax.shard_map(layers, mesh=mesh, in_specs=in_specs, out_specs=out_specs, check_vma=False)
```

time: 154 us -> 152 us (0.987)
  the two profiles are of different devices: /device:TPU:8 before, /device:TPU:56 now
where the time goes in v3:
time: 152 us
  blocking collectives  65.9 us (43%)
  waiting for transfers between devices  38.3 us (25%)
  starting transfers between devices  26.2 us (17%)
  Pallas kernels  17.6 us (12%)
  local copies, waits for them, and re-layouts  3.09 us (2%)
    all_to_all x2, blocking collectives, exchanged(): lax.all_to_all(stream.reshape(rows, tokens // rows, width), 'view', split...  52.1 us
    ppermute x1, waiting for transfers between devices, layers(): far2 = lax.ppermute(far2, 'band', across)  16.5 us
    all_gather x1, blocking collectives, layers(): lax.all_gather(images.reshape(tokens, width), 'band', axis=0, tiled=False)  13.9 us
    ppermute x1, waiting for transfers between devices, layers(): far1 = lax.ppermute(far1, 'band', across)  13.8 us
    pallas_call x2, Pallas kernels, row_layer(): pl.pallas_call(row_body, out_shape=jax.ShapeDtypeStruct(shape, jnp.bfloat...  11.9 us
    all_to_all x2, starting transfers between devices, shared(): lax.all_to_all(copies, 'view', split_axis=0, concat_axis=0, tiled=True, a...  10.7 us
    pallas_call x1, Pallas kernels, frame_layer(): pl.pallas_call(frame_body, out_shape=(jax.ShapeDtypeStruct((tokens, width...  5.74 us
    ppermute x1, starting transfers between devices, layers(): far1 = lax.ppermute(far1, 'band', across)  4.58 us
  transfers between devices with their start and end apart: 8, of which 5 were waited for; matrix products, arithmetic and copies ran while one was open for 0% of the time, Pallas kernels for 0%

profile of v3, /device:TPU:56, one launch (start us, length us, event | category | flops | bytes accessed | tf_op | source)
XLA Modules:
  0.0 151.5 jit_solution(4943349151292160679)
XLA Ops:
  0.0 13.9 %all_gather.3.all_ref = bf16[4,128,768]{2,1,0:T(8,128)(2,1)S(1)} all-gather(bf16[1,128,768]{2,1,0:T(8,128)(2,1)} %bitcast.15), channel_id=1, replica_groups=mesh['view'=32,'band'=4,'batch'=4] {'band'}, dimensions={0}, use_global_device_ids=true | all-gather | bytes 983040 | tf_op jit(solution)/shard_map/all_gather | solution.py:320
  13.9 0.0 copy-start
  13.9 0.7 copy-done
  14.5 5.7 %frame.1 = (bf16[128,768]{1,0:T(8,128)(2,1)S(1)}, bf16[192,2048]{1,0:T(8,128)(2,1)S(1)}, bf16[96,2048]{1,0:T(8,128)(2,1)S(1)}, bf16[192,2048]{1,0:T(8,128)(2,1)S(1)}, bf16[96,2048]{1,0:T(8,128)(2,1)S(1)}) custom-call(bf16[4,128,768]{2,1,0:T(8,128)(2,1)S(1)} %all_gather.3.all_ref, f32[768]{0:T(1024)S(1)} %copy-done, bf16[768,1536]{1,0:T(8,128)(2,1)} %qkv_ref.3, ...), custom_call_target="tpu_custom_call" | custom-call | flops 1140850688 | bytes 3932160 | tf_op jit(solution)/shard_map/frame/pallas_call | solution.py:157
  20.3 29.6 %all_to_all.20 = bf16[8,16,768]{2,1,0:T(8,128)(2,1)S(1)} all-to-all(bf16[8,16,768]{2,1,0:T(8,128)(2,1)S(1)} %bitcast.7), channel_id=1, replica_groups={{0,32,64,96,128,160,192,224},{16,48,80,112,144,176,208,240},{256,288,32..., dimensions={0} | all-to-all | bytes 393216 | tf_op jit(solution)/shard_map/all_to_all | solution.py:268
  49.9 0.9 broadcast_in_dim.8
  50.9 6.5 %all-to-all-start.1 = ((bf16[4,128,768]{2,1,0:T(8,128)(2,1)}), bf16[4,128,768]{2,1,0:T(8,128)(2,1)S(1)}, u32[]{:S(2)}, u32[]{:S(2)}) async-start(bf16[4,128,768]{2,1,0:T(8,128)(2,1)} %broadcast_in_dim.8), calls=%async_computation.1 | async-start | bytes 1572864 | tf_op jit(solution)/shard_map/all_to_all | solution.py:279
  57.4 2.2 %collective-permute-start = (bf16[192,2048]{1,0:T(8,128)(2,1)S(1)}, bf16[192,2048]{1,0:T(8,128)(2,1)S(1)}, u32[]{:S(2)}, u32[]{:S(2)}) collective-permute-start(bf16[192,2048]{1,0:T(8,128)(2,1)S(1)} %get-tuple-element.11), channel_id=1, source_target_pairs={{0,4},{1,13},{2,6},{3,15},{4,8},{5,1},{6,10},{7,3},{8,12},{9,5},{1... | collective-permute-start | bytes 2359304 | tf_op jit(solution)/shard_map/ppermute | solution.py:326
  59.6 0.0 copy-start.5
  59.6 4.6 %collective-permute-start.1 = (bf16[96,2048]{1,0:T(8,128)(2,1)S(1)}, bf16[96,2048]{1,0:T(8,128)(2,1)S(1)}, u32[]{:S(2)}, u32[]{:S(2)}) collective-permute-start(bf16[96,2048]{1,0:T(8,128)(2,1)S(1)} %get-tuple-element.12), channel_id=1, source_target_pairs={{0,8},{4,12},{8,0},{12,4},{1,9},{5,13},{9,1},{13,5},{2,10},{6,14},... | collective-permute-start | bytes 1179656 | tf_op jit(solution)/shard_map/ppermute | solution.py:327
  64.2 13.8 %collective-permute-done.1.far_ref = bf16[96,2048]{1,0:T(8,128)(2,1)S(1)} collective-permute-done((bf16[96,2048]{1,0:T(8,128)(2,1)S(1)}, bf16[96,2048]{1,0:T(8,128)(2,1)S(1)}, u32[]{:S(2)}, u32[]{:S(2)}) %collective-permute-start.1) | collective-permute-done | bytes 393248 | tf_op jit(solution)/shard_map/ppermute | solution.py:327
  78.0 0.0 copy-start.2
  78.0 0.0 collective-permute-done.near_ref
  78.0 0.0 copy-start.1
  78.0 0.1 pad_maximum_fusion
  78.2 1.9 %collective-permute-start.2 = (bf16[288,2048]{1,0:T(8,128)(2,1)S(1)}, bf16[288,2048]{1,0:T(8,128)(2,1)}, u32[]{:S(2)}, u32[]{:S(2)}) collective-permute-start(bf16[288,2048]{1,0:T(8,128)(2,1)S(1)} %pad_maximum_fusion), channel_id=1, source_target_pairs={{0,1},{1,0},{2,3},{3,2},{4,5},{5,4},{6,7},{7,6},{8,9},{9,8},{10,11... | collective-permute-start | bytes 3538952 | tf_op jit(solution)/shard_map/ppermute | solution.py:332
  80.1 0.0 copy-done.5
  80.1 0.0 copy-done.2
  80.1 0.0 copy-done.1
  80.1 2.9 %collective-permute-done.2.other_ref = bf16[288,2048]{1,0:T(8,128)(2,1)} collective-permute-done((bf16[288,2048]{1,0:T(8,128)(2,1)S(1)}, bf16[288,2048]{1,0:T(8,128)(2,1)}, u32[]{:S(2)}, u32[]{:S(2)}) %collective-permute-start.2) | collective-permute-done | bytes 1179680 | tf_op jit(solution)/shard_map/ppermute | solution.py:332
  83.0 0.0 all-to-all-done.1.all_ref
  83.0 6.4 %shard_map.100 = bf16[4,128,768]{2,1,0:T(8,128)(2,1)} custom-call(bf16[4,128,768]{2,1,0:T(8,128)(2,1)S(1)} %all-to-all-done.1.all_ref, f32[1,768]{1,0:T(1,128)S(1)} %reshape.14.gain_ref, bf16[192,1536]{1,0:T(8,128)(2,1)} %qkv_ref.4, bf16[192,512]{1,0:T(8,128)(2,1)} %bitcast.10, bf16[192,2048]{1,0:T(8,128)(2,1)} %copy-done.1, bf16[96,2048]{1,0:T(8,128)(2,1)} %copy-done.2, ...), custom_call_target="tpu_custom_call" | custom-call | flops 1140850688 | bytes 3932160 | tf_op jit(solution)/shard_map/pallas_call | solution.py:250
  89.4 4.2 %all-to-all-start.2 = ((bf16[4,128,768]{2,1,0:T(8,128)(2,1)}), bf16[4,128,768]{2,1,0:T(8,128)(2,1)S(1)}, u32[]{:S(2)}, u32[]{:S(2)}) async-start(bf16[4,128,768]{2,1,0:T(8,128)(2,1)} %shard_map.100), calls=%async_computation.2 | async-start | bytes 1572864 | tf_op jit(solution)/shard_map/all_to_all | solution.py:279
  93.7 1.9 %collective-permute-start.3 = (bf16[192,2048]{1,0:T(8,128)(2,1)S(1)}, bf16[192,2048]{1,0:T(8,128)(2,1)S(1)}, u32[]{:S(2)}, u32[]{:S(2)}) collective-permute-start(bf16[192,2048]{1,0:T(8,128)(2,1)S(1)} %get-tuple-element.13), channel_id=1, source_target_pairs={{0,4},{1,13},{2,6},{3,15},{4,8},{5,1},{6,10},{7,3},{8,12},{9,5},{1... | collective-permute-start | bytes 2359304 | tf_op jit(solution)/shard_map/ppermute | solution.py:328
  95.6 0.0 copy-start.6
  95.6 3.0 %collective-permute-start.4 = (bf16[96,2048]{1,0:T(8,128)(2,1)S(1)}, bf16[96,2048]{1,0:T(8,128)(2,1)S(1)}, u32[]{:S(2)}, u32[]{:S(2)}) collective-permute-start(bf16[96,2048]{1,0:T(8,128)(2,1)S(1)} %get-tuple-element.14), channel_id=1, source_target_pairs={{0,8},{4,12},{8,0},{12,4},{1,9},{5,13},{9,1},{13,5},{2,10},{6,14},... | collective-permute-start | bytes 1179656 | tf_op jit(solution)/shard_map/ppermute | solution.py:329
  98.6 16.5 %collective-permute-done.4.far_ref = bf16[96,2048]{1,0:T(8,128)(2,1)S(1)} collective-permute-done((bf16[96,2048]{1,0:T(8,128)(2,1)S(1)}, bf16[96,2048]{1,0:T(8,128)(2,1)S(1)}, u32[]{:S(2)}, u32[]{:S(2)}) %collective-permute-start.4) | collective-permute-done | bytes 393248 | tf_op jit(solution)/shard_map/ppermute | solution.py:329
  115.1 0.0 copy-start.4
  115.1 2.0 %collective-permute-done.3.near_ref = bf16[192,2048]{1,0:T(8,128)(2,1)S(1)} collective-permute-done((bf16[192,2048]{1,0:T(8,128)(2,1)S(1)}, bf16[192,2048]{1,0:T(8,128)(2,1)S(1)}, u32[]{:S(2)}, u32[]{:S(2)}) %collective-permute-start.3) | collective-permute-done | bytes 786464 | tf_op jit(solution)/shard_map/ppermute | solution.py:328
  117.2 0.0 copy-start.3
  117.2 0.1 pad_maximum_fusion.1
  117.3 0.0 copy-done.4
  117.3 0.7 copy-done.3
  118.0 1.9 %collective-permute-start.5 = (bf16[288,2048]{1,0:T(8,128)(2,1)S(1)}, bf16[288,2048]{1,0:T(8,128)(2,1)}, u32[]{:S(2)}, u32[]{:S(2)}) collective-permute-start(bf16[288,2048]{1,0:T(8,128)(2,1)S(1)} %pad_maximum_fusion.1), channel_id=1, source_target_pairs={{0,1},{1,0},{2,3},{3,2},{4,5},{5,4},{6,7},{7,6},{8,9},{9,8},{10,11... | collective-permute-start | bytes 3538952 | tf_op jit(solution)/shard_map/ppermute | solution.py:333
  120.0 0.0 copy-done.6
  120.0 2.9 %collective-permute-done.5.other_ref = bf16[288,2048]{1,0:T(8,128)(2,1)} collective-permute-done((bf16[288,2048]{1,0:T(8,128)(2,1)S(1)}, bf16[288,2048]{1,0:T(8,128)(2,1)}, u32[]{:S(2)}, u32[]{:S(2)}) %collective-permute-start.5) | collective-permute-done | bytes 1179680 | tf_op jit(solution)/shard_map/ppermute | solution.py:333
  122.9 0.0 all-to-all-done.2.all_ref
  122.9 5.5 %shard_map.101 = bf16[128,768]{1,0:T(8,128)(2,1)S(1)} custom-call(bf16[4,128,768]{2,1,0:T(8,128)(2,1)S(1)} %all-to-all-done.2.all_ref, f32[1,768]{1,0:T(1,128)S(1)} %reshape.15.gain_ref, bf16[192,1536]{1,0:T(8,128)(2,1)} %qkv_ref.5, bf16[192,512]{1,0:T(8,128)(2,1)} %bitcast.14, bf16[192,2048]{1,0:T(8,128)(2,1)} %copy-done.3, bf16[96,2048]{1,0:T(8,128)(2,1)} %copy-done.4, ...), custom_call_target="tpu_custom_call" | custom-call | flops 1140850688 | bytes 3932160 | tf_op jit(solution)/shard_map/pallas_call | solution.py:250
  128.4 22.4 %all_to_all.21 = bf16[8,16,768]{2,1,0:T(8,128)(2,1)S(1)} all-to-all(bf16[8,16,768]{2,1,0:T(8,128)(2,1)S(1)} %bitcast.8), channel_id=1, replica_groups={{0,32,64,96,128,160,192,224},{16,48,80,112,144,176,208,240},{256,288,32..., dimensions={0} | all-to-all | bytes 393216 | tf_op jit(solution)/shard_map/all_to_all | solution.py:268
  150.8 0.7 copy.12
  (2 shorter events, 0.0 us)
Async XLA Ops:
  13.9 0.7 copy-start
  50.9 32.1 %all-to-all-start.1 = ((bf16[4,128,768]{2,1,0:T(8,128)(2,1)}), bf16[4,128,768]{2,1,0:T(8,128)(2,1)S(1)}, u32[]{:S(2)}, u32[]{:S(2)}) async-start(bf16[4,128,768]{2,1,0:T(8,128)(2,1)} %broadcast_in_dim.8), calls=%async_computation.1 | async-start | bytes 1572864 | tf_op jit(solution)/shard_map/all_to_all | solution.py:279
  57.4 20.7 %collective-permute-start = (bf16[192,2048]{1,0:T(8,128)(2,1)S(1)}, bf16[192,2048]{1,0:T(8,128)(2,1)S(1)}, u32[]{:S(2)}, u32[]{:S(2)}) collective-permute-start(bf16[192,2048]{1,0:T(8,128)(2,1)S(1)} %get-tuple-element.11), channel_id=1, source_target_pairs={{0,4},{1,13},{2,6},{3,15},{4,8},{5,1},{6,10},{7,3},{8,12},{9,5},{1... | collective-permute-start | bytes 2359304 | tf_op jit(solution)/shard_map/ppermute | solution.py:326
  59.6 20.5 %copy-start.5 = (f32[768]{0:T(1024)S(1)}, f32[768]{0:T(1024)}, u32[]{:S(2)}) copy-start(f32[768]{0:T(1024)} %param.14) | copy-start | bytes 9220
  59.6 18.4 %collective-permute-start.1 = (bf16[96,2048]{1,0:T(8,128)(2,1)S(1)}, bf16[96,2048]{1,0:T(8,128)(2,1)S(1)}, u32[]{:S(2)}, u32[]{:S(2)}) collective-permute-start(bf16[96,2048]{1,0:T(8,128)(2,1)S(1)} %get-tuple-element.12), channel_id=1, source_target_pairs={{0,8},{4,12},{8,0},{12,4},{1,9},{5,13},{9,1},{13,5},{2,10},{6,14},... | collective-permute-start | bytes 1179656 | tf_op jit(solution)/shard_map/ppermute | solution.py:327
  78.0 2.1 %copy-start.2 = (bf16[96,2048]{1,0:T(8,128)(2,1)}, bf16[96,2048]{1,0:T(8,128)(2,1)S(1)}, u32[]{:S(2)}) copy-start(bf16[96,2048]{1,0:T(8,128)(2,1)S(1)} %collective-permute-done.1.far_ref) | copy-start | bytes 1179652
  78.0 2.1 %copy-start.1 = (bf16[192,2048]{1,0:T(8,128)(2,1)}, bf16[192,2048]{1,0:T(8,128)(2,1)S(1)}, u32[]{:S(2)}) copy-start(bf16[192,2048]{1,0:T(8,128)(2,1)S(1)} %collective-permute-done.near_ref) | copy-start | bytes 2359300
  78.2 4.9 %collective-permute-start.2 = (bf16[288,2048]{1,0:T(8,128)(2,1)S(1)}, bf16[288,2048]{1,0:T(8,128)(2,1)}, u32[]{:S(2)}, u32[]{:S(2)}) collective-permute-start(bf16[288,2048]{1,0:T(8,128)(2,1)S(1)} %pad_maximum_fusion), channel_id=1, source_target_pairs={{0,1},{1,0},{2,3},{3,2},{4,5},{5,4},{6,7},{7,6},{8,9},{9,8},{10,11... | collective-permute-start | bytes 3538952 | tf_op jit(solution)/shard_map/ppermute | solution.py:332
  89.4 33.5 %all-to-all-start.2 = ((bf16[4,128,768]{2,1,0:T(8,128)(2,1)}), bf16[4,128,768]{2,1,0:T(8,128)(2,1)S(1)}, u32[]{:S(2)}, u32[]{:S(2)}) async-start(bf16[4,128,768]{2,1,0:T(8,128)(2,1)} %shard_map.100), calls=%async_computation.2 | async-start | bytes 1572864 | tf_op jit(solution)/shard_map/all_to_all | solution.py:279
  93.7 23.5 %collective-permute-start.3 = (bf16[192,2048]{1,0:T(8,128)(2,1)S(1)}, bf16[192,2048]{1,0:T(8,128)(2,1)S(1)}, u32[]{:S(2)}, u32[]{:S(2)}) collective-permute-start(bf16[192,2048]{1,0:T(8,128)(2,1)S(1)} %get-tuple-element.13), channel_id=1, source_target_pairs={{0,4},{1,13},{2,6},{3,15},{4,8},{5,1},{6,10},{7,3},{8,12},{9,5},{1... | collective-permute-start | bytes 2359304 | tf_op jit(solution)/shard_map/ppermute | solution.py:328
  95.6 24.4 %copy-start.6 = (f32[768]{0:T(1024)S(1)}, f32[768]{0:T(1024)}, u32[]{:S(2)}) copy-start(f32[768]{0:T(1024)} %param.17) | copy-start | bytes 9220
  95.6 19.6 %collective-permute-start.4 = (bf16[96,2048]{1,0:T(8,128)(2,1)S(1)}, bf16[96,2048]{1,0:T(8,128)(2,1)S(1)}, u32[]{:S(2)}, u32[]{:S(2)}) collective-permute-start(bf16[96,2048]{1,0:T(8,128)(2,1)S(1)} %get-tuple-element.14), channel_id=1, source_target_pairs={{0,8},{4,12},{8,0},{12,4},{1,9},{5,13},{9,1},{13,5},{2,10},{6,14},... | collective-permute-start | bytes 1179656 | tf_op jit(solution)/shard_map/ppermute | solution.py:329
  115.1 2.1 %copy-start.4 = (bf16[96,2048]{1,0:T(8,128)(2,1)}, bf16[96,2048]{1,0:T(8,128)(2,1)S(1)}, u32[]{:S(2)}) copy-start(bf16[96,2048]{1,0:T(8,128)(2,1)S(1)} %collective-permute-done.4.far_ref) | copy-start | bytes 1179652
  117.2 0.9 copy-start.3
  118.0 4.9 %collective-permute-start.5 = (bf16[288,2048]{1,0:T(8,128)(2,1)S(1)}, bf16[288,2048]{1,0:T(8,128)(2,1)}, u32[]{:S(2)}, u32[]{:S(2)}) collective-permute-start(bf16[288,2048]{1,0:T(8,128)(2,1)S(1)} %pad_maximum_fusion.1), channel_id=1, source_target_pairs={{0,1},{1,0},{2,3},{3,2},{4,5},{5,4},{6,7},{7,6},{8,9},{9,8},{10,11... | collective-permute-start | bytes 3538952 | tf_op jit(solution)/shard_map/ppermute | solution.py:333

commit v4 on v3

v4 whole, which is shorter than its diff:
```python
import jax
import jax.numpy as jnp
from jax import lax
from jax.experimental import pallas as pl
from jax.experimental.pallas import tpu as pltpu
from jax.sharding import PartitionSpec as P


HEAD_DIM = 64
EPSILON = 1e-06
PAIR = 2 * HEAD_DIM


def project(all_ref, gain_ref, waits, weight_ref, normed_ref, kv_ref):
    chunks, tokens, width = all_ref.shape
    inner = kv_ref.shape[1] // 2
    gain = gain_ref[...].reshape(1, width)
    for chunk in range(chunks):
        values = all_ref[chunk].astype(jnp.float32)
        factor = lax.rsqrt(jnp.mean(values * values, axis=-1, keepdims=True) + EPSILON)
        normed_ref[chunk * tokens : (chunk + 1) * tokens, :] = (values * factor * gain).astype(
            jnp.bfloat16
        )
    for part in range(2):
        waits[1 + part]()
        for chunk in range(chunks):
            rows = slice(chunk * tokens, (chunk + 1) * tokens)
            kv_ref[rows, part * inner : (part + 1) * inner] = jnp.dot(
                normed_ref[rows, :],
                weight_ref[:, (1 + part) * inner : (2 + part) * inner],
                preferred_element_type=jnp.float32,
            ).astype(jnp.bfloat16)
    waits[0]()


def attend(own, all_ref, weight_ref, out_ref, contract, normed_ref, kv_ref):
    _, tokens, _ = all_ref.shape
    inner = kv_ref.shape[1] // 2
    start = own * tokens
    if not isinstance(own, int):
        start = pl.multiple_of(start, tokens)
    queries = jnp.dot(
        normed_ref[pl.ds(start, tokens), :], weight_ref[:, :inner], preferred_element_type=jnp.float32
    ).astype(jnp.bfloat16) * jnp.bfloat16(HEAD_DIM ** (-0.5))
    first = lax.broadcasted_iota(jnp.int32, (tokens, PAIR), 1) < HEAD_DIM
    attended = []
    for pair in range(inner // PAIR):
        columns = slice(pair * PAIR, (pair + 1) * PAIR)
        query = queries[:, columns]
        keys = kv_ref[:, columns]
        values = kv_ref[:, inner + pair * PAIR : inner + (pair + 1) * PAIR]
        halves = []
        for mask in (first, jnp.logical_not(first)):
            scores = lax.dot_general(
                jnp.where(mask, query, jnp.zeros_like(query)),
                keys,
                (((1,), (1,)), ((), ())),
                preferred_element_type=jnp.float32,
            )
            weights = jnp.exp(scores - jnp.max(scores, axis=-1, keepdims=True))
            total = jnp.sum(weights, axis=-1, keepdims=True)
            mixed = jnp.dot(
                weights.astype(jnp.bfloat16), values, preferred_element_type=jnp.float32
            )
            halves.append(mixed / total)
        attended.append(jnp.where(first, halves[0], halves[1]).astype(jnp.bfloat16))
    update = lax.dot_general(
        jnp.concatenate(attended, axis=1), out_ref[...], contract, preferred_element_type=jnp.float32
    )
    return (all_ref[own].astype(jnp.float32) + update).astype(jnp.bfloat16)


def started(copies):
    for copy in copies:
        copy.start()

    def wait():
        for copy in copies:
            copy.wait()

    return wait


def packing(qkv, out, near, far, whole, sems, core):
    columns = qkv.shape[1]
    rows = far.shape[0]
    half = pl.ds(pl.multiple_of(core * rows, rows), rows)
    load = started(
        [
            pltpu.make_async_copy(qkv, whole.at[:, :columns], sems.at[0]),
            pltpu.make_async_copy(out, whole.at[:, columns:], sems.at[1]),
        ]
    )

    def store():
        load()
        return started(
            [
                pltpu.make_async_copy(whole, near, sems.at[2]),
                pltpu.make_async_copy(whole.at[half, :], far, sems.at[3]),
            ]
        )

    return store


def pack_body(qkv_ref, out_ref, near_ref, far_ref, whole_ref, sems):
    core = lax.rem(lax.axis_index("batch"), 2)
    packing(qkv_ref, out_ref, near_ref, far_ref, whole_ref, sems, core)()()


def pack_layer(qkv, out):
    rows, columns = qkv.shape[0], qkv.shape[1] + out.shape[1]
    hbm = pl.BlockSpec(memory_space=pltpu.HBM)
    return pl.pallas_call(
        pack_body,
        out_shape=(
            jax.ShapeDtypeStruct((rows, columns), jnp.bfloat16),
            jax.ShapeDtypeStruct((rows // 2, columns), jnp.bfloat16),
        ),
        in_specs=[hbm, hbm],
        out_specs=(hbm, hbm),
        scratch_shapes=[pltpu.VMEM((rows, columns), jnp.bfloat16), pltpu.SemaphoreType.DMA((4,))],
        compiler_params=pltpu.CompilerParams(vmem_limit_bytes=4 << 20),
        name="pack",
    )(*kept(qkv, out))


def frame_body(
    all_ref,
    gain_ref,
    qkv_ref,
    out_ref,
    row_qkv_ref,
    row_out_ref,
    result_ref,
    near_ref,
    far_ref,
    weight_ref,
    mix_ref,
    normed_ref,
    kv_ref,
    whole_ref,
    sems,
    pack_sems,
):
    inner = kv_ref.shape[1] // 2
    band = lax.axis_index("band")
    core = lax.rem(lax.axis_index("batch"), 2)
    waits = {}
    for order, part in enumerate((1, 2, 0)):
        columns = slice(part * inner, (part + 1) * inner)
        waits[part] = started(
            [pltpu.make_async_copy(qkv_ref.at[:, columns], weight_ref.at[:, columns], sems.at[order])]
        )
    mix = started([pltpu.make_async_copy(out_ref, mix_ref, sems.at[3])])
    store = packing(row_qkv_ref, row_out_ref, near_ref, far_ref, whole_ref, pack_sems, core)
    project(all_ref, gain_ref, waits, weight_ref, normed_ref, kv_ref)
    mix()
    stored = store()
    result_ref[...] = attend(
        band, all_ref, weight_ref, mix_ref, (((1,), (0,)), ((), ())), normed_ref, kv_ref
    )
    stored()


def kept(*arrays):
    return [pltpu.with_memory_space_constraint(array, pltpu.HBM) for array in arrays]


def frame_layer(everything, gain, qkv, out, row_qkv, row_out):
    chunks, tokens, width = everything.shape
    inner = out.shape[0]
    count = chunks * tokens
    rows = row_qkv.shape[0]
    vmem = pl.BlockSpec(memory_space=pltpu.VMEM)
    hbm = pl.BlockSpec(memory_space=pltpu.HBM)
    return pl.pallas_call(
        frame_body,
        out_shape=(
            jax.ShapeDtypeStruct((tokens, width), jnp.bfloat16),
            jax.ShapeDtypeStruct((rows, 4 * inner), jnp.bfloat16),
            jax.ShapeDtypeStruct((rows // 2, 4 * inner), jnp.bfloat16),
        ),
        in_specs=[vmem, vmem] + [hbm] * 4,
        out_specs=(vmem, hbm, hbm),
        scratch_shapes=[
            pltpu.VMEM((width, 3 * inner), jnp.bfloat16),
            pltpu.VMEM((inner, width), jnp.bfloat16),
            pltpu.VMEM((count, width), jnp.bfloat16),
            pltpu.VMEM((count, 2 * inner), jnp.bfloat16),
            pltpu.VMEM((rows, 4 * inner), jnp.bfloat16),
            pltpu.SemaphoreType.DMA((4,)),
            pltpu.SemaphoreType.DMA((4,)),
        ],
        compiler_params=pltpu.CompilerParams(vmem_limit_bytes=20 << 20),
        cost_estimate=estimate(chunks, tokens, width, inner),
        name="frame",
    )(everything, gain, *kept(qkv, out, row_qkv, row_out))


def estimate(chunks, tokens, width, inner):
    count = chunks * tokens
    return pl.CostEstimate(
        flops=4 * count * width * inner + 4 * tokens * width * inner + 4 * tokens * count * inner,
        bytes_accessed=2 * (count * width + 4 * width * inner),
        transcendentals=tokens * count * inner // HEAD_DIM,
    )


def assembled(parts, weight_ref, sems, band, bands, core):
    qkv_ref, out_ref, near_ref, far_ref, other_ref = parts
    inner = out_ref.shape[1]
    rows = far_ref.shape[0]

    def place(index, half, count):
        return pl.ds(pl.multiple_of((2 * lax.rem(index, bands) + half) * rows, rows), count)

    down, up = band + bands - 1, band + 1
    target = (
        place(band, 0, 2 * rows),
        place(down + 2 * core, 0, 2 * rows),
        place(band + 2, core, rows),
        place(up + 2 * core, 0, 2 * rows),
        place(band + 2, 1 - core, rows),
    )
    waits = {}
    for order, part in enumerate((1, 2, 0, 3)):
        columns = slice(part * inner, (part + 1) * inner)
        sources = (
            out_ref if part == 3 else qkv_ref.at[:, columns],
            near_ref.at[:, columns],
            far_ref.at[:, columns],
            other_ref.at[: 2 * rows, columns],
            other_ref.at[2 * rows :, columns],
        )
        waits[part] = started(
            [
                pltpu.make_async_copy(source, weight_ref.at[goal, columns], sems.at[order, index])
                for index, (source, goal) in enumerate(zip(sources, target))
            ]
        )
    return waits


def rows_body(all_ref, gain1_ref, gain2_ref, *refs):
    parts1, parts2 = refs[:5], refs[5:10]
    result_ref, weight1_ref, weight2_ref, normed_ref, kv_ref, stream_ref, sems = refs[10:]
    chunks = all_ref.shape[0]
    inner = kv_ref.shape[1] // 2
    bands = lax.axis_size("band")
    band = lax.axis_index("band")
    core = lax.rem(lax.axis_index("batch"), 2)
    view = lax.axis_index("view")
    deep = lax.axis_size("view") // 2
    left = lax.rem(view, 2)
    own = jnp.where(view < deep, left, chunks - 1 - left)
    contract = (((1,), (1,)), ((), ()))
    waits1 = assembled(parts1, weight1_ref, sems.at[0], band, bands, core)
    waits2 = assembled(parts2, weight2_ref, sems.at[1], band, bands, core)
    project(all_ref, gain1_ref, waits1, weight1_ref, normed_ref, kv_ref)
    waits1[3]()

    @pl.loop(0, chunks)
    def _(chunk):
        stream_ref[chunk] = attend(
            chunk, all_ref, weight1_ref, weight1_ref.at[:, 3 * inner :], contract, normed_ref, kv_ref
        )

    project(stream_ref, gain2_ref, waits2, weight2_ref, normed_ref, kv_ref)
    waits2[3]()
    result_ref[...] = attend(
        own, stream_ref, weight2_ref, weight2_ref.at[:, 3 * inner :], contract, normed_ref, kv_ref
    )


def rows_layer(everything, gain1, gain2, weights1, weights2):
    chunks, tokens, width = everything.shape
    inner = weights1[1].shape[1]
    count = chunks * tokens
    vmem = pl.BlockSpec(memory_space=pltpu.VMEM)
    return pl.pallas_call(
        rows_body,
        out_shape=jax.ShapeDtypeStruct((tokens, width), jnp.bfloat16),
        in_specs=[vmem] * 3 + [pl.BlockSpec(memory_space=pltpu.HBM)] * 10,
        out_specs=vmem,
        scratch_shapes=[
            pltpu.VMEM((width, 4 * inner), jnp.bfloat16),
            pltpu.VMEM((width, 4 * inner), jnp.bfloat16),
            pltpu.VMEM((count, width), jnp.bfloat16),
            pltpu.VMEM((count, 2 * inner), jnp.bfloat16),
            pltpu.VMEM((chunks, tokens, width), jnp.bfloat16),
            pltpu.SemaphoreType.DMA((2, 4, 5)),
        ],
        compiler_params=pltpu.CompilerParams(vmem_limit_bytes=24 << 20),
        cost_estimate=estimate(chunks, tokens, width, inner),
        name="rows",
    )(everything, gain1, gain2, *kept(*weights1, *weights2))


def exchanged(stream, rows, groups):
    tokens, width = stream.shape
    return lax.all_to_all(
        stream.reshape(rows, tokens // rows, width),
        "view",
        split_axis=0,
        concat_axis=0,
        tiled=True,
        axis_index_groups=groups,
    ).reshape(tokens, width)


def shared(copies, groups):
    return lax.all_to_all(
        copies, "view", split_axis=0, concat_axis=0, tiled=True, axis_index_groups=groups
    )


def layers(
    images,
    frame_gain,
    frame_qkv,
    frame_out,
    row1_gain,
    row1_qkv,
    row1_out,
    row2_gain,
    row2_qkv,
    row2_out,
):
    _, row_count, col_count, width = images.shape
    tokens = row_count * col_count
    views = lax.axis_size("view")
    bands = lax.axis_size("band")
    batches = lax.axis_size("batch")
    share = views // row_count
    near = 2
    deep = views // near
    side = share // near
    spread = [
        [y * deep + h * side + l for h in range(row_count)] for y in range(near) for l in range(side)
    ]
    ring = [
        [h * side + l for l in range(side)] + [deep + h * side + l for l in reversed(range(side))]
        for h in range(row_count)
    ]
    siblings = [(i, i ^ 1) for i in range(batches)]
    turn = [
        (b * batches + c, ((b + 1 - 2 * (c % 2)) % bands) * batches + c)
        for b in range(bands)
        for c in range(batches)
    ]
    across = [(b, (b + 2) % bands) for b in range(bands)]

    shards = (row1_qkv, row1_out.T, row2_qkv, row2_out.T)
    near1, far1 = pack_layer(*shards[:2])
    everything = lax.all_gather(images.reshape(tokens, width), "band", axis=0, tiled=False)
    everything, near1, far1 = lax.optimization_barrier((everything, near1, far1))
    near1 = lax.ppermute(near1, ("band", "batch"), turn)
    far1 = lax.ppermute(far1, "band", across)
    stream, near2, far2 = frame_layer(everything, frame_gain, frame_qkv, frame_out, *shards[2:])
    stream = exchanged(stream, row_count, spread)
    near2 = lax.ppermute(near2, ("band", "batch"), turn)
    far2 = lax.ppermute(far2, "band", across)
    other1 = lax.ppermute(jnp.concatenate([near1, far1]), "batch", siblings)
    gain1 = row1_gain.reshape(1, width)
    gain2 = row2_gain.reshape(1, width)
    everything = shared(jnp.broadcast_to(stream[None], (share, tokens, width)), ring)
    other2 = lax.ppermute(jnp.concatenate([near2, far2]), "batch", siblings)
    stream = rows_layer(
        everything,
        gain1,
        gain2,
        (*shards[:2], near1, far1, other1),
        (*shards[2:], near2, far2, other2),
    )
    stream = exchanged(stream, row_count, spread)
    return stream.reshape(images.shape)


def solution(mesh):
    in_specs = (
        P(("batch", "view"), "band", None, None),
        P(),
        P(),
        P(),
        P(),
        P("band", None),
        P(None, "band"),
        P(),
        P("band", None),
        P(None, "band"),
    )
    out_specs = P(("batch", "view"), "band", None, None)
    return jax.shard_map(layers, mesh=mesh, in_specs=in_specs, out_specs=out_specs, check_vma=False)
```

time: 152 us -> 135 us (0.89)
  blocking collectives: 65.9 us -> 36.5 us
  starting transfers between devices: 26.2 us -> 37.9 us
  waiting for transfers between devices: 38.3 us -> 29.9 us
  Pallas kernels: 17.6 us -> 25.2 us
    all_to_all x2 -> x1, blocking collectives: 52.1 us -> 22.5 us  [exchanged(): lax.all_to_all(stream.reshape(rows, tokens // rows, width), 'view', split...]
    all_to_all x0 -> x1, starting transfers between devices: none -> 14.2 us  [exchanged(): lax.all_to_all(stream.reshape(rows, tokens // rows, width), 'view', split...]
    ppermute x1, waiting for transfers between devices: 13.8 us -> 0.89 us  [layers(): far1 = lax.ppermute(far1, 'band', across)]
    all_to_all x0 -> x1, waiting for transfers between devices: none -> 11.8 us  [exchanged(): lax.all_to_all(stream.reshape(rows, tokens // rows, width), 'view', split...]
    pallas_call x2, Pallas kernels: 11.9 us -> 19.2 us  [the longest x1 17.8 us: rows_layer(): pl.pallas_call(rows_body, out_shape=jax.ShapeDtypeStruct((tokens, width),...]
    all_to_all x2 -> x1, starting transfers between devices: 10.7 us -> 6.46 us  [shared(): lax.all_to_all(copies, 'view', split_axis=0, concat_axis=0, tiled=True, a...]
    ppermute x1, waiting for transfers between devices: 2.92 us -> 0.01 us  [layers(): other2 = lax.ppermute(jnp.concatenate([near2, far2]), 'batch', siblings)]
    ppermute x1, waiting for transfers between devices: 2.02 us -> 0.01 us  [layers(): near2 = lax.ppermute(near2, ('band', 'batch'), turn)]
  transfers between devices with their start and end apart: 8 -> 8, of which waited for: 5 -> 4; matrix products, arithmetic and copies ran while one was open for 0% -> 2% of each run, Pallas kernels for 0% -> 0%
where the time goes in v4:
time: 135 us
  starting transfers between devices  37.9 us (28%)
  blocking collectives  36.5 us (27%)
  waiting for transfers between devices  29.9 us (22%)
  Pallas kernels  25.2 us (19%)
  local copies, waits for them, and re-layouts  3.56 us (3%)
  other arithmetic  1.44 us (1%)
    all_to_all x1, blocking collectives, exchanged(): lax.all_to_all(stream.reshape(rows, tokens // rows, width), 'view', split...  22.5 us
    pallas_call x1, Pallas kernels, rows_layer(): pl.pallas_call(rows_body, out_shape=jax.ShapeDtypeStruct((tokens, width),...  17.8 us
    ppermute x1, waiting for transfers between devices, layers(): far2 = lax.ppermute(far2, 'band', across)  15.2 us
    all_to_all x1, starting transfers between devices, exchanged(): lax.all_to_all(stream.reshape(rows, tokens // rows, width), 'view', split...  14.2 us
    all_gather x1, blocking collectives, layers(): lax.all_gather(images.reshape(tokens, width), 'band', axis=0, tiled=False)  14 us
    all_to_all x1, waiting for transfers between devices, exchanged(): lax.all_to_all(stream.reshape(rows, tokens // rows, width), 'view', split...  11.8 us
    all_to_all x1, starting transfers between devices, shared(): lax.all_to_all(copies, 'view', split_axis=0, concat_axis=0, tiled=True, a...  6.46 us
    pallas_call x1, Pallas kernels, frame_layer(): pl.pallas_call(frame_body, out_shape=(jax.ShapeDtypeStruct((tokens, width...  6.01 us
  transfers between devices with their start and end apart: 8, of which 4 were waited for; matrix products, arithmetic and copies ran while one was open for 2% of the time, Pallas kernels for 0%

profile of v4, /device:TPU:56, one launch (start us, length us, event | category | flops | bytes accessed | tf_op | source)
XLA Modules:
  0.0 134.6 jit_solution(13472633216254087977)
XLA Ops:
  0.0 0.0 copy-start
  0.0 14.0 %all_gather.3.all_ref = bf16[4,128,768]{2,1,0:T(8,128)(2,1)S(1)} all-gather(bf16[1,128,768]{2,1,0:T(8,128)(2,1)} %bitcast.14), channel_id=1, replica_groups=mesh['view'=32,'band'=4,'batch'=4] {'band'}, dimensions={0}, use_global_device_ids=true | all-gather | bytes 983040 | tf_op jit(solution)/shard_map/all_gather | solution.py:357
  14.0 1.4 %pack.1 = (bf16[192,2048]{1,0:T(8,128)(2,1)S(1)}, bf16[96,2048]{1,0:T(8,128)(2,1)S(1)}) custom-call(bf16[192,1536]{1,0:T(8,128)(2,1)} %refs_0_.1, bf16[192,512]{1,0:T(8,128)(2,1)} %bitcast.10), custom_call_target="tpu_custom_call" | custom-call | tf_op jit(solution)/shard_map/pack/pallas_call | solution.py:115
  15.4 0.0 copy-done
  15.4 6.0 %frame.1 = (bf16[128,768]{1,0:T(8,128)(2,1)}, bf16[192,2048]{1,0:T(8,128)(2,1)S(1)}, bf16[96,2048]{1,0:T(8,128)(2,1)S(1)}) custom-call(bf16[4,128,768]{2,1,0:T(8,128)(2,1)S(1)} %all_gather.3.all_ref, f32[768]{0:T(1024)S(1)} %copy-done, bf16[768,1536]{1,0:T(8,128)(2,1)} %qkv_ref.3, bf16[512,768]{1,0:T(8,128)(2,1)} %out_ref.1, bf16[192,1536]{1,0:T(8,128)(2,1)} %refs_5_.1, ...), custom_call_target="tpu_custom_call" | custom-call | flops 1140850688 | bytes 3932160 | tf_op jit(solution)/shard_map/frame/pallas_call | solution.py:178
  21.4 14.2 %all-to-all-start = ((bf16[8,16,768]{2,1,0:T(8,128)(2,1)}), bf16[8,16,768]{2,1,0:T(8,128)(2,1)S(1)}, u32[]{:S(2)}, u32[]{:S(2)}) async-start(bf16[8,16,768]{2,1,0:T(8,128)(2,1)} %bitcast.3), calls=%async_computation | async-start | bytes 393216 | tf_op jit(solution)/shard_map/all_to_all | solution.py:303
  35.6 3.8 %collective-permute-start.3 = (bf16[192,2048]{1,0:T(8,128)(2,1)S(1)}, bf16[192,2048]{1,0:T(8,128)(2,1)}, u32[]{:S(2)}, u32[]{:S(2)}) collective-permute-start(bf16[192,2048]{1,0:T(8,128)(2,1)S(1)} %get-tuple-element.19), channel_id=1, source_target_pairs={{0,4},{1,13},{2,6},{3,15},{4,8},{5,1},{6,10},{7,3},{8,12},{9,5},{1... | collective-permute-start | bytes 2359304 | tf_op jit(solution)/shard_map/ppermute | solution.py:363
  39.5 11.8 %all-to-all-done = bf16[8,16,768]{2,1,0:T(8,128)(2,1)S(1)} async-done(((bf16[8,16,768]{2,1,0:T(8,128)(2,1)}), bf16[8,16,768]{2,1,0:T(8,128)(2,1)S(1)}, u32[]{:S(2)}, u32[]{:S(2)}) %all-to-all-start) | async-done | bytes 196640 | tf_op jit(solution)/shard_map/all_to_all | solution.py:303
  51.3 0.9 broadcast_in_dim.8
  52.2 6.5 %all-to-all-start.1 = ((bf16[4,128,768]{2,1,0:T(8,128)(2,1)}), bf16[4,128,768]{2,1,0:T(8,128)(2,1)S(1)}, u32[]{:S(2)}, u32[]{:S(2)}) async-start(bf16[4,128,768]{2,1,0:T(8,128)(2,1)} %broadcast_in_dim.8), calls=%async_computation.1 | async-start | bytes 1572864 | tf_op jit(solution)/shard_map/all_to_all | solution.py:314
  58.7 2.2 %collective-permute-start = (bf16[192,2048]{1,0:T(8,128)(2,1)S(1)}, bf16[192,2048]{1,0:T(8,128)(2,1)S(1)}, u32[]{:S(2)}, u32[]{:S(2)}) collective-permute-start(bf16[192,2048]{1,0:T(8,128)(2,1)S(1)} %get-tuple-element.17), channel_id=1, source_target_pairs={{0,4},{1,13},{2,6},{3,15},{4,8},{5,1},{6,10},{7,3},{8,12},{9,5},{1... | collective-permute-start | bytes 2359304 | tf_op jit(solution)/shard_map/ppermute | solution.py:359
  60.9 4.6 %collective-permute-start.4 = (bf16[96,2048]{1,0:T(8,128)(2,1)S(1)}, bf16[96,2048]{1,0:T(8,128)(2,1)S(1)}, u32[]{:S(2)}, u32[]{:S(2)}) collective-permute-start(bf16[96,2048]{1,0:T(8,128)(2,1)S(1)} %get-tuple-element.20), channel_id=1, source_target_pairs={{0,8},{4,12},{8,0},{12,4},{1,9},{5,13},{9,1},{13,5},{2,10},{6,14},... | collective-permute-start | bytes 1179656 | tf_op jit(solution)/shard_map/ppermute | solution.py:364
  65.5 2.8 %collective-permute-start.1 = (bf16[96,2048]{1,0:T(8,128)(2,1)S(1)}, bf16[96,2048]{1,0:T(8,128)(2,1)S(1)}, u32[]{:S(2)}, u32[]{:S(2)}) collective-permute-start(bf16[96,2048]{1,0:T(8,128)(2,1)S(1)} %get-tuple-element.18), channel_id=1, source_target_pairs={{0,8},{4,12},{8,0},{12,4},{1,9},{5,13},{9,1},{13,5},{2,10},{6,14},... | collective-permute-start | bytes 1179656 | tf_op jit(solution)/shard_map/ppermute | solution.py:360
  68.3 15.2 %collective-permute-done.4.refs_8_ = bf16[96,2048]{1,0:T(8,128)(2,1)S(1)} collective-permute-done((bf16[96,2048]{1,0:T(8,128)(2,1)S(1)}, bf16[96,2048]{1,0:T(8,128)(2,1)S(1)}, u32[]{:S(2)}, u32[]{:S(2)}) %collective-permute-start.4) | collective-permute-done | bytes 393248 | tf_op jit(solution)/shard_map/ppermute | solution.py:364
  83.5 0.0 copy-start.2
  83.5 0.0 collective-permute-done.3.refs_7_
  83.5 1.4 %pad_maximum_fusion.1 = bf16[288,2048]{1,0:T(8,128)(2,1)S(1)} fusion(bf16[96,2048]{1,0:T(8,128)(2,1)S(1)} %collective-permute-done.4.refs_8_, bf16[192,2048]{1,0:T(8,128)(2,1)} %collective-permute-done.3.refs_7_), kind=kLoop, calls=%fused_computation.1 | loop fusion | flops 2359296 | bytes 2359296 | tf_op jit(solution)/shard_map/concatenate | solution.py:369
  84.9 0.0 copy-start.5
  84.9 0.0 copy-start.6
  84.9 1.9 %collective-permute-start.5 = (bf16[288,2048]{1,0:T(8,128)(2,1)S(1)}, bf16[288,2048]{1,0:T(8,128)(2,1)S(1)}, u32[]{:S(2)}, u32[]{:S(2)}) collective-permute-start(bf16[288,2048]{1,0:T(8,128)(2,1)S(1)} %pad_maximum_fusion.1), channel_id=1, source_target_pairs={{0,1},{1,0},{2,3},{3,2},{4,5},{5,4},{6,7},{7,6},{8,9},{9,8},{10,11... | collective-permute-start | bytes 3538952 | tf_op jit(solution)/shard_map/ppermute | solution.py:369
  86.8 0.9 collective-permute-done.1.refs_3_
  87.7 0.0 copy-start.3
  87.7 0.0 collective-permute-done.refs_2_
  87.7 0.0 copy-start.1
  87.7 0.1 pad_maximum_fusion
  87.8 0.0 copy-done.2
  87.8 0.6 copy-done.3
  88.5 0.3 copy-done.1
  88.7 1.9 %collective-permute-start.2 = (bf16[288,2048]{1,0:T(8,128)(2,1)S(1)}, bf16[288,2048]{1,0:T(8,128)(2,1)}, u32[]{:S(2)}, u32[]{:S(2)}) collective-permute-start(bf16[288,2048]{1,0:T(8,128)(2,1)S(1)} %pad_maximum_fusion), channel_id=1, source_target_pairs={{0,1},{1,0},{2,3},{3,2},{4,5},{5,4},{6,7},{7,6},{8,9},{9,8},{10,11... | collective-permute-start | bytes 3538952 | tf_op jit(solution)/shard_map/ppermute | solution.py:365
  90.7 0.0 copy-done.5
  90.7 0.0 copy-done.6
  90.7 0.0 collective-permute-done.5.refs_9_
  90.7 0.0 copy-start.4
  90.7 1.0 copy-done.4
  91.7 1.9 %collective-permute-done.2.refs_4_ = bf16[288,2048]{1,0:T(8,128)(2,1)} collective-permute-done((bf16[288,2048]{1,0:T(8,128)(2,1)S(1)}, bf16[288,2048]{1,0:T(8,128)(2,1)}, u32[]{:S(2)}, u32[]{:S(2)}) %collective-permute-start.2) | collective-permute-done | bytes 1179680 | tf_op jit(solution)/shard_map/ppermute | solution.py:365
  93.6 0.0 all-to-all-done.1.all_ref
  93.6 17.8 %rows.1 = bf16[128,768]{1,0:T(8,128)(2,1)S(1)} custom-call(bf16[4,128,768]{2,1,0:T(8,128)(2,1)S(1)} %all-to-all-done.1.all_ref, f32[1,768]{1,0:T(1,128)S(1)} %reshape.14.gain1_ref, f32[1,768]{1,0:T(1,128)S(1)} %reshape.15.gain2_ref, bf16[192,1536]{1,0:T(8,128)(2,1)} %refs_0_.1, bf16[192,512]{1,0:T(8,128)(2,1)} %bitcast.11, bf16[192,2048]{1,0:T(8,128)(2,1)} %copy-done.1, ...), custom_call_target="tpu_custom_call" | custom-call | flops 1140850688 | bytes 3932160 | tf_op jit(solution)/shard_map/rows/pallas_call | solution.py:282
  111.4 22.5 %all_to_all.15 = bf16[8,16,768]{2,1,0:T(8,128)(2,1)S(1)} all-to-all(bf16[8,16,768]{2,1,0:T(8,128)(2,1)S(1)} %bitcast.7), channel_id=1, replica_groups={{0,32,64,96,128,160,192,224},{16,48,80,112,144,176,208,240},{256,288,32..., dimensions={0} | all-to-all | bytes 393216 | tf_op jit(solution)/shard_map/all_to_all | solution.py:303
  133.9 0.7 copy.12
  (2 shorter events, 0.0 us)
Async XLA Ops:
  0.0 15.4 %copy-start = (f32[768]{0:T(1024)S(1)}, f32[768]{0:T(1024)}, u32[]{:S(2)}) copy-start(f32[768]{0:T(1024)} %gain_ref.1) | copy-start | bytes 9220
  21.4 29.9 %all-to-all-start = ((bf16[8,16,768]{2,1,0:T(8,128)(2,1)}), bf16[8,16,768]{2,1,0:T(8,128)(2,1)S(1)}, u32[]{:S(2)}, u32[]{:S(2)}) async-start(bf16[8,16,768]{2,1,0:T(8,128)(2,1)} %bitcast.3), calls=%async_computation | async-start | bytes 393216 | tf_op jit(solution)/shard_map/all_to_all | solution.py:303
  35.6 47.9 %collective-permute-start.3 = (bf16[192,2048]{1,0:T(8,128)(2,1)S(1)}, bf16[192,2048]{1,0:T(8,128)(2,1)}, u32[]{:S(2)}, u32[]{:S(2)}) collective-permute-start(bf16[192,2048]{1,0:T(8,128)(2,1)S(1)} %get-tuple-element.19), channel_id=1, source_target_pairs={{0,4},{1,13},{2,6},{3,15},{4,8},{5,1},{6,10},{7,3},{8,12},{9,5},{1... | collective-permute-start | bytes 2359304 | tf_op jit(solution)/shard_map/ppermute | solution.py:363
  52.2 41.4 %all-to-all-start.1 = ((bf16[4,128,768]{2,1,0:T(8,128)(2,1)}), bf16[4,128,768]{2,1,0:T(8,128)(2,1)S(1)}, u32[]{:S(2)}, u32[]{:S(2)}) async-start(bf16[4,128,768]{2,1,0:T(8,128)(2,1)} %broadcast_in_dim.8), calls=%async_computation.1 | async-start | bytes 1572864 | tf_op jit(solution)/shard_map/all_to_all | solution.py:314
  58.7 29.1 %collective-permute-start = (bf16[192,2048]{1,0:T(8,128)(2,1)S(1)}, bf16[192,2048]{1,0:T(8,128)(2,1)S(1)}, u32[]{:S(2)}, u32[]{:S(2)}) collective-permute-start(bf16[192,2048]{1,0:T(8,128)(2,1)S(1)} %get-tuple-element.17), channel_id=1, source_target_pairs={{0,4},{1,13},{2,6},{3,15},{4,8},{5,1},{6,10},{7,3},{8,12},{9,5},{1... | collective-permute-start | bytes 2359304 | tf_op jit(solution)/shard_map/ppermute | solution.py:359
  60.9 22.6 %collective-permute-start.4 = (bf16[96,2048]{1,0:T(8,128)(2,1)S(1)}, bf16[96,2048]{1,0:T(8,128)(2,1)S(1)}, u32[]{:S(2)}, u32[]{:S(2)}) collective-permute-start(bf16[96,2048]{1,0:T(8,128)(2,1)S(1)} %get-tuple-element.20), channel_id=1, source_target_pairs={{0,8},{4,12},{8,0},{12,4},{1,9},{5,13},{9,1},{13,5},{2,10},{6,14},... | collective-permute-start | bytes 1179656 | tf_op jit(solution)/shard_map/ppermute | solution.py:364
  65.5 22.2 %collective-permute-start.1 = (bf16[96,2048]{1,0:T(8,128)(2,1)S(1)}, bf16[96,2048]{1,0:T(8,128)(2,1)S(1)}, u32[]{:S(2)}, u32[]{:S(2)}) collective-permute-start(bf16[96,2048]{1,0:T(8,128)(2,1)S(1)} %get-tuple-element.18), channel_id=1, source_target_pairs={{0,8},{4,12},{8,0},{12,4},{1,9},{5,13},{9,1},{13,5},{2,10},{6,14},... | collective-permute-start | bytes 1179656 | tf_op jit(solution)/shard_map/ppermute | solution.py:360
  83.5 4.3 %copy-start.2 = (bf16[96,2048]{1,0:T(8,128)(2,1)}, bf16[96,2048]{1,0:T(8,128)(2,1)S(1)}, u32[]{:S(2)}) copy-start(bf16[96,2048]{1,0:T(8,128)(2,1)S(1)} %collective-permute-done.4.refs_8_) | copy-start | bytes 1179652
  84.9 5.8 %copy-start.5 = (f32[768]{0:T(1024)S(1)}, f32[768]{0:T(1024)}, u32[]{:S(2)}) copy-start(f32[768]{0:T(1024)} %param.14) | copy-start | bytes 9220
  84.9 5.8 %copy-start.6 = (f32[768]{0:T(1024)S(1)}, f32[768]{0:T(1024)}, u32[]{:S(2)}) copy-start(f32[768]{0:T(1024)} %param.17) | copy-start | bytes 9220
  84.9 5.8 %collective-permute-start.5 = (bf16[288,2048]{1,0:T(8,128)(2,1)S(1)}, bf16[288,2048]{1,0:T(8,128)(2,1)S(1)}, u32[]{:S(2)}, u32[]{:S(2)}) collective-permute-start(bf16[288,2048]{1,0:T(8,128)(2,1)S(1)} %pad_maximum_fusion.1), channel_id=1, source_target_pairs={{0,1},{1,0},{2,3},{3,2},{4,5},{5,4},{6,7},{7,6},{8,9},{9,8},{10,11... | collective-permute-start | bytes 3538952 | tf_op jit(solution)/shard_map/ppermute | solution.py:369
  87.7 0.8 copy-start.3
  87.7 1.0 copy-start.1
  88.7 4.9 %collective-permute-start.2 = (bf16[288,2048]{1,0:T(8,128)(2,1)S(1)}, bf16[288,2048]{1,0:T(8,128)(2,1)}, u32[]{:S(2)}, u32[]{:S(2)}) collective-permute-start(bf16[288,2048]{1,0:T(8,128)(2,1)S(1)} %pad_maximum_fusion), channel_id=1, source_target_pairs={{0,1},{1,0},{2,3},{3,2},{4,5},{5,4},{6,7},{7,6},{8,9},{9,8},{10,11... | collective-permute-start | bytes 3538952 | tf_op jit(solution)/shard_map/ppermute | solution.py:365
  90.7 1.0 copy-start.4

commit v5 on v4

--- a/solution.py
+++ b/solution.py
@@ -1,3 +1,5 @@
+import math
+
 import jax
 import jax.numpy as jnp
 from jax import lax
@@ -9,6 +11,9 @@
 HEAD_DIM = 64
 EPSILON = 1e-06
 PAIR = 2 * HEAD_DIM
+SCALE = HEAD_DIM ** (-0.5) * math.log2(math.e)
+NORM_ROWS = 32
+SOFTMAX_ROWS = 32
 
 
 def project(all_ref, gain_ref, waits, weight_ref, normed_ref, kv_ref):
@@ -16,58 +21,72 @@
     inner = kv_ref.shape[1] // 2
     gain = gain_ref[...].reshape(1, width)
     for chunk in range(chunks):
-        values = all_ref[chunk].astype(jnp.float32)
-        factor = lax.rsqrt(jnp.mean(values * values, axis=-1, keepdims=True) + EPSILON)
-        normed_ref[chunk * tokens : (chunk + 1) * tokens, :] = (values * factor * gain).astype(
-            jnp.bfloat16
-        )
+        for start in range(0, tokens, NORM_ROWS):
+            values = all_ref[chunk, start : start + NORM_ROWS].astype(jnp.float32)
+            factor = lax.rsqrt(jnp.mean(values * values, axis=-1, keepdims=True) + EPSILON)
+            at = chunk * tokens + start
+            normed_ref[at : at + NORM_ROWS, :] = (values * factor * gain).astype(jnp.bfloat16)
     for part in range(2):
         waits[1 + part]()
-        for chunk in range(chunks):
-            rows = slice(chunk * tokens, (chunk + 1) * tokens)
-            kv_ref[rows, part * inner : (part + 1) * inner] = jnp.dot(
-                normed_ref[rows, :],
-                weight_ref[:, (1 + part) * inner : (2 + part) * inner],
-                preferred_element_type=jnp.float32,
-            ).astype(jnp.bfloat16)
+        kv_ref[:, part * inner : (part + 1) * inner] = jnp.dot(
+            normed_ref[...],
+            weight_ref[:, (1 + part) * inner : (2 + part) * inner],
+            preferred_element_type=jnp.float32,
+        ).astype(jnp.bfloat16)
     waits[0]()
 
 
-def attend(own, all_ref, weight_ref, out_ref, contract, normed_ref, kv_ref):
-    _, tokens, _ = all_ref.shape
+def mixed(normed, weight_ref, kv_ref, query_ref, score_ref, rounded_ref, inverse_ref, attended_ref):
+    count = normed.shape[0]
     inner = kv_ref.shape[1] // 2
-    start = own * tokens
-    if not isinstance(own, int):
-        start = pl.multiple_of(start, tokens)
-    queries = jnp.dot(
-        normed_ref[pl.ds(start, tokens), :], weight_ref[:, :inner], preferred_element_type=jnp.float32
-    ).astype(jnp.bfloat16) * jnp.bfloat16(HEAD_DIM ** (-0.5))
-    first = lax.broadcasted_iota(jnp.int32, (tokens, PAIR), 1) < HEAD_DIM
-    attended = []
+    queries = (
+        jnp.dot(normed, weight_ref[:, :inner], preferred_element_type=jnp.float32) * SCALE
+    ).astype(jnp.bfloat16)
+    first = lax.broadcasted_iota(jnp.int32, (count, PAIR), 1) < HEAD_DIM
+    zeros = jnp.zeros((count, PAIR), jnp.bfloat16)
     for pair in range(inner // PAIR):
+        query = queries[:, pair * PAIR : (pair + 1) * PAIR]
+        query_ref[pair, :count] = jnp.where(first, query, zeros)
+        query_ref[pair, count:] = jnp.where(first, zeros, query)
+    for pair in range(inner // PAIR):
+        slot = pair % 2
         columns = slice(pair * PAIR, (pair + 1) * PAIR)
-        query = queries[:, columns]
-        keys = kv_ref[:, columns]
-        values = kv_ref[:, inner + pair * PAIR : inner + (pair + 1) * PAIR]
-        halves = []
-        for mask in (first, jnp.logical_not(first)):
-            scores = lax.dot_general(
-                jnp.where(mask, query, jnp.zeros_like(query)),
-                keys,
-                (((1,), (1,)), ((), ())),
-                preferred_element_type=jnp.float32,
-            )
-            weights = jnp.exp(scores - jnp.max(scores, axis=-1, keepdims=True))
+        score_ref[slot] = lax.dot_general(
+            query_ref[pair],
+            kv_ref[:, columns],
+            (((1,), (1,)), ((), ())),
+            preferred_element_type=jnp.float32,
+        )
+        for start in range(0, 2 * count, SOFTMAX_ROWS):
+            rows = slice(start, start + SOFTMAX_ROWS)
+            scores = score_ref[slot, rows]
+            weights = jnp.exp2(scores - jnp.max(scores, axis=-1, keepdims=True))
             total = jnp.sum(weights, axis=-1, keepdims=True)
-            mixed = jnp.dot(
-                weights.astype(jnp.bfloat16), values, preferred_element_type=jnp.float32
-            )
-            halves.append(mixed / total)
-        attended.append(jnp.where(first, halves[0], halves[1]).astype(jnp.bfloat16))
-    update = lax.dot_general(
-        jnp.concatenate(attended, axis=1), out_ref[...], contract, preferred_element_type=jnp.float32
-    )
-    return (all_ref[own].astype(jnp.float32) + update).astype(jnp.bfloat16)
+            rounded_ref[slot, rows] = weights.astype(jnp.bfloat16)
+            inverse_ref[slot, rows] = jnp.broadcast_to(1.0 / total, (SOFTMAX_ROWS, PAIR))
+        result = inverse_ref[slot] * jnp.dot(
+            rounded_ref[slot],
+            kv_ref[:, inner + pair * PAIR : inner + (pair + 1) * PAIR],
+            preferred_element_type=jnp.float32,
+        )
+        attended_ref[:, columns] = jnp.where(first, result[:count], result[count:]).astype(
+            jnp.bfloat16
+        )
+
+
+def mixing_scratch(count, keys, inner):
+    pairs = inner // PAIR
+    return [
+        pltpu.VMEM((pairs, 2 * count, PAIR), jnp.bfloat16),
+        pltpu.VMEM((2, 2 * count, keys), jnp.float32),
+        pltpu.VMEM((2, 2 * count, keys), jnp.bfloat16),
+        pltpu.VMEM((2, 2 * count, PAIR), jnp.float32),
+        pltpu.VMEM((count, inner), jnp.bfloat16),
+    ]
+
+
+def chunk_of(normed_ref, own, tokens):
+    return normed_ref[pl.ds(pl.multiple_of(own * tokens, tokens), tokens), :]
 
 
 def started(copies):
@@ -143,6 +162,7 @@
     whole_ref,
     sems,
     pack_sems,
+    *mixing,
 ):
     inner = kv_ref.shape[1] // 2
     band = lax.axis_index("band")
@@ -158,9 +178,10 @@
     project(all_ref, gain_ref, waits, weight_ref, normed_ref, kv_ref)
     mix()
     stored = store()
-    result_ref[...] = attend(
-        band, all_ref, weight_ref, mix_ref, (((1,), (0,)), ((), ())), normed_ref, kv_ref
-    )
+    _, tokens, _ = all_ref.shape
+    mixed(chunk_of(normed_ref, band, tokens), weight_ref, kv_ref, *mixing)
+    update = jnp.dot(mixing[-1][...], mix_ref[...], preferred_element_type=jnp.float32)
+    result_ref[...] = (all_ref[band].astype(jnp.float32) + update).astype(jnp.bfloat16)
     stored()
 
 
@@ -192,7 +213,8 @@
             pltpu.VMEM((rows, 4 * inner), jnp.bfloat16),
             pltpu.SemaphoreType.DMA((4,)),
             pltpu.SemaphoreType.DMA((4,)),
-        ],
+        ]
+        + mixing_scratch(tokens, count, inner),
         compiler_params=pltpu.CompilerParams(vmem_limit_bytes=20 << 20),
         cost_estimate=estimate(chunks, tokens, width, inner),
         name="frame",
@@ -245,7 +267,8 @@
 
 def rows_body(all_ref, gain1_ref, gain2_ref, *refs):
     parts1, parts2 = refs[:5], refs[5:10]
-    result_ref, weight1_ref, weight2_ref, normed_ref, kv_ref, stream_ref, sems = refs[10:]
+    result_ref, weight1_ref, weight2_ref, normed_ref, kv_ref, stream_ref, sems = refs[10:17]
+    mixing1, mixing2 = refs[17:22], refs[22:]
     chunks = all_ref.shape[0]
     inner = kv_ref.shape[1] // 2
     bands = lax.axis_size("band")
@@ -259,19 +282,23 @@
     waits1 = assembled(parts1, weight1_ref, sems.at[0], band, bands, core)
     waits2 = assembled(parts2, weight2_ref, sems.at[1], band, bands, core)
     project(all_ref, gain1_ref, waits1, weight1_ref, normed_ref, kv_ref)
+    _, tokens, _ = all_ref.shape
+    mixed(normed_ref[...], weight1_ref, kv_ref, *mixing1)
     waits1[3]()
-
-    @pl.loop(0, chunks)
-    def _(chunk):
-        stream_ref[chunk] = attend(
-            chunk, all_ref, weight1_ref, weight1_ref.at[:, 3 * inner :], contract, normed_ref, kv_ref
-        )
-
+    update = lax.dot_general(
+        mixing1[-1][...], weight1_ref[:, 3 * inner :], contract, preferred_element_type=jnp.float32
+    )
+    for chunk in range(chunks):
+        stream_ref[chunk] = (
+            all_ref[chunk].astype(jnp.float32) + update[chunk * tokens : (chunk + 1) * tokens]
+        ).astype(jnp.bfloat16)
     project(stream_ref, gain2_ref, waits2, weight2_ref, normed_ref, kv_ref)
+    mixed(chunk_of(normed_ref, own, tokens), weight2_ref, kv_ref, *mixing2)
     waits2[3]()
-    result_ref[...] = attend(
-        own, stream_ref, weight2_ref, weight2_ref.at[:, 3 * inner :], contract, normed_ref, kv_ref
-    )
+    update = lax.dot_general(
+        mixing2[-1][...], weight2_ref[:, 3 * inner :], contract, preferred_element_type=jnp.float32
+    )
+    result_ref[...] = (stream_ref[own].astype(jnp.float32) + update).astype(jnp.bfloat16)
 
 
 def rows_layer(everything, gain1, gain2, weights1, weights2):
@@ -291,8 +318,10 @@
             pltpu.VMEM((count, 2 * inner), jnp.bfloat16),
             pltpu.VMEM((chunks, tokens, width), jnp.bfloat16),
             pltpu.SemaphoreType.DMA((2, 4, 5)),
-        ],
-        compiler_params=pltpu.CompilerParams(vmem_limit_bytes=24 << 20),
+        ]
+        + mixing_scratch(count, count, inner)
+        + mixing_scratch(tokens, count, inner),
+        compiler_params=pltpu.CompilerParams(vmem_limit_bytes=32 << 20),
         cost_estimate=estimate(chunks, tokens, width, inner),
         name="rows",
     )(everything, gain1, gain2, *kept(*weights1, *weights2))

time: 135 us -> 127 us (0.941)
  Pallas kernels: 25.2 us -> 16.9 us
    pallas_call x1, Pallas kernels: 17.8 us -> 10.3 us  [rows_layer(): pl.pallas_call(rows_body, out_shape=jax.ShapeDtypeStruct((tokens, width),...]
where the time goes in v5:
time: 127 us; the launch traced here: 126 us
  starting transfers between devices  37.9 us (30%)
  blocking collectives  36.5 us (29%)
  waiting for transfers between devices  29.8 us (23%)
  Pallas kernels  16.9 us (13%)
  local copies, waits for them, and re-layouts  3.56 us (3%)
  other arithmetic  1.44 us (1%)
    all_to_all x1, blocking collectives, exchanged(): lax.all_to_all(stream.reshape(rows, tokens // rows, width), 'view', split...  22.5 us
    ppermute x1, waiting for transfers between devices, layers(): far2 = lax.ppermute(far2, 'band', across)  15.3 us
    all_to_all x1, starting transfers between devices, exchanged(): lax.all_to_all(stream.reshape(rows, tokens // rows, width), 'view', split...  14.2 us
    all_gather x1, blocking collectives, layers(): lax.all_gather(images.reshape(tokens, width), 'band', axis=0, tiled=False)  14 us
    all_to_all x1, waiting for transfers between devices, exchanged(): lax.all_to_all(stream.reshape(rows, tokens // rows, width), 'view', split...  11.8 us
    pallas_call x1, Pallas kernels, rows_layer(): pl.pallas_call(rows_body, out_shape=jax.ShapeDtypeStruct((tokens, width),...  10.3 us
    all_to_all x1, starting transfers between devices, shared(): lax.all_to_all(copies, 'view', split_axis=0, concat_axis=0, tiled=True, a...  6.46 us
    pallas_call x1, Pallas kernels, frame_layer(): pl.pallas_call(frame_body, out_shape=(jax.ShapeDtypeStruct((tokens, width...  5.17 us
  transfers between devices with their start and end apart: 8, of which 4 were waited for; matrix products, arithmetic and copies ran while one was open for 2% of the time, Pallas kernels for 0%

profile of v5, /device:TPU:56, one launch (start us, length us, event | category | flops | bytes accessed | tf_op | source)
XLA Modules:
  0.0 126.3 jit_solution(6107926692205640054)
XLA Ops:
  0.0 0.0 copy-start
  0.0 14.0 %all_gather.3.all_ref = bf16[4,128,768]{2,1,0:T(8,128)(2,1)S(1)} all-gather(bf16[1,128,768]{2,1,0:T(8,128)(2,1)} %bitcast.14), channel_id=1, replica_groups=mesh['view'=32,'band'=4,'batch'=4] {'band'}, dimensions={0}, use_global_device_ids=true | all-gather | bytes 983040 | tf_op jit(solution)/shard_map/all_gather | solution.py:386
  14.0 1.4 %pack.1 = (bf16[192,2048]{1,0:T(8,128)(2,1)S(1)}, bf16[96,2048]{1,0:T(8,128)(2,1)S(1)}) custom-call(bf16[192,1536]{1,0:T(8,128)(2,1)} %refs_0_.1, bf16[192,512]{1,0:T(8,128)(2,1)} %bitcast.10), custom_call_target="tpu_custom_call" | custom-call | tf_op jit(solution)/shard_map/pack/pallas_call | solution.py:134
  15.4 0.0 copy-done
  15.4 5.2 %frame.1 = (bf16[128,768]{1,0:T(8,128)(2,1)}, bf16[192,2048]{1,0:T(8,128)(2,1)S(1)}, bf16[96,2048]{1,0:T(8,128)(2,1)S(1)}) custom-call(bf16[4,128,768]{2,1,0:T(8,128)(2,1)S(1)} %all_gather.3.all_ref, f32[768]{0:T(1024)S(1)} %copy-done, bf16[768,1536]{1,0:T(8,128)(2,1)} %qkv_ref.3, bf16[512,768]{1,0:T(8,128)(2,1)} %out_ref.1, bf16[192,1536]{1,0:T(8,128)(2,1)} %refs_5_.1, ...), custom_call_target="tpu_custom_call" | custom-call | flops 1140850688 | bytes 3932160 | tf_op jit(solution)/shard_map/frame/pallas_call | solution.py:199
  20.6 14.2 %all-to-all-start = ((bf16[8,16,768]{2,1,0:T(8,128)(2,1)}), bf16[8,16,768]{2,1,0:T(8,128)(2,1)S(1)}, u32[]{:S(2)}, u32[]{:S(2)}) async-start(bf16[8,16,768]{2,1,0:T(8,128)(2,1)} %bitcast.3), calls=%async_computation | async-start | bytes 393216 | tf_op jit(solution)/shard_map/all_to_all | solution.py:332
  34.8 3.8 %collective-permute-start.3 = (bf16[192,2048]{1,0:T(8,128)(2,1)S(1)}, bf16[192,2048]{1,0:T(8,128)(2,1)}, u32[]{:S(2)}, u32[]{:S(2)}) collective-permute-start(bf16[192,2048]{1,0:T(8,128)(2,1)S(1)} %get-tuple-element.19), channel_id=1, source_target_pairs={{0,4},{1,13},{2,6},{3,15},{4,8},{5,1},{6,10},{7,3},{8,12},{9,5},{1... | collective-permute-start | bytes 2359304 | tf_op jit(solution)/shard_map/ppermute | solution.py:392
  38.6 11.8 %all-to-all-done = bf16[8,16,768]{2,1,0:T(8,128)(2,1)S(1)} async-done(((bf16[8,16,768]{2,1,0:T(8,128)(2,1)}), bf16[8,16,768]{2,1,0:T(8,128)(2,1)S(1)}, u32[]{:S(2)}, u32[]{:S(2)}) %all-to-all-start) | async-done | bytes 196640 | tf_op jit(solution)/shard_map/all_to_all | solution.py:332
  50.4 0.9 broadcast_in_dim.8
  51.4 6.5 %all-to-all-start.1 = ((bf16[4,128,768]{2,1,0:T(8,128)(2,1)}), bf16[4,128,768]{2,1,0:T(8,128)(2,1)S(1)}, u32[]{:S(2)}, u32[]{:S(2)}) async-start(bf16[4,128,768]{2,1,0:T(8,128)(2,1)} %broadcast_in_dim.8), calls=%async_computation.1 | async-start | bytes 1572864 | tf_op jit(solution)/shard_map/all_to_all | solution.py:343
  57.8 2.2 %collective-permute-start = (bf16[192,2048]{1,0:T(8,128)(2,1)S(1)}, bf16[192,2048]{1,0:T(8,128)(2,1)S(1)}, u32[]{:S(2)}, u32[]{:S(2)}) collective-permute-start(bf16[192,2048]{1,0:T(8,128)(2,1)S(1)} %get-tuple-element.17), channel_id=1, source_target_pairs={{0,4},{1,13},{2,6},{3,15},{4,8},{5,1},{6,10},{7,3},{8,12},{9,5},{1... | collective-permute-start | bytes 2359304 | tf_op jit(solution)/shard_map/ppermute | solution.py:388
  60.0 4.6 %collective-permute-start.4 = (bf16[96,2048]{1,0:T(8,128)(2,1)S(1)}, bf16[96,2048]{1,0:T(8,128)(2,1)S(1)}, u32[]{:S(2)}, u32[]{:S(2)}) collective-permute-start(bf16[96,2048]{1,0:T(8,128)(2,1)S(1)} %get-tuple-element.20), channel_id=1, source_target_pairs={{0,8},{4,12},{8,0},{12,4},{1,9},{5,13},{9,1},{13,5},{2,10},{6,14},... | collective-permute-start | bytes 1179656 | tf_op jit(solution)/shard_map/ppermute | solution.py:393
  64.6 2.8 %collective-permute-start.1 = (bf16[96,2048]{1,0:T(8,128)(2,1)S(1)}, bf16[96,2048]{1,0:T(8,128)(2,1)S(1)}, u32[]{:S(2)}, u32[]{:S(2)}) collective-permute-start(bf16[96,2048]{1,0:T(8,128)(2,1)S(1)} %get-tuple-element.18), channel_id=1, source_target_pairs={{0,8},{4,12},{8,0},{12,4},{1,9},{5,13},{9,1},{13,5},{2,10},{6,14},... | collective-permute-start | bytes 1179656 | tf_op jit(solution)/shard_map/ppermute | solution.py:389
  67.4 15.3 %collective-permute-done.4.refs_8_ = bf16[96,2048]{1,0:T(8,128)(2,1)S(1)} collective-permute-done((bf16[96,2048]{1,0:T(8,128)(2,1)S(1)}, bf16[96,2048]{1,0:T(8,128)(2,1)S(1)}, u32[]{:S(2)}, u32[]{:S(2)}) %collective-permute-start.4) | collective-permute-done | bytes 393248 | tf_op jit(solution)/shard_map/ppermute | solution.py:393
  82.7 0.0 copy-start.2
  82.7 0.0 collective-permute-done.3.refs_7_
  82.7 1.4 %pad_maximum_fusion.1 = bf16[288,2048]{1,0:T(8,128)(2,1)S(1)} fusion(bf16[96,2048]{1,0:T(8,128)(2,1)S(1)} %collective-permute-done.4.refs_8_, bf16[192,2048]{1,0:T(8,128)(2,1)} %collective-permute-done.3.refs_7_), kind=kLoop, calls=%fused_computation.1 | loop fusion | flops 2359296 | bytes 2359296 | tf_op jit(solution)/shard_map/concatenate | solution.py:398
  84.0 0.0 copy-start.5
  84.0 0.0 copy-start.6
  84.1 1.9 %collective-permute-start.5 = (bf16[288,2048]{1,0:T(8,128)(2,1)S(1)}, bf16[288,2048]{1,0:T(8,128)(2,1)S(1)}, u32[]{:S(2)}, u32[]{:S(2)}) collective-permute-start(bf16[288,2048]{1,0:T(8,128)(2,1)S(1)} %pad_maximum_fusion.1), channel_id=1, source_target_pairs={{0,1},{1,0},{2,3},{3,2},{4,5},{5,4},{6,7},{7,6},{8,9},{9,8},{10,11... | collective-permute-start | bytes 3538952 | tf_op jit(solution)/shard_map/ppermute | solution.py:398
  86.0 0.9 collective-permute-done.1.refs_3_
  86.9 0.0 copy-start.3
  86.9 0.0 collective-permute-done.refs_2_
  86.9 0.0 copy-start.1
  86.9 0.1 pad_maximum_fusion
  87.0 0.0 copy-done.2
  87.0 0.6 copy-done.3
  87.6 0.3 copy-done.1
  87.9 1.9 %collective-permute-start.2 = (bf16[288,2048]{1,0:T(8,128)(2,1)S(1)}, bf16[288,2048]{1,0:T(8,128)(2,1)}, u32[]{:S(2)}, u32[]{:S(2)}) collective-permute-start(bf16[288,2048]{1,0:T(8,128)(2,1)S(1)} %pad_maximum_fusion), channel_id=1, source_target_pairs={{0,1},{1,0},{2,3},{3,2},{4,5},{5,4},{6,7},{7,6},{8,9},{9,8},{10,11... | collective-permute-start | bytes 3538952 | tf_op jit(solution)/shard_map/ppermute | solution.py:394
  89.8 0.0 copy-done.5
  89.8 0.0 copy-done.6
  89.9 0.0 collective-permute-done.5.refs_9_
  89.9 0.0 copy-start.4
  89.9 1.0 copy-done.4
  90.9 1.9 %collective-permute-done.2.refs_4_ = bf16[288,2048]{1,0:T(8,128)(2,1)} collective-permute-done((bf16[288,2048]{1,0:T(8,128)(2,1)S(1)}, bf16[288,2048]{1,0:T(8,128)(2,1)}, u32[]{:S(2)}, u32[]{:S(2)}) %collective-permute-start.2) | collective-permute-done | bytes 1179680 | tf_op jit(solution)/shard_map/ppermute | solution.py:394
  92.8 0.0 all-to-all-done.1.all_ref
  92.8 10.3 %rows.1 = bf16[128,768]{1,0:T(8,128)(2,1)S(1)} custom-call(bf16[4,128,768]{2,1,0:T(8,128)(2,1)S(1)} %all-to-all-done.1.all_ref, f32[1,768]{1,0:T(1,128)S(1)} %reshape.14.gain1_ref, f32[1,768]{1,0:T(1,128)S(1)} %reshape.15.gain2_ref, bf16[192,1536]{1,0:T(8,128)(2,1)} %refs_0_.1, bf16[192,512]{1,0:T(8,128)(2,1)} %bitcast.11, bf16[192,2048]{1,0:T(8,128)(2,1)} %copy-done.1, ...), custom_call_target="tpu_custom_call" | custom-call | flops 1140850688 | bytes 3932160 | tf_op jit(solution)/shard_map/rows/pallas_call | solution.py:309
  103.1 22.5 %all_to_all.15 = bf16[8,16,768]{2,1,0:T(8,128)(2,1)S(1)} all-to-all(bf16[8,16,768]{2,1,0:T(8,128)(2,1)S(1)} %bitcast.7), channel_id=1, replica_groups={{0,32,64,96,128,160,192,224},{16,48,80,112,144,176,208,240},{256,288,32..., dimensions={0} | all-to-all | bytes 393216 | tf_op jit(solution)/shard_map/all_to_all | solution.py:332
  125.6 0.7 copy.12
  (2 shorter events, 0.0 us)
Async XLA Ops:
  0.0 15.4 %copy-start = (f32[768]{0:T(1024)S(1)}, f32[768]{0:T(1024)}, u32[]{:S(2)}) copy-start(f32[768]{0:T(1024)} %gain_ref.1) | copy-start | bytes 9220
  20.6 29.8 %all-to-all-start = ((bf16[8,16,768]{2,1,0:T(8,128)(2,1)}), bf16[8,16,768]{2,1,0:T(8,128)(2,1)S(1)}, u32[]{:S(2)}, u32[]{:S(2)}) async-start(bf16[8,16,768]{2,1,0:T(8,128)(2,1)} %bitcast.3), calls=%async_computation | async-start | bytes 393216 | tf_op jit(solution)/shard_map/all_to_all | solution.py:332
  34.8 47.9 %collective-permute-start.3 = (bf16[192,2048]{1,0:T(8,128)(2,1)S(1)}, bf16[192,2048]{1,0:T(8,128)(2,1)}, u32[]{:S(2)}, u32[]{:S(2)}) collective-permute-start(bf16[192,2048]{1,0:T(8,128)(2,1)S(1)} %get-tuple-element.19), channel_id=1, source_target_pairs={{0,4},{1,13},{2,6},{3,15},{4,8},{5,1},{6,10},{7,3},{8,12},{9,5},{1... | collective-permute-start | bytes 2359304 | tf_op jit(solution)/shard_map/ppermute | solution.py:392
  51.4 41.4 %all-to-all-start.1 = ((bf16[4,128,768]{2,1,0:T(8,128)(2,1)}), bf16[4,128,768]{2,1,0:T(8,128)(2,1)S(1)}, u32[]{:S(2)}, u32[]{:S(2)}) async-start(bf16[4,128,768]{2,1,0:T(8,128)(2,1)} %broadcast_in_dim.8), calls=%async_computation.1 | async-start | bytes 1572864 | tf_op jit(solution)/shard_map/all_to_all | solution.py:343
  57.8 29.1 %collective-permute-start = (bf16[192,2048]{1,0:T(8,128)(2,1)S(1)}, bf16[192,2048]{1,0:T(8,128)(2,1)S(1)}, u32[]{:S(2)}, u32[]{:S(2)}) collective-permute-start(bf16[192,2048]{1,0:T(8,128)(2,1)S(1)} %get-tuple-element.17), channel_id=1, source_target_pairs={{0,4},{1,13},{2,6},{3,15},{4,8},{5,1},{6,10},{7,3},{8,12},{9,5},{1... | collective-permute-start | bytes 2359304 | tf_op jit(solution)/shard_map/ppermute | solution.py:388
  60.0 22.6 %collective-permute-start.4 = (bf16[96,2048]{1,0:T(8,128)(2,1)S(1)}, bf16[96,2048]{1,0:T(8,128)(2,1)S(1)}, u32[]{:S(2)}, u32[]{:S(2)}) collective-permute-start(bf16[96,2048]{1,0:T(8,128)(2,1)S(1)} %get-tuple-element.20), channel_id=1, source_target_pairs={{0,8},{4,12},{8,0},{12,4},{1,9},{5,13},{9,1},{13,5},{2,10},{6,14},... | collective-permute-start | bytes 1179656 | tf_op jit(solution)/shard_map/ppermute | solution.py:393
  64.6 22.2 %collective-permute-start.1 = (bf16[96,2048]{1,0:T(8,128)(2,1)S(1)}, bf16[96,2048]{1,0:T(8,128)(2,1)S(1)}, u32[]{:S(2)}, u32[]{:S(2)}) collective-permute-start(bf16[96,2048]{1,0:T(8,128)(2,1)S(1)} %get-tuple-element.18), channel_id=1, source_target_pairs={{0,8},{4,12},{8,0},{12,4},{1,9},{5,13},{9,1},{13,5},{2,10},{6,14},... | collective-permute-start | bytes 1179656 | tf_op jit(solution)/shard_map/ppermute | solution.py:389
  82.7 4.3 %copy-start.2 = (bf16[96,2048]{1,0:T(8,128)(2,1)}, bf16[96,2048]{1,0:T(8,128)(2,1)S(1)}, u32[]{:S(2)}) copy-start(bf16[96,2048]{1,0:T(8,128)(2,1)S(1)} %collective-permute-done.4.refs_8_) | copy-start | bytes 1179652
  84.0 5.8 %copy-start.5 = (f32[768]{0:T(1024)S(1)}, f32[768]{0:T(1024)}, u32[]{:S(2)}) copy-start(f32[768]{0:T(1024)} %param.14) | copy-start | bytes 9220
  84.0 5.8 %copy-start.6 = (f32[768]{0:T(1024)S(1)}, f32[768]{0:T(1024)}, u32[]{:S(2)}) copy-start(f32[768]{0:T(1024)} %param.17) | copy-start | bytes 9220
  84.1 5.8 %collective-permute-start.5 = (bf16[288,2048]{1,0:T(8,128)(2,1)S(1)}, bf16[288,2048]{1,0:T(8,128)(2,1)S(1)}, u32[]{:S(2)}, u32[]{:S(2)}) collective-permute-start(bf16[288,2048]{1,0:T(8,128)(2,1)S(1)} %pad_maximum_fusion.1), channel_id=1, source_target_pairs={{0,1},{1,0},{2,3},{3,2},{4,5},{5,4},{6,7},{7,6},{8,9},{9,8},{10,11... | collective-permute-start | bytes 3538952 | tf_op jit(solution)/shard_map/ppermute | solution.py:398
  86.9 0.8 copy-start.3
  86.9 1.0 copy-start.1
  87.9 4.9 %collective-permute-start.2 = (bf16[288,2048]{1,0:T(8,128)(2,1)S(1)}, bf16[288,2048]{1,0:T(8,128)(2,1)}, u32[]{:S(2)}, u32[]{:S(2)}) collective-permute-start(bf16[288,2048]{1,0:T(8,128)(2,1)S(1)} %pad_maximum_fusion), channel_id=1, source_target_pairs={{0,1},{1,0},{2,3},{3,2},{4,5},{5,4},{6,7},{7,6},{8,9},{9,8},{10,11... | collective-permute-start | bytes 3538952 | tf_op jit(solution)/shard_map/ppermute | solution.py:394
  89.9 1.0 copy-start.4

commit v6 on v5

--- a/solution.py
+++ b/solution.py
@@ -100,49 +100,32 @@
     return wait
 
 
-def packing(qkv, out, near, far, whole, sems, core):
-    columns = qkv.shape[1]
-    rows = far.shape[0]
-    half = pl.ds(pl.multiple_of(core * rows, rows), rows)
-    load = started(
-        [
-            pltpu.make_async_copy(qkv, whole.at[:, :columns], sems.at[0]),
-            pltpu.make_async_copy(out, whole.at[:, columns:], sems.at[1]),
-        ]
-    )
-
-    def store():
-        load()
-        return started(
-            [
-                pltpu.make_async_copy(whole, near, sems.at[2]),
-                pltpu.make_async_copy(whole.at[half, :], far, sems.at[3]),
-            ]
-        )
-
-    return store
-
-
-def pack_body(qkv_ref, out_ref, near_ref, far_ref, whole_ref, sems):
-    core = lax.rem(lax.axis_index("batch"), 2)
-    packing(qkv_ref, out_ref, near_ref, far_ref, whole_ref, sems, core)()()
-
-
-def pack_layer(qkv, out):
-    rows, columns = qkv.shape[0], qkv.shape[1] + out.shape[1]
-    hbm = pl.BlockSpec(memory_space=pltpu.HBM)
+def pack_body(*refs):
+    shards, near_ref, sems = refs[:4], refs[4], refs[5]
+    columns = shards[0].shape[1]
+    copies = []
+    for layer in range(2):
+        qkv, out = shards[2 * layer : 2 * layer + 2]
+        copies.append(
+            pltpu.make_async_copy(qkv, near_ref.at[layer, :, :columns], sems.at[2 * layer])
+        )
+        copies.append(
+            pltpu.make_async_copy(out, near_ref.at[layer, :, columns:], sems.at[2 * layer + 1])
+        )
+    started(copies)()
+
+
+def pack_layer(shards):
+    qkv, out = shards[:2]
     return pl.pallas_call(
         pack_body,
-        out_shape=(
-            jax.ShapeDtypeStruct((rows, columns), jnp.bfloat16),
-            jax.ShapeDtypeStruct((rows // 2, columns), jnp.bfloat16),
-        ),
-        in_specs=[hbm, hbm],
-        out_specs=(hbm, hbm),
-        scratch_shapes=[pltpu.VMEM((rows, columns), jnp.bfloat16), pltpu.SemaphoreType.DMA((4,))],
+        out_shape=jax.ShapeDtypeStruct((2, qkv.shape[0], qkv.shape[1] + out.shape[1]), jnp.bfloat16),
+        in_specs=[pl.BlockSpec(memory_space=pltpu.HBM)] * 4,
+        out_specs=pl.BlockSpec(memory_space=pltpu.VMEM),
+        scratch_shapes=[pltpu.SemaphoreType.DMA((4,))],
         compiler_params=pltpu.CompilerParams(vmem_limit_bytes=4 << 20),
         name="pack",
-    )(*kept(qkv, out))
+    )(*kept(*shards))
 
 
 def frame_body(
@@ -150,23 +133,16 @@
     gain_ref,
     qkv_ref,
     out_ref,
-    row_qkv_ref,
-    row_out_ref,
     result_ref,
-    near_ref,
-    far_ref,
     weight_ref,
     mix_ref,
     normed_ref,
     kv_ref,
-    whole_ref,
     sems,
-    pack_sems,
     *mixing,
 ):
     inner = kv_ref.shape[1] // 2
     band = lax.axis_index("band")
-    core = lax.rem(lax.axis_index("batch"), 2)
     waits = {}
     for order, part in enumerate((1, 2, 0)):
         columns = slice(part * inner, (part + 1) * inner)
@@ -174,51 +150,41 @@
             [pltpu.make_async_copy(qkv_ref.at[:, columns], weight_ref.at[:, columns], sems.at[order])]
         )
     mix = started([pltpu.make_async_copy(out_ref, mix_ref, sems.at[3])])
-    store = packing(row_qkv_ref, row_out_ref, near_ref, far_ref, whole_ref, pack_sems, core)
     project(all_ref, gain_ref, waits, weight_ref, normed_ref, kv_ref)
     mix()
-    stored = store()
     _, tokens, _ = all_ref.shape
     mixed(chunk_of(normed_ref, band, tokens), weight_ref, kv_ref, *mixing)
     update = jnp.dot(mixing[-1][...], mix_ref[...], preferred_element_type=jnp.float32)
     result_ref[...] = (all_ref[band].astype(jnp.float32) + update).astype(jnp.bfloat16)
-    stored()
 
 
 def kept(*arrays):
     return [pltpu.with_memory_space_constraint(array, pltpu.HBM) for array in arrays]
 
 
-def frame_layer(everything, gain, qkv, out, row_qkv, row_out):
+def frame_layer(everything, gain, qkv, out):
     chunks, tokens, width = everything.shape
     inner = out.shape[0]
     count = chunks * tokens
-    rows = row_qkv.shape[0]
     vmem = pl.BlockSpec(memory_space=pltpu.VMEM)
     hbm = pl.BlockSpec(memory_space=pltpu.HBM)
     return pl.pallas_call(
         frame_body,
-        out_shape=(
-            jax.ShapeDtypeStruct((tokens, width), jnp.bfloat16),
-            jax.ShapeDtypeStruct((rows, 4 * inner), jnp.bfloat16),
-            jax.ShapeDtypeStruct((rows // 2, 4 * inner), jnp.bfloat16),
-        ),
-        in_specs=[vmem, vmem] + [hbm] * 4,
-        out_specs=(vmem, hbm, hbm),
+        out_shape=jax.ShapeDtypeStruct((tokens, width), jnp.bfloat16),
+        in_specs=[vmem, vmem, hbm, hbm],
+        out_specs=vmem,
         scratch_shapes=[
             pltpu.VMEM((width, 3 * inner), jnp.bfloat16),
             pltpu.VMEM((inner, width), jnp.bfloat16),
             pltpu.VMEM((count, width), jnp.bfloat16),
             pltpu.VMEM((count, 2 * inner), jnp.bfloat16),
-            pltpu.VMEM((rows, 4 * inner), jnp.bfloat16),
-            pltpu.SemaphoreType.DMA((4,)),
             pltpu.SemaphoreType.DMA((4,)),
         ]
         + mixing_scratch(tokens, count, inner),
         compiler_params=pltpu.CompilerParams(vmem_limit_bytes=20 << 20),
         cost_estimate=estimate(chunks, tokens, width, inner),
         name="frame",
-    )(everything, gain, *kept(qkv, out, row_qkv, row_out))
+    )(everything, gain, *kept(qkv, out))
 
 
 def estimate(chunks, tokens, width, inner):
@@ -231,7 +197,7 @@
 
 
 def assembled(parts, weight_ref, sems, band, bands, core):
-    qkv_ref, out_ref, near_ref, far_ref, other_ref = parts
+    qkv_ref, out_ref, near_ref, far_ref, other_near_ref, other_far_ref = parts
     inner = out_ref.shape[1]
     rows = far_ref.shape[0]
 
@@ -253,8 +219,8 @@
             out_ref if part == 3 else qkv_ref.at[:, columns],
             near_ref.at[:, columns],
             far_ref.at[:, columns],
-            other_ref.at[: 2 * rows, columns],
-            other_ref.at[2 * rows :, columns],
+            other_near_ref.at[:, columns],
+            other_far_ref.at[:, columns],
         )
         waits[part] = started(
             [
@@ -266,9 +232,11 @@
 
 
 def rows_body(all_ref, gain1_ref, gain2_ref, *refs):
-    parts1, parts2 = refs[:5], refs[5:10]
-    result_ref, weight1_ref, weight2_ref, normed_ref, kv_ref, stream_ref, sems = refs[10:17]
-    mixing1, mixing2 = refs[17:22], refs[22:]
+    shards, moved, refs = refs[:4], refs[4:8], refs[8:]
+    parts1 = (*shards[:2], *(ref.at[0] for ref in moved))
+    parts2 = (*shards[2:], *(ref.at[1] for ref in moved))
+    result_ref, weight1_ref, weight2_ref, normed_ref, kv_ref, stream_ref, sems = refs[:7]
+    mixing1, mixing2 = refs[7:12], refs[12:]
     chunks = all_ref.shape[0]
     inner = kv_ref.shape[1] // 2
     bands = lax.axis_size("band")
@@ -301,15 +269,15 @@
     result_ref[...] = (stream_ref[own].astype(jnp.float32) + update).astype(jnp.bfloat16)
 
 
-def rows_layer(everything, gain1, gain2, weights1, weights2):
+def rows_layer(everything, gain1, gain2, weights):
     chunks, tokens, width = everything.shape
-    inner = weights1[1].shape[1]
+    inner = weights[1].shape[1]
     count = chunks * tokens
     vmem = pl.BlockSpec(memory_space=pltpu.VMEM)
     return pl.pallas_call(
         rows_body,
         out_shape=jax.ShapeDtypeStruct((tokens, width), jnp.bfloat16),
-        in_specs=[vmem] * 3 + [pl.BlockSpec(memory_space=pltpu.HBM)] * 10,
+        in_specs=[vmem] * 3 + [pl.BlockSpec(memory_space=pltpu.HBM)] * 8,
         out_specs=vmem,
         scratch_shapes=[
             pltpu.VMEM((width, 4 * inner), jnp.bfloat16),
@@ -324,7 +292,7 @@
         compiler_params=pltpu.CompilerParams(vmem_limit_bytes=32 << 20),
         cost_estimate=estimate(chunks, tokens, width, inner),
         name="rows",
-    )(everything, gain1, gain2, *kept(*weights1, *weights2))
+    )(everything, gain1, gain2, *kept(*weights))
 
 
 def exchanged(stream, rows, groups):
@@ -337,12 +305,6 @@
         tiled=True,
         axis_index_groups=groups,
     ).reshape(tokens, width)
-
-
-def shared(copies, groups):
-    return lax.all_to_all(
-        copies, "view", split_axis=0, concat_axis=0, tiled=True, axis_index_groups=groups
-    )
 
 
 def layers(
@@ -379,29 +341,24 @@
         for b in range(bands)
         for c in range(batches)
     ]
-    across = [(b, (b + 2) % bands) for b in range(bands)]
 
     shards = (row1_qkv, row1_out.T, row2_qkv, row2_out.T)
-    near1, far1 = pack_layer(*shards[:2])
+    core = lax.rem(lax.axis_index("batch"), 2)
     everything = lax.all_gather(images.reshape(tokens, width), "band", axis=0, tiled=False)
-    everything, near1, far1 = lax.optimization_barrier((everything, near1, far1))
-    near1 = lax.ppermute(near1, ("band", "batch"), turn)
-    far1 = lax.ppermute(far1, "band", across)
-    stream, near2, far2 = frame_layer(everything, frame_gain, frame_qkv, frame_out, *shards[2:])
+    everything, near = lax.optimization_barrier((everything, pack_layer(shards)))
+    near = lax.ppermute(near, ("band", "batch"), turn)
+    stream = frame_layer(everything, frame_gain, frame_qkv, frame_out)
     stream = exchanged(stream, row_count, spread)
-    near2 = lax.ppermute(near2, ("band", "batch"), turn)
-    far2 = lax.ppermute(far2, "band", across)
-    other1 = lax.ppermute(jnp.concatenate([near1, far1]), "batch", siblings)
+    half = near.shape[1] // 2
+    far = lax.dynamic_slice_in_dim(near, core * half, half, axis=1)
+    far = lax.ppermute(far, ("band", "batch"), turn)
+    other_near = lax.ppermute(near, "batch", siblings)
     gain1 = row1_gain.reshape(1, width)
     gain2 = row2_gain.reshape(1, width)
-    everything = shared(jnp.broadcast_to(stream[None], (share, tokens, width)), ring)
-    other2 = lax.ppermute(jnp.concatenate([near2, far2]), "batch", siblings)
+    other_far = lax.ppermute(far, "batch", siblings)
+    everything = lax.all_gather(stream, "view", axis=0, tiled=False, axis_index_groups=ring)
     stream = rows_layer(
-        everything,
-        gain1,
-        gain2,
-        (*shards[:2], near1, far1, other1),
-        (*shards[2:], near2, far2, other2),
+        everything, gain1, gain2, (*shards, near, far, other_near, other_far)
     )
     stream = exchanged(stream, row_count, spread)
     return stream.reshape(images.shape)

time: 127 us -> 127 us (level)
  the two profiles are of different devices: /device:TPU:56 before, /device:TPU:16 now
where the time goes in v6:
time: 127 us
  blocking collectives  44.7 us (35%)
  waiting for transfers between devices  36.9 us (29%)
  starting transfers between devices  25.6 us (20%)
  Pallas kernels  16.6 us (13%)
  local copies, waits for them, and re-layouts  2.77 us (2%)
    ppermute x1, waiting for transfers between devices, layers(): near = lax.ppermute(near, ('band', 'batch'), turn)  19.8 us
    all_to_all x1, blocking collectives, exchanged(): lax.all_to_all(stream.reshape(rows, tokens // rows, width), 'view', split...  18.9 us
    all_to_all x1, waiting for transfers between devices, exchanged(): lax.all_to_all(stream.reshape(rows, tokens // rows, width), 'view', split...  17.1 us
    all_to_all x1, starting transfers between devices, exchanged(): lax.all_to_all(stream.reshape(rows, tokens // rows, width), 'view', split...  15.1 us
    all_gather x1, blocking collectives, layers(): lax.all_gather(images.reshape(tokens, width), 'band', axis=0, tiled=False)  13.9 us
    all_gather x1, blocking collectives, layers(): lax.all_gather(stream, 'view', axis=0, tiled=False, axis_index_groups=ring)  11.9 us
    pallas_call x1, Pallas kernels, rows_layer(): pl.pallas_call(rows_body, out_shape=jax.ShapeDtypeStruct((tokens, width),...  10.3 us
    pallas_call x1, Pallas kernels, frame_layer(): pl.pallas_call(frame_body, out_shape=jax.ShapeDtypeStruct((tokens, width)...  4.89 us
  transfers between devices with their start and end apart: 5, of which 2 were waited for; matrix products, arithmetic and copies ran while one was open for 0% of the time, Pallas kernels for 4%

profile of v6, /device:TPU:16, one launch (start us, length us, event | category | flops | bytes accessed | tf_op | source)
XLA Modules:
  0.0 126.7 jit_solution(6039955927150636029)
XLA Ops:
  0.0 13.9 %all_gather.6.all_ref = bf16[4,128,768]{2,1,0:T(8,128)(2,1)S(1)} all-gather(bf16[1,128,768]{2,1,0:T(8,128)(2,1)} %bitcast.14), channel_id=1, replica_groups=mesh['view'=32,'band'=4,'batch'=4] {'band'}, dimensions={0}, use_global_device_ids=true | all-gather | bytes 983040 | tf_op jit(solution)/shard_map/all_gather | solution.py:347
  13.9 1.4 %pack.1 = bf16[2,192,2048]{2,1,0:T(8,128)(2,1)S(1)} custom-call(bf16[192,1536]{1,0:T(8,128)(2,1)} %refs_0_.3, bf16[192,512]{1,0:T(8,128)(2,1)} %bitcast.10, bf16[192,1536]{1,0:T(8,128)(2,1)} %refs_2_.3, bf16[192,512]{1,0:T(8,128)(2,1)} %bitcast.12), custom_call_target="tpu_custom_call" | custom-call | tf_op jit(solution)/shard_map/pack/pallas_call | solution.py:120
  15.2 0.0 copy-start
  15.3 3.8 %collective-permute-start = (bf16[2,192,2048]{2,1,0:T(8,128)(2,1)S(1)}, bf16[2,192,2048]{2,1,0:T(8,128)(2,1)}, u32[]{:S(2)}, u32[]{:S(2)}) collective-permute-start(bf16[2,192,2048]{2,1,0:T(8,128)(2,1)S(1)} %pack.1), channel_id=1, source_target_pairs={{0,4},{1,13},{2,6},{3,15},{4,8},{5,1},{6,10},{7,3},{8,12},{9,5},{1... | collective-permute-start | bytes 4718600 | tf_op jit(solution)/shard_map/ppermute | solution.py:349
  19.1 19.8 %collective-permute-done.refs_4_ = bf16[2,192,2048]{2,1,0:T(8,128)(2,1)} collective-permute-done((bf16[2,192,2048]{2,1,0:T(8,128)(2,1)S(1)}, bf16[2,192,2048]{2,1,0:T(8,128)(2,1)}, u32[]{:S(2)}, u32[]{:S(2)}) %collective-permute-start) | collective-permute-done | bytes 1572896 | tf_op jit(solution)/shard_map/ppermute | solution.py:349
  38.9 1.2 constant_dynamic-slice_fusion
  40.1 0.0 copy-start.3
  40.1 0.0 copy-start.4
  40.1 2.6 %collective-permute-start.1 = (bf16[2,96,2048]{2,1,0:T(8,128)(2,1)S(1)}, bf16[2,96,2048]{2,1,0:T(8,128)(2,1)S(1)}, u32[]{:S(2)}, u32[]{:S(2)}) collective-permute-start(bf16[2,96,2048]{2,1,0:T(8,128)(2,1)S(1)} %constant_dynamic-slice_fusion), channel_id=1, source_target_pairs={{0,4},{1,13},{2,6},{3,15},{4,8},{5,1},{6,10},{7,3},{8,12},{9,5},{1... | collective-permute-start | bytes 2359304 | tf_op jit(solution)/shard_map/ppermute | solution.py:354
  42.7 1.9 %collective-permute-start.2 = (bf16[2,192,2048]{2,1,0:T(8,128)(2,1)}, bf16[2,192,2048]{2,1,0:T(8,128)(2,1)}, u32[]{:S(2)}, u32[]{:S(2)}) collective-permute-start(bf16[2,192,2048]{2,1,0:T(8,128)(2,1)} %collective-permute-done.refs_4_), channel_id=1, source_target_pairs={{0,1},{1,0},{2,3},{3,2},{4,5},{5,4},{6,7},{7,6},{8,9},{9,8},{10,11... | collective-permute-start | bytes 4718600 | tf_op jit(solution)/shard_map/ppermute | solution.py:355
  44.7 0.0 copy-done
  44.7 4.9 %frame.1 = bf16[128,768]{1,0:T(8,128)(2,1)} custom-call(bf16[4,128,768]{2,1,0:T(8,128)(2,1)S(1)} %all_gather.6.all_ref, f32[768]{0:T(1024)S(1)} %copy-done, bf16[768,1536]{1,0:T(8,128)(2,1)} %qkv_ref.1, bf16[512,768]{1,0:T(8,128)(2,1)} %out_ref.1), custom_call_target="tpu_custom_call" | custom-call | flops 1140850688 | bytes 3932160 | tf_op jit(solution)/shard_map/frame/pallas_call | solution.py:171
  49.6 15.1 %all-to-all-start = ((bf16[8,16,768]{2,1,0:T(8,128)(2,1)}), bf16[8,16,768]{2,1,0:T(8,128)(2,1)S(1)}, u32[]{:S(2)}, u32[]{:S(2)}) async-start(bf16[8,16,768]{2,1,0:T(8,128)(2,1)} %bitcast.3), calls=%async_computation | async-start | bytes 393216 | tf_op jit(solution)/shard_map/all_to_all | solution.py:300
  64.7 0.0 collective-permute-done.1.refs_5_
  64.7 0.0 copy-start.1
  64.7 2.1 %collective-permute-start.3 = (bf16[2,96,2048]{2,1,0:T(8,128)(2,1)S(1)}, bf16[2,96,2048]{2,1,0:T(8,128)(2,1)S(1)}, u32[]{:S(2)}, u32[]{:S(2)}) collective-permute-start(bf16[2,96,2048]{2,1,0:T(8,128)(2,1)S(1)} %collective-permute-done.1.refs_5_), channel_id=1, source_target_pairs={{0,1},{1,0},{2,3},{3,2},{4,5},{5,4},{6,7},{7,6},{8,9},{9,8},{10,11... | collective-permute-start | bytes 2359304 | tf_op jit(solution)/shard_map/ppermute | solution.py:358
  66.8 0.0 copy-done.3
  66.8 0.0 copy-done.4
  66.9 17.1 %all-to-all-done = bf16[8,16,768]{2,1,0:T(8,128)(2,1)S(1)} async-done(((bf16[8,16,768]{2,1,0:T(8,128)(2,1)}), bf16[8,16,768]{2,1,0:T(8,128)(2,1)S(1)}, u32[]{:S(2)}, u32[]{:S(2)}) %all-to-all-start) | async-done | bytes 196640 | tf_op jit(solution)/shard_map/all_to_all | solution.py:300
  84.0 11.9 %all_gather.7.all_ref = bf16[4,128,768]{2,1,0:T(8,128)(2,1)S(1)} all-gather(bf16[1,128,768]{2,1,0:T(8,128)(2,1)S(1)} %bitcast.9), channel_id=1, replica_groups={{0,16,272,256},{32,48,304,288},{64,80,336,320},{96,112,368,352},{128,14..., dimensions={0}, use_global_device_ids=true | all-gather | bytes 983040 | tf_op jit(solution)/shard_map/all_gather | solution.py:359
  95.9 0.0 collective-permute-done.3.refs_7_
  95.9 0.0 copy-start.2
  95.9 0.0 collective-permute-done.2.refs_6_
  95.9 0.0 copy-done.1
  95.9 0.9 copy-done.2
  96.8 10.3 %rows.1 = bf16[128,768]{1,0:T(8,128)(2,1)S(1)} custom-call(bf16[4,128,768]{2,1,0:T(8,128)(2,1)S(1)} %all_gather.7.all_ref, f32[1,768]{1,0:T(1,128)S(1)} %reshape.13.gain1_ref, f32[1,768]{1,0:T(1,128)S(1)} %reshape.14.gain2_ref, bf16[192,1536]{1,0:T(8,128)(2,1)} %refs_0_.3, bf16[192,512]{1,0:T(8,128)(2,1)} %bitcast.11, bf16[192,1536]{1,0:T(8,128)(2,1)} %refs_2_.3, ...), custom_call_target="tpu_custom_call" | custom-call | flops 1140850688 | bytes 3932160 | tf_op jit(solution)/shard_map/rows/pallas_call | solution.py:277
  107.1 18.9 %all_to_all.10 = bf16[8,16,768]{2,1,0:T(8,128)(2,1)S(1)} all-to-all(bf16[8,16,768]{2,1,0:T(8,128)(2,1)S(1)} %bitcast.7), channel_id=1, replica_groups={{0,32,64,96,128,160,192,224},{16,48,80,112,144,176,208,240},{256,288,32..., dimensions={0} | all-to-all | bytes 393216 | tf_op jit(solution)/shard_map/all_to_all | solution.py:300
  126.1 0.7 copy.12
  (2 shorter events, 0.0 us)
Async XLA Ops:
  15.2 29.4 %copy-start = (f32[768]{0:T(1024)S(1)}, f32[768]{0:T(1024)}, u32[]{:S(2)}) copy-start(f32[768]{0:T(1024)} %gain_ref.1) | copy-start | bytes 9220
  15.3 23.6 %collective-permute-start = (bf16[2,192,2048]{2,1,0:T(8,128)(2,1)S(1)}, bf16[2,192,2048]{2,1,0:T(8,128)(2,1)}, u32[]{:S(2)}, u32[]{:S(2)}) collective-permute-start(bf16[2,192,2048]{2,1,0:T(8,128)(2,1)S(1)} %pack.1), channel_id=1, source_target_pairs={{0,4},{1,13},{2,6},{3,15},{4,8},{5,1},{6,10},{7,3},{8,12},{9,5},{1... | collective-permute-start | bytes 4718600 | tf_op jit(solution)/shard_map/ppermute | solution.py:349
  40.1 26.8 %copy-start.3 = (f32[768]{0:T(1024)S(1)}, f32[768]{0:T(1024)}, u32[]{:S(2)}) copy-start(f32[768]{0:T(1024)} %param.14) | copy-start | bytes 9220
  40.1 26.8 %copy-start.4 = (f32[768]{0:T(1024)S(1)}, f32[768]{0:T(1024)}, u32[]{:S(2)}) copy-start(f32[768]{0:T(1024)} %param.17) | copy-start | bytes 9220
  40.1 24.6 %collective-permute-start.1 = (bf16[2,96,2048]{2,1,0:T(8,128)(2,1)S(1)}, bf16[2,96,2048]{2,1,0:T(8,128)(2,1)S(1)}, u32[]{:S(2)}, u32[]{:S(2)}) collective-permute-start(bf16[2,96,2048]{2,1,0:T(8,128)(2,1)S(1)} %constant_dynamic-slice_fusion), channel_id=1, source_target_pairs={{0,4},{1,13},{2,6},{3,15},{4,8},{5,1},{6,10},{7,3},{8,12},{9,5},{1... | collective-permute-start | bytes 2359304 | tf_op jit(solution)/shard_map/ppermute | solution.py:354
  42.7 53.2 %collective-permute-start.2 = (bf16[2,192,2048]{2,1,0:T(8,128)(2,1)}, bf16[2,192,2048]{2,1,0:T(8,128)(2,1)}, u32[]{:S(2)}, u32[]{:S(2)}) collective-permute-start(bf16[2,192,2048]{2,1,0:T(8,128)(2,1)} %collective-permute-done.refs_4_), channel_id=1, source_target_pairs={{0,1},{1,0},{2,3},{3,2},{4,5},{5,4},{6,7},{7,6},{8,9},{9,8},{10,11... | collective-permute-start | bytes 4718600 | tf_op jit(solution)/shard_map/ppermute | solution.py:355
  49.6 34.4 %all-to-all-start = ((bf16[8,16,768]{2,1,0:T(8,128)(2,1)}), bf16[8,16,768]{2,1,0:T(8,128)(2,1)S(1)}, u32[]{:S(2)}, u32[]{:S(2)}) async-start(bf16[8,16,768]{2,1,0:T(8,128)(2,1)} %bitcast.3), calls=%async_computation | async-start | bytes 393216 | tf_op jit(solution)/shard_map/all_to_all | solution.py:300
  64.7 31.2 %copy-start.1 = (bf16[2,96,2048]{2,1,0:T(8,128)(2,1)}, bf16[2,96,2048]{2,1,0:T(8,128)(2,1)S(1)}, u32[]{:S(2)}) copy-start(bf16[2,96,2048]{2,1,0:T(8,128)(2,1)S(1)} %collective-permute-done.1.refs_5_) | copy-start | bytes 2359300
  64.7 31.2 %collective-permute-start.3 = (bf16[2,96,2048]{2,1,0:T(8,128)(2,1)S(1)}, bf16[2,96,2048]{2,1,0:T(8,128)(2,1)S(1)}, u32[]{:S(2)}, u32[]{:S(2)}) collective-permute-start(bf16[2,96,2048]{2,1,0:T(8,128)(2,1)S(1)} %collective-permute-done.1.refs_5_), channel_id=1, source_target_pairs={{0,1},{1,0},{2,3},{3,2},{4,5},{5,4},{6,7},{7,6},{8,9},{9,8},{10,11... | collective-permute-start | bytes 2359304 | tf_op jit(solution)/shard_map/ppermute | solution.py:358
  95.9 0.9 copy-start.2

commit v7 on v6

--- a/solution.py
+++ b/solution.py
@@ -356,7 +356,14 @@
     gain1 = row1_gain.reshape(1, width)
     gain2 = row2_gain.reshape(1, width)
     other_far = lax.ppermute(far, "batch", siblings)
-    everything = lax.all_gather(stream, "view", axis=0, tiled=False, axis_index_groups=ring)
+    everything = lax.all_to_all(
+        jnp.broadcast_to(stream[None], (share, tokens, width)),
+        "view",
+        split_axis=0,
+        concat_axis=0,
+        tiled=True,
+        axis_index_groups=ring,
+    )
     stream = rows_layer(
         everything, gain1, gain2, (*shards, near, far, other_near, other_far)
     )

time: 127 us -> 114 us (0.90)
  the two profiles are of different devices: /device:TPU:16 before, /device:TPU:56 now
where the time goes in v7:
time: 114 us; the launch traced here: 113 us
  blocking collectives  64.3 us (56%)
  starting transfers between devices  17.1 us (15%)
  Pallas kernels  15.9 us (14%)
  waiting for transfers between devices  11.9 us (10%)
  local copies, waits for them, and re-layouts  3.98 us (3%)
    all_to_all x2, blocking collectives, exchanged(): lax.all_to_all(stream.reshape(rows, tokens // rows, width), 'view', split...  50.5 us
    all_gather x1, blocking collectives, layers(): lax.all_gather(images.reshape(tokens, width), 'band', axis=0, tiled=False)  13.9 us
    pallas_call x1, Pallas kernels, rows_layer(): pl.pallas_call(rows_body, out_shape=jax.ShapeDtypeStruct((tokens, width),...  10.3 us
    ppermute x1, waiting for transfers between devices, layers(): far = lax.ppermute(far, ('band', 'batch'), turn)  9.54 us
    all_to_all x1, starting transfers between devices, layers(): lax.all_to_all(jnp.broadcast_to(stream[None], (share, tokens, width)), 'v...  5.84 us
    pallas_call x1, Pallas kernels, frame_layer(): pl.pallas_call(frame_body, out_shape=jax.ShapeDtypeStruct((tokens, width)...  4.19 us
    ppermute x1, starting transfers between devices, layers(): near = lax.ppermute(near, ('band', 'batch'), turn)  3.85 us
    ppermute x1, starting transfers between devices, layers(): far = lax.ppermute(far, ('band', 'batch'), turn)  3.61 us
  transfers between devices with their start and end apart: 5, of which 2 were waited for; matrix products, arithmetic and copies ran while one was open for 2% of the time, Pallas kernels for 4%

profile of v7, /device:TPU:56, one launch (start us, length us, event | category | flops | bytes accessed | tf_op | source)
XLA Modules:
  0.0 113.4 jit_solution(9321519788395151459)
XLA Ops:
  0.0 13.9 %all_gather.3.all_ref = bf16[4,128,768]{2,1,0:T(8,128)(2,1)S(1)} all-gather(bf16[1,128,768]{2,1,0:T(8,128)(2,1)} %bitcast.15), channel_id=1, replica_groups=mesh['view'=32,'band'=4,'batch'=4] {'band'}, dimensions={0}, use_global_device_ids=true | all-gather | bytes 983040 | tf_op jit(solution)/shard_map/all_gather | solution.py:347
  13.9 0.0 copy-start
  13.9 1.4 %pack.1 = bf16[2,192,2048]{2,1,0:T(8,128)(2,1)S(1)} custom-call(bf16[192,1536]{1,0:T(8,128)(2,1)} %refs_0_.3, bf16[192,512]{1,0:T(8,128)(2,1)} %bitcast.11, bf16[192,1536]{1,0:T(8,128)(2,1)} %refs_2_.3, bf16[192,512]{1,0:T(8,128)(2,1)} %bitcast.13), custom_call_target="tpu_custom_call" | custom-call | tf_op jit(solution)/shard_map/pack/pallas_call | solution.py:120
  15.3 3.8 %collective-permute-start = (bf16[2,192,2048]{2,1,0:T(8,128)(2,1)S(1)}, bf16[2,192,2048]{2,1,0:T(8,128)(2,1)}, u32[]{:S(2)}, u32[]{:S(2)}) collective-permute-start(bf16[2,192,2048]{2,1,0:T(8,128)(2,1)S(1)} %pack.1), channel_id=1, source_target_pairs={{0,4},{1,13},{2,6},{3,15},{4,8},{5,1},{6,10},{7,3},{8,12},{9,5},{1... | collective-permute-start | bytes 4718600 | tf_op jit(solution)/shard_map/ppermute | solution.py:349
  19.1 0.0 copy-done
  19.1 4.2 %frame.1 = bf16[128,768]{1,0:T(8,128)(2,1)S(1)} custom-call(bf16[4,128,768]{2,1,0:T(8,128)(2,1)S(1)} %all_gather.3.all_ref, f32[768]{0:T(1024)S(1)} %copy-done, bf16[768,1536]{1,0:T(8,128)(2,1)} %qkv_ref.1, bf16[512,768]{1,0:T(8,128)(2,1)} %out_ref.1), custom_call_target="tpu_custom_call" | custom-call | flops 1140850688 | bytes 3932160 | tf_op jit(solution)/shard_map/frame/pallas_call | solution.py:171
  23.3 28.5 %all_to_all.15 = bf16[8,16,768]{2,1,0:T(8,128)(2,1)S(1)} all-to-all(bf16[8,16,768]{2,1,0:T(8,128)(2,1)S(1)} %bitcast.8), channel_id=1, replica_groups={{0,32,64,96,128,160,192,224},{16,48,80,112,144,176,208,240},{256,288,32..., dimensions={0} | all-to-all | bytes 393216 | tf_op jit(solution)/shard_map/all_to_all | solution.py:300
  51.8 0.9 broadcast_in_dim.8
  52.7 0.0 copy-start.3
  52.7 0.0 copy-start.4
  52.7 5.8 %all-to-all-start.1 = ((bf16[4,128,768]{2,1,0:T(8,128)(2,1)}), bf16[4,128,768]{2,1,0:T(8,128)(2,1)S(1)}, u32[]{:S(2)}, u32[]{:S(2)}) async-start(bf16[4,128,768]{2,1,0:T(8,128)(2,1)} %broadcast_in_dim.8), calls=%async_computation.1 | async-start | bytes 1572864 | tf_op jit(solution)/shard_map/all_to_all | solution.py:359
  58.6 0.0 collective-permute-done.refs_4_
  58.6 1.2 %constant_dynamic-slice_fusion = bf16[2,96,2048]{2,1,0:T(8,128)(2,1)S(1)} fusion(bf16[2,192,2048]{2,1,0:T(8,128)(2,1)} %collective-permute-done.refs_4_, s32[]{:T(128)S(6)} %select_n.3), kind=kLoop, calls=%fused_computation | loop fusion | bytes 1572868 | tf_op jit(solution)/shard_map/dynamic_slice | solution.py:353
  59.8 3.6 %collective-permute-start.1 = (bf16[2,96,2048]{2,1,0:T(8,128)(2,1)S(1)}, bf16[2,96,2048]{2,1,0:T(8,128)(2,1)S(1)}, u32[]{:S(2)}, u32[]{:S(2)}) collective-permute-start(bf16[2,96,2048]{2,1,0:T(8,128)(2,1)S(1)} %constant_dynamic-slice_fusion), channel_id=1, source_target_pairs={{0,4},{1,13},{2,6},{3,15},{4,8},{5,1},{6,10},{7,3},{8,12},{9,5},{1... | collective-permute-start | bytes 2359304 | tf_op jit(solution)/shard_map/ppermute | solution.py:354
  63.4 1.9 %collective-permute-start.2 = (bf16[2,192,2048]{2,1,0:T(8,128)(2,1)}, bf16[2,192,2048]{2,1,0:T(8,128)(2,1)S(1)}, u32[]{:S(2)}, u32[]{:S(2)}) collective-permute-start(bf16[2,192,2048]{2,1,0:T(8,128)(2,1)} %collective-permute-done.refs_4_), channel_id=1, source_target_pairs={{0,1},{1,0},{2,3},{3,2},{4,5},{5,4},{6,7},{7,6},{8,9},{9,8},{10,11... | collective-permute-start | bytes 4718600 | tf_op jit(solution)/shard_map/ppermute | solution.py:355
  65.3 9.5 %collective-permute-done.1.refs_5_ = bf16[2,96,2048]{2,1,0:T(8,128)(2,1)S(1)} collective-permute-done((bf16[2,96,2048]{2,1,0:T(8,128)(2,1)S(1)}, bf16[2,96,2048]{2,1,0:T(8,128)(2,1)S(1)}, u32[]{:S(2)}, u32[]{:S(2)}) %collective-permute-start.1) | collective-permute-done | bytes 786464 | tf_op jit(solution)/shard_map/ppermute | solution.py:354
  74.9 0.0 copy-start.2
  74.9 1.9 %collective-permute-start.3 = (bf16[2,96,2048]{2,1,0:T(8,128)(2,1)S(1)}, bf16[2,96,2048]{2,1,0:T(8,128)(2,1)}, u32[]{:S(2)}, u32[]{:S(2)}) collective-permute-start(bf16[2,96,2048]{2,1,0:T(8,128)(2,1)S(1)} %collective-permute-done.1.refs_5_), channel_id=1, source_target_pairs={{0,1},{1,0},{2,3},{3,2},{4,5},{5,4},{6,7},{7,6},{8,9},{9,8},{10,11... | collective-permute-start | bytes 2359304 | tf_op jit(solution)/shard_map/ppermute | solution.py:358
  76.8 0.0 copy-done.3
  76.8 0.0 copy-done.4
  76.9 0.0 all-to-all-done.1.all_ref
  76.9 2.3 %collective-permute-done.3.refs_7_ = bf16[2,96,2048]{2,1,0:T(8,128)(2,1)} collective-permute-done((bf16[2,96,2048]{2,1,0:T(8,128)(2,1)S(1)}, bf16[2,96,2048]{2,1,0:T(8,128)(2,1)}, u32[]{:S(2)}, u32[]{:S(2)}) %collective-permute-start.3) | collective-permute-done | bytes 786464 | tf_op jit(solution)/shard_map/ppermute | solution.py:358
  79.2 0.0 collective-permute-done.2.refs_6_
  79.2 0.0 copy-done.2
  79.2 0.0 copy-start.1
  79.2 1.2 %copy-done.1 = bf16[2,192,2048]{2,1,0:T(8,128)(2,1)} copy-done((bf16[2,192,2048]{2,1,0:T(8,128)(2,1)}, bf16[2,192,2048]{2,1,0:T(8,128)(2,1)S(1)}, u32[]{:S(2)}) %copy-start.1) | copy-done | bytes 1572888
  80.4 10.3 %rows.1 = bf16[128,768]{1,0:T(8,128)(2,1)S(1)} custom-call(bf16[4,128,768]{2,1,0:T(8,128)(2,1)S(1)} %all-to-all-done.1.all_ref, f32[1,768]{1,0:T(1,128)S(1)} %reshape.14.gain1_ref, f32[1,768]{1,0:T(1,128)S(1)} %reshape.15.gain2_ref, bf16[192,1536]{1,0:T(8,128)(2,1)} %refs_0_.3, bf16[192,512]{1,0:T(8,128)(2,1)} %bitcast.12, bf16[192,1536]{1,0:T(8,128)(2,1)} %refs_2_.3, ...), custom_call_target="tpu_custom_call" | custom-call | flops 1140850688 | bytes 3932160 | tf_op jit(solution)/shard_map/rows/pallas_call | solution.py:277
  90.7 22.0 %all_to_all.16 = bf16[8,16,768]{2,1,0:T(8,128)(2,1)S(1)} all-to-all(bf16[8,16,768]{2,1,0:T(8,128)(2,1)S(1)} %bitcast.7), channel_id=1, replica_groups={{0,32,64,96,128,160,192,224},{16,48,80,112,144,176,208,240},{256,288,32..., dimensions={0} | all-to-all | bytes 393216 | tf_op jit(solution)/shard_map/all_to_all | solution.py:300
  112.7 0.7 copy.12
  (2 shorter events, 0.0 us)
Async XLA Ops:
  13.9 5.3 %copy-start = (f32[768]{0:T(1024)S(1)}, f32[768]{0:T(1024)}, u32[]{:S(2)}) copy-start(f32[768]{0:T(1024)} %gain_ref.1) | copy-start | bytes 9220
  15.3 43.3 %collective-permute-start = (bf16[2,192,2048]{2,1,0:T(8,128)(2,1)S(1)}, bf16[2,192,2048]{2,1,0:T(8,128)(2,1)}, u32[]{:S(2)}, u32[]{:S(2)}) collective-permute-start(bf16[2,192,2048]{2,1,0:T(8,128)(2,1)S(1)} %pack.1), channel_id=1, source_target_pairs={{0,4},{1,13},{2,6},{3,15},{4,8},{5,1},{6,10},{7,3},{8,12},{9,5},{1... | collective-permute-start | bytes 4718600 | tf_op jit(solution)/shard_map/ppermute | solution.py:349
  52.7 24.1 %copy-start.3 = (f32[768]{0:T(1024)S(1)}, f32[768]{0:T(1024)}, u32[]{:S(2)}) copy-start(f32[768]{0:T(1024)} %param.14) | copy-start | bytes 9220
  52.7 24.1 %copy-start.4 = (f32[768]{0:T(1024)S(1)}, f32[768]{0:T(1024)}, u32[]{:S(2)}) copy-start(f32[768]{0:T(1024)} %param.17) | copy-start | bytes 9220
  52.7 24.1 %all-to-all-start.1 = ((bf16[4,128,768]{2,1,0:T(8,128)(2,1)}), bf16[4,128,768]{2,1,0:T(8,128)(2,1)S(1)}, u32[]{:S(2)}, u32[]{:S(2)}) async-start(bf16[4,128,768]{2,1,0:T(8,128)(2,1)} %broadcast_in_dim.8), calls=%async_computation.1 | async-start | bytes 1572864 | tf_op jit(solution)/shard_map/all_to_all | solution.py:359
  59.8 15.1 %collective-permute-start.1 = (bf16[2,96,2048]{2,1,0:T(8,128)(2,1)S(1)}, bf16[2,96,2048]{2,1,0:T(8,128)(2,1)S(1)}, u32[]{:S(2)}, u32[]{:S(2)}) collective-permute-start(bf16[2,96,2048]{2,1,0:T(8,128)(2,1)S(1)} %constant_dynamic-slice_fusion), channel_id=1, source_target_pairs={{0,4},{1,13},{2,6},{3,15},{4,8},{5,1},{6,10},{7,3},{8,12},{9,5},{1... | collective-permute-start | bytes 2359304 | tf_op jit(solution)/shard_map/ppermute | solution.py:354
  63.4 15.8 %collective-permute-start.2 = (bf16[2,192,2048]{2,1,0:T(8,128)(2,1)}, bf16[2,192,2048]{2,1,0:T(8,128)(2,1)S(1)}, u32[]{:S(2)}, u32[]{:S(2)}) collective-permute-start(bf16[2,192,2048]{2,1,0:T(8,128)(2,1)} %collective-permute-done.refs_4_), channel_id=1, source_target_pairs={{0,1},{1,0},{2,3},{3,2},{4,5},{5,4},{6,7},{7,6},{8,9},{9,8},{10,11... | collective-permute-start | bytes 4718600 | tf_op jit(solution)/shard_map/ppermute | solution.py:355
  74.9 4.3 %copy-start.2 = (bf16[2,96,2048]{2,1,0:T(8,128)(2,1)}, bf16[2,96,2048]{2,1,0:T(8,128)(2,1)S(1)}, u32[]{:S(2)}) copy-start(bf16[2,96,2048]{2,1,0:T(8,128)(2,1)S(1)} %collective-permute-done.1.refs_5_) | copy-start | bytes 2359300
  74.9 4.3 %collective-permute-start.3 = (bf16[2,96,2048]{2,1,0:T(8,128)(2,1)S(1)}, bf16[2,96,2048]{2,1,0:T(8,128)(2,1)}, u32[]{:S(2)}, u32[]{:S(2)}) collective-permute-start(bf16[2,96,2048]{2,1,0:T(8,128)(2,1)S(1)} %collective-permute-done.1.refs_5_), channel_id=1, source_target_pairs={{0,1},{1,0},{2,3},{3,2},{4,5},{5,4},{6,7},{7,6},{8,9},{9,8},{10,11... | collective-permute-start | bytes 2359304 | tf_op jit(solution)/shard_map/ppermute | solution.py:358
  79.2 1.2 %copy-start.1 = (bf16[2,192,2048]{2,1,0:T(8,128)(2,1)}, bf16[2,192,2048]{2,1,0:T(8,128)(2,1)S(1)}, u32[]{:S(2)}) copy-start(bf16[2,192,2048]{2,1,0:T(8,128)(2,1)S(1)} %collective-permute-done.2.refs_6_) | copy-start | bytes 4718596

commit v8 on v6

--- a/solution.py
+++ b/solution.py
@@ -27,36 +27,44 @@
             at = chunk * tokens + start
             normed_ref[at : at + NORM_ROWS, :] = (values * factor * gain).astype(jnp.bfloat16)
     for part in range(2):
-        waits[1 + part]()
+        if waits:
+            waits[1 + part]()
         kv_ref[:, part * inner : (part + 1) * inner] = jnp.dot(
             normed_ref[...],
             weight_ref[:, (1 + part) * inner : (2 + part) * inner],
             preferred_element_type=jnp.float32,
         ).astype(jnp.bfloat16)
-    waits[0]()
-
-
-def mixed(normed, weight_ref, kv_ref, query_ref, score_ref, rounded_ref, inverse_ref, attended_ref):
-    count = normed.shape[0]
+    if waits:
+        waits[0]()
+
+
+def mixed(fence, read_normed, weight_ref, kv_ref, query_ref, score_ref, rounded_ref, inverse_ref, attended_ref):
+    count = attended_ref.shape[0]
     inner = kv_ref.shape[1] // 2
-    queries = (
-        jnp.dot(normed, weight_ref[:, :inner], preferred_element_type=jnp.float32) * SCALE
-    ).astype(jnp.bfloat16)
-    first = lax.broadcasted_iota(jnp.int32, (count, PAIR), 1) < HEAD_DIM
-    zeros = jnp.zeros((count, PAIR), jnp.bfloat16)
-    for pair in range(inner // PAIR):
-        query = queries[:, pair * PAIR : (pair + 1) * PAIR]
-        query_ref[pair, :count] = jnp.where(first, query, zeros)
-        query_ref[pair, count:] = jnp.where(first, zeros, query)
-    for pair in range(inner // PAIR):
-        slot = pair % 2
-        columns = slice(pair * PAIR, (pair + 1) * PAIR)
-        score_ref[slot] = lax.dot_general(
+    pairs = inner // PAIR
+
+    @pl.when(fence)
+    def _():
+        first = lax.broadcasted_iota(jnp.int32, (count, PAIR), 1) < HEAD_DIM
+        zeros = jnp.zeros((count, PAIR), jnp.bfloat16)
+        queries = (
+            jnp.dot(read_normed(), weight_ref[:, :inner], preferred_element_type=jnp.float32) * SCALE
+        ).astype(jnp.bfloat16)
+        for pair in range(pairs):
+            query = queries[:, pair * PAIR : (pair + 1) * PAIR]
+            query_ref[pair, :count] = jnp.where(first, query, zeros)
+            query_ref[pair, count:] = jnp.where(first, zeros, query)
+
+    def score(pair):
+        score_ref[pair % 2] = lax.dot_general(
             query_ref[pair],
-            kv_ref[:, columns],
+            kv_ref[:, pair * PAIR : (pair + 1) * PAIR],
             (((1,), (1,)), ((), ())),
             preferred_element_type=jnp.float32,
         )
+
+    def weigh(pair):
+        slot = pair % 2
         for start in range(0, 2 * count, SOFTMAX_ROWS):
             rows = slice(start, start + SOFTMAX_ROWS)
             scores = score_ref[slot, rows]
@@ -64,14 +72,29 @@
             total = jnp.sum(weights, axis=-1, keepdims=True)
             rounded_ref[slot, rows] = weights.astype(jnp.bfloat16)
             inverse_ref[slot, rows] = jnp.broadcast_to(1.0 / total, (SOFTMAX_ROWS, PAIR))
+
+    def mix(pair):
+        slot = pair % 2
+        first = lax.broadcasted_iota(jnp.int32, (count, PAIR), 1) < HEAD_DIM
         result = inverse_ref[slot] * jnp.dot(
             rounded_ref[slot],
             kv_ref[:, inner + pair * PAIR : inner + (pair + 1) * PAIR],
             preferred_element_type=jnp.float32,
         )
-        attended_ref[:, columns] = jnp.where(first, result[:count], result[count:]).astype(
-            jnp.bfloat16
-        )
+        attended_ref[:, pair * PAIR : (pair + 1) * PAIR] = jnp.where(
+            first, result[:count], result[count:]
+        ).astype(jnp.bfloat16)
+
+    for stage in range(pairs + 2):
+
+        @pl.when(fence)
+        def _(stage=stage):
+            if stage < pairs:
+                score(stage)
+            if 0 <= stage - 1 < pairs:
+                weigh(stage - 1)
+            if 0 <= stage - 2:
+                mix(stage - 2)
 
 
 def mixing_scratch(count, keys, inner):
@@ -153,7 +176,7 @@
     project(all_ref, gain_ref, waits, weight_ref, normed_ref, kv_ref)
     mix()
     _, tokens, _ = all_ref.shape
-    mixed(chunk_of(normed_ref, band, tokens), weight_ref, kv_ref, *mixing)
+    mixed(band >= 0, lambda: chunk_of(normed_ref, band, tokens), weight_ref, kv_ref, *mixing)
     update = jnp.dot(mixing[-1][...], mix_ref[...], preferred_element_type=jnp.float32)
     result_ref[...] = (all_ref[band].astype(jnp.float32) + update).astype(jnp.bfloat16)
 
@@ -197,31 +220,17 @@
 
 
 def assembled(parts, weight_ref, sems, band, bands, core):
-    qkv_ref, out_ref, near_ref, far_ref, other_near_ref, other_far_ref = parts
-    inner = out_ref.shape[1]
-    rows = far_ref.shape[0]
-
-    def place(index, half, count):
-        return pl.ds(pl.multiple_of((2 * lax.rem(index, bands) + half) * rows, rows), count)
-
-    down, up = band + bands - 1, band + 1
-    target = (
-        place(band, 0, 2 * rows),
-        place(down + 2 * core, 0, 2 * rows),
-        place(band + 2, core, rows),
-        place(up + 2 * core, 0, 2 * rows),
-        place(band + 2, 1 - core, rows),
-    )
+    inner = parts[1].shape[1]
+    rows = parts[1].shape[0]
+    target = [
+        pl.ds(pl.multiple_of(lax.rem(band + step, bands) * rows, rows), rows)
+        for step in (0, bands - 1 + 2 * core, 2, 1 + 2 * core)
+    ]
     waits = {}
     for order, part in enumerate((1, 2, 0, 3)):
         columns = slice(part * inner, (part + 1) * inner)
-        sources = (
-            out_ref if part == 3 else qkv_ref.at[:, columns],
-            near_ref.at[:, columns],
-            far_ref.at[:, columns],
-            other_near_ref.at[:, columns],
-            other_far_ref.at[:, columns],
-        )
+        sources = (parts[1] if part == 3 else parts[0].at[:, columns],)
+        sources += tuple(ref.at[:, columns] for ref in parts[2:])
         waits[part] = started(
             [
                 pltpu.make_async_copy(source, weight_ref.at[goal, columns], sems.at[order, index])
@@ -232,7 +241,7 @@
 
 
 def rows_body(all_ref, gain1_ref, gain2_ref, *refs):
-    shards, moved, refs = refs[:4], refs[4:8], refs[8:]
+    shards, moved, refs = refs[:4], refs[4:7], refs[7:]
     parts1 = (*shards[:2], *(ref.at[0] for ref in moved))
     parts2 = (*shards[2:], *(ref.at[1] for ref in moved))
     result_ref, weight1_ref, weight2_ref, normed_ref, kv_ref, stream_ref, sems = refs[:7]
@@ -251,7 +260,7 @@
     waits2 = assembled(parts2, weight2_ref, sems.at[1], band, bands, core)
     project(all_ref, gain1_ref, waits1, weight1_ref, normed_ref, kv_ref)
     _, tokens, _ = all_ref.shape
-    mixed(normed_ref[...], weight1_ref, kv_ref, *mixing1)
+    mixed(band >= 0, lambda: normed_ref[...], weight1_ref, kv_ref, *mixing1)
     waits1[3]()
     update = lax.dot_general(
         mixing1[-1][...], weight1_ref[:, 3 * inner :], contract, preferred_element_type=jnp.float32
@@ -260,9 +269,10 @@
         stream_ref[chunk] = (
             all_ref[chunk].astype(jnp.float32) + update[chunk * tokens : (chunk + 1) * tokens]
         ).astype(jnp.bfloat16)
-    project(stream_ref, gain2_ref, waits2, weight2_ref, normed_ref, kv_ref)
-    mixed(chunk_of(normed_ref, own, tokens), weight2_ref, kv_ref, *mixing2)
-    waits2[3]()
+    for part in range(4):
+        waits2[part]()
+    project(stream_ref, gain2_ref, None, weight2_ref, normed_ref, kv_ref)
+    mixed(band >= 0, lambda: chunk_of(normed_ref, own, tokens), weight2_ref, kv_ref, *mixing2)
     update = lax.dot_general(
         mixing2[-1][...], weight2_ref[:, 3 * inner :], contract, preferred_element_type=jnp.float32
     )
@@ -277,7 +287,7 @@
     return pl.pallas_call(
         rows_body,
         out_shape=jax.ShapeDtypeStruct((tokens, width), jnp.bfloat16),
-        in_specs=[vmem] * 3 + [pl.BlockSpec(memory_space=pltpu.HBM)] * 8,
+        in_specs=[vmem] * 3 + [pl.BlockSpec(memory_space=pltpu.HBM)] * 7,
         out_specs=vmem,
         scratch_shapes=[
             pltpu.VMEM((width, 4 * inner), jnp.bfloat16),
@@ -285,7 +295,7 @@
             pltpu.VMEM((count, width), jnp.bfloat16),
             pltpu.VMEM((count, 2 * inner), jnp.bfloat16),
             pltpu.VMEM((chunks, tokens, width), jnp.bfloat16),
-            pltpu.SemaphoreType.DMA((2, 4, 5)),
+            pltpu.SemaphoreType.DMA((2, 4, 4)),
         ]
         + mixing_scratch(count, count, inner)
         + mixing_scratch(tokens, count, inner),
@@ -343,22 +353,18 @@
     ]
 
     shards = (row1_qkv, row1_out.T, row2_qkv, row2_out.T)
-    core = lax.rem(lax.axis_index("batch"), 2)
     everything = lax.all_gather(images.reshape(tokens, width), "band", axis=0, tiled=False)
     everything, near = lax.optimization_barrier((everything, pack_layer(shards)))
     near = lax.ppermute(near, ("band", "batch"), turn)
     stream = frame_layer(everything, frame_gain, frame_qkv, frame_out)
     stream = exchanged(stream, row_count, spread)
-    half = near.shape[1] // 2
-    far = lax.dynamic_slice_in_dim(near, core * half, half, axis=1)
-    far = lax.ppermute(far, ("band", "batch"), turn)
-    other_near = lax.ppermute(near, "batch", siblings)
+    far = lax.ppermute(near, ("band", "batch"), turn)
+    other = lax.ppermute(near, "batch", siblings)
     gain1 = row1_gain.reshape(1, width)
     gain2 = row2_gain.reshape(1, width)
-    other_far = lax.ppermute(far, "batch", siblings)
     everything = lax.all_gather(stream, "view", axis=0, tiled=False, axis_index_groups=ring)
     stream = rows_layer(
-        everything, gain1, gain2, (*shards, near, far, other_near, other_far)
+        everything, gain1, gain2, (*shards, near, far, other)
     )
     stream = exchanged(stream, row_count, spread)
     return stream.reshape(images.shape)

time: 127 us -> 126 us (level)
  starting transfers between devices: 25.6 us -> 23.5 us
  waiting for transfers between devices: 36.9 us -> 38.9 us
  blocking collectives: 44.7 us -> 46.5 us
  Pallas kernels: 16.6 us -> 14.9 us
    all_to_all x1, waiting for transfers between devices: 17.1 us -> 19.2 us  [exchanged(): lax.all_to_all(stream.reshape(rows, tokens // rows, width), 'view', split...]
    ppermute x3 -> x2, starting transfers between devices: 6.69 us -> 4.55 us  [the longest x1 2.64 us: layers(): far = lax.ppermute(near, ('band', 'batch'), turn)]
    all_to_all x1, blocking collectives: 18.9 us -> 20.9 us  [exchanged(): lax.all_to_all(stream.reshape(rows, tokens // rows, width), 'view', split...]
  transfers between devices with their start and end apart: 5 -> 4, of which waited for: 2 -> 2; matrix products, arithmetic and copies ran while one was open for 0% -> 0% of each run, Pallas kernels for 4% -> 3%
where the time goes in v8:
time: 126 us
  blocking collectives  46.5 us (37%)
  waiting for transfers between devices  38.9 us (31%)
  starting transfers between devices  23.5 us (19%)
  Pallas kernels  14.9 us (12%)
  local copies, waits for them, and re-layouts  1.86 us (1%)
    all_to_all x1, blocking collectives, exchanged(): lax.all_to_all(stream.reshape(rows, tokens // rows, width), 'view', split...  20.9 us
    ppermute x1, waiting for transfers between devices, layers(): near = lax.ppermute(near, ('band', 'batch'), turn)  19.7 us
    all_to_all x1, waiting for transfers between devices, exchanged(): lax.all_to_all(stream.reshape(rows, tokens // rows, width), 'view', split...  19.2 us
    all_to_all x1, starting transfers between devices, exchanged(): lax.all_to_all(stream.reshape(rows, tokens // rows, width), 'view', split...  15.1 us
    all_gather x1, blocking collectives, layers(): lax.all_gather(images.reshape(tokens, width), 'band', axis=0, tiled=False)  13.9 us
    all_gather x1, blocking collectives, layers(): lax.all_gather(stream, 'view', axis=0, tiled=False, axis_index_groups=ring)  11.8 us
    pallas_call x1, Pallas kernels, rows_layer(): pl.pallas_call(rows_body, out_shape=jax.ShapeDtypeStruct((tokens, width),...  9.19 us
    pallas_call x1, Pallas kernels, frame_layer(): pl.pallas_call(frame_body, out_shape=jax.ShapeDtypeStruct((tokens, width)...  4.36 us
  transfers between devices with their start and end apart: 4, of which 2 were waited for; matrix products, arithmetic and copies ran while one was open for 0% of the time, Pallas kernels for 3%

profile of v8, /device:TPU:16, one launch (start us, length us, event | category | flops | bytes accessed | tf_op | source)
XLA Modules:
  0.0 125.9 jit_solution(7464412475189933168)
XLA Ops:
  0.0 13.9 %all_gather.6.all_ref = bf16[4,128,768]{2,1,0:T(8,128)(2,1)S(1)} all-gather(bf16[1,128,768]{2,1,0:T(8,128)(2,1)} %bitcast.14), channel_id=1, replica_groups=mesh['view'=32,'band'=4,'batch'=4] {'band'}, dimensions={0}, use_global_device_ids=true | all-gather | bytes 983040 | tf_op jit(solution)/shard_map/all_gather | solution.py:356
  13.9 0.0 copy-start
  13.9 1.4 %pack.1 = bf16[2,192,2048]{2,1,0:T(8,128)(2,1)S(1)} custom-call(bf16[192,1536]{1,0:T(8,128)(2,1)} %refs_0_.3, bf16[192,512]{1,0:T(8,128)(2,1)} %bitcast.10, bf16[192,1536]{1,0:T(8,128)(2,1)} %refs_2_.3, bf16[192,512]{1,0:T(8,128)(2,1)} %bitcast.12), custom_call_target="tpu_custom_call" | custom-call | tf_op jit(solution)/shard_map/pack/pallas_call | solution.py:143
  15.3 0.0 copy-start.3
  15.3 0.0 copy-start.4
  15.3 3.8 %collective-permute-start = (bf16[2,192,2048]{2,1,0:T(8,128)(2,1)S(1)}, bf16[2,192,2048]{2,1,0:T(8,128)(2,1)S(1)}, u32[]{:S(2)}, u32[]{:S(2)}) collective-permute-start(bf16[2,192,2048]{2,1,0:T(8,128)(2,1)S(1)} %pack.1), channel_id=1, source_target_pairs={{0,4},{1,13},{2,6},{3,15},{4,8},{5,1},{6,10},{7,3},{8,12},{9,5},{1... | collective-permute-start | bytes 4718600 | tf_op jit(solution)/shard_map/ppermute | solution.py:358
  19.1 19.7 %collective-permute-done.refs_4_ = bf16[2,192,2048]{2,1,0:T(8,128)(2,1)S(1)} collective-permute-done((bf16[2,192,2048]{2,1,0:T(8,128)(2,1)S(1)}, bf16[2,192,2048]{2,1,0:T(8,128)(2,1)S(1)}, u32[]{:S(2)}, u32[]{:S(2)}) %collective-permute-start) | collective-permute-done | bytes 1572896 | tf_op jit(solution)/shard_map/ppermute | solution.py:358
  38.8 0.0 copy-start.1
  38.8 1.9 %collective-permute-start.2 = (bf16[2,192,2048]{2,1,0:T(8,128)(2,1)S(1)}, bf16[2,192,2048]{2,1,0:T(8,128)(2,1)S(1)}, u32[]{:S(2)}, u32[]{:S(2)}) collective-permute-start(bf16[2,192,2048]{2,1,0:T(8,128)(2,1)S(1)} %collective-permute-done.refs_4_), channel_id=1, source_target_pairs={{0,1},{1,0},{2,3},{3,2},{4,5},{5,4},{6,7},{7,6},{8,9},{9,8},{10,11... | collective-permute-start | bytes 4718600 | tf_op jit(solution)/shard_map/ppermute | solution.py:362
  40.7 2.6 %collective-permute-start.1 = (bf16[2,192,2048]{2,1,0:T(8,128)(2,1)S(1)}, bf16[2,192,2048]{2,1,0:T(8,128)(2,1)}, u32[]{:S(2)}, u32[]{:S(2)}) collective-permute-start(bf16[2,192,2048]{2,1,0:T(8,128)(2,1)S(1)} %collective-permute-done.refs_4_), channel_id=1, source_target_pairs={{0,4},{1,13},{2,6},{3,15},{4,8},{5,1},{6,10},{7,3},{8,12},{9,5},{1... | collective-permute-start | bytes 4718600 | tf_op jit(solution)/shard_map/ppermute | solution.py:361
  43.4 0.0 copy-done
  43.4 4.4 %frame.1 = bf16[128,768]{1,0:T(8,128)(2,1)} custom-call(bf16[4,128,768]{2,1,0:T(8,128)(2,1)S(1)} %all_gather.6.all_ref, f32[768]{0:T(1024)S(1)} %copy-done, bf16[768,1536]{1,0:T(8,128)(2,1)} %qkv_ref.1, bf16[512,768]{1,0:T(8,128)(2,1)} %out_ref.1), custom_call_target="tpu_custom_call" | custom-call | flops 1140850688 | bytes 3932160 | tf_op jit(solution)/shard_map/frame/pallas_call | solution.py:194
  47.7 0.0 copy-done.1
  47.8 15.1 %all-to-all-start = ((bf16[8,16,768]{2,1,0:T(8,128)(2,1)}), bf16[8,16,768]{2,1,0:T(8,128)(2,1)S(1)}, u32[]{:S(2)}, u32[]{:S(2)}) async-start(bf16[8,16,768]{2,1,0:T(8,128)(2,1)} %bitcast.3), calls=%async_computation | async-start | bytes 393216 | tf_op jit(solution)/shard_map/all_to_all | solution.py:310
  62.9 0.0 copy-done.3
  62.9 0.0 copy-done.4
  62.9 19.2 %all-to-all-done = bf16[8,16,768]{2,1,0:T(8,128)(2,1)S(1)} async-done(((bf16[8,16,768]{2,1,0:T(8,128)(2,1)}), bf16[8,16,768]{2,1,0:T(8,128)(2,1)S(1)}, u32[]{:S(2)}, u32[]{:S(2)}) %all-to-all-start) | async-done | bytes 196640 | tf_op jit(solution)/shard_map/all_to_all | solution.py:310
  82.1 11.8 %all_gather.7.all_ref = bf16[4,128,768]{2,1,0:T(8,128)(2,1)S(1)} all-gather(bf16[1,128,768]{2,1,0:T(8,128)(2,1)S(1)} %bitcast.9), channel_id=1, replica_groups={{0,16,272,256},{32,48,304,288},{64,80,336,320},{96,112,368,352},{128,14..., dimensions={0}, use_global_device_ids=true | all-gather | bytes 983040 | tf_op jit(solution)/shard_map/all_gather | solution.py:365
  94.0 0.0 collective-permute-done.2.refs_6_
  94.0 0.0 copy-start.2
  94.0 0.0 collective-permute-done.1.refs_5_
  94.0 1.2 copy-done.2
  95.1 9.2 %rows.1 = bf16[128,768]{1,0:T(8,128)(2,1)S(1)} custom-call(bf16[4,128,768]{2,1,0:T(8,128)(2,1)S(1)} %all_gather.7.all_ref, f32[1,768]{1,0:T(1,128)S(1)} %reshape.13.gain1_ref, f32[1,768]{1,0:T(1,128)S(1)} %reshape.14.gain2_ref, bf16[192,1536]{1,0:T(8,128)(2,1)} %refs_0_.3, bf16[192,512]{1,0:T(8,128)(2,1)} %bitcast.11, bf16[192,1536]{1,0:T(8,128)(2,1)} %refs_2_.3, ...), custom_call_target="tpu_custom_call" | custom-call | flops 1140850688 | bytes 3932160 | tf_op jit(solution)/shard_map/rows/pallas_call | solution.py:287
  104.3 20.9 %all_to_all.10 = bf16[8,16,768]{2,1,0:T(8,128)(2,1)S(1)} all-to-all(bf16[8,16,768]{2,1,0:T(8,128)(2,1)S(1)} %bitcast.7), channel_id=1, replica_groups={{0,32,64,96,128,160,192,224},{16,48,80,112,144,176,208,240},{256,288,32..., dimensions={0} | all-to-all | bytes 393216 | tf_op jit(solution)/shard_map/all_to_all | solution.py:310
  125.2 0.7 copy.12
  (2 shorter events, 0.0 us)
Async XLA Ops:
  13.9 29.5 %copy-start = (f32[768]{0:T(1024)S(1)}, f32[768]{0:T(1024)}, u32[]{:S(2)}) copy-start(f32[768]{0:T(1024)} %gain_ref.1) | copy-start | bytes 9220
  15.3 47.6 %copy-start.3 = (f32[768]{0:T(1024)S(1)}, f32[768]{0:T(1024)}, u32[]{:S(2)}) copy-start(f32[768]{0:T(1024)} %param.14) | copy-start | bytes 9220
  15.3 47.6 %copy-start.4 = (f32[768]{0:T(1024)S(1)}, f32[768]{0:T(1024)}, u32[]{:S(2)}) copy-start(f32[768]{0:T(1024)} %param.17) | copy-start | bytes 9220
  15.3 23.5 %collective-permute-start = (bf16[2,192,2048]{2,1,0:T(8,128)(2,1)S(1)}, bf16[2,192,2048]{2,1,0:T(8,128)(2,1)S(1)}, u32[]{:S(2)}, u32[]{:S(2)}) collective-permute-start(bf16[2,192,2048]{2,1,0:T(8,128)(2,1)S(1)} %pack.1), channel_id=1, source_target_pairs={{0,4},{1,13},{2,6},{3,15},{4,8},{5,1},{6,10},{7,3},{8,12},{9,5},{1... | collective-permute-start | bytes 4718600 | tf_op jit(solution)/shard_map/ppermute | solution.py:358
  38.8 8.9 %copy-start.1 = (bf16[2,192,2048]{2,1,0:T(8,128)(2,1)}, bf16[2,192,2048]{2,1,0:T(8,128)(2,1)S(1)}, u32[]{:S(2)}) copy-start(bf16[2,192,2048]{2,1,0:T(8,128)(2,1)S(1)} %collective-permute-done.refs_4_) | copy-start | bytes 4718596
  38.8 55.2 %collective-permute-start.2 = (bf16[2,192,2048]{2,1,0:T(8,128)(2,1)S(1)}, bf16[2,192,2048]{2,1,0:T(8,128)(2,1)S(1)}, u32[]{:S(2)}, u32[]{:S(2)}) collective-permute-start(bf16[2,192,2048]{2,1,0:T(8,128)(2,1)S(1)} %collective-permute-done.refs_4_), channel_id=1, source_target_pairs={{0,1},{1,0},{2,3},{3,2},{4,5},{5,4},{6,7},{7,6},{8,9},{9,8},{10,11... | collective-permute-start | bytes 4718600 | tf_op jit(solution)/shard_map/ppermute | solution.py:362
  40.7 53.2 %collective-permute-start.1 = (bf16[2,192,2048]{2,1,0:T(8,128)(2,1)S(1)}, bf16[2,192,2048]{2,1,0:T(8,128)(2,1)}, u32[]{:S(2)}, u32[]{:S(2)}) collective-permute-start(bf16[2,192,2048]{2,1,0:T(8,128)(2,1)S(1)} %collective-permute-done.refs_4_), channel_id=1, source_target_pairs={{0,4},{1,13},{2,6},{3,15},{4,8},{5,1},{6,10},{7,3},{8,12},{9,5},{1... | collective-permute-start | bytes 4718600 | tf_op jit(solution)/shard_map/ppermute | solution.py:361
  47.8 34.4 %all-to-all-start = ((bf16[8,16,768]{2,1,0:T(8,128)(2,1)}), bf16[8,16,768]{2,1,0:T(8,128)(2,1)S(1)}, u32[]{:S(2)}, u32[]{:S(2)}) async-start(bf16[8,16,768]{2,1,0:T(8,128)(2,1)} %bitcast.3), calls=%async_computation | async-start | bytes 393216 | tf_op jit(solution)/shard_map/all_to_all | solution.py:310
  94.0 1.2 copy-start.2
